TPU v7x, 128 devices: a whole 4x4x4 slice. The times are simulated.
128 devices in a mesh: bx: 16 (over x, z), by: 8 (over y, core).
Axes of the slice: x: 4, y: 4, z: 4, core: 2. Of those that a mesh axis runs over, the one named last changes fastest.
Arguments:
- features: bfloat16 [16, 8, 1024, 128], P('bx', 'by'), may hold values from -13 to 13
- live_count: int32 [16, 8], P('bx', 'by'), may hold values from 128 to 1024, as said below
- neighbour_map: int32 [16, 8, 27, 1024], P('bx', 'by'), may hold values from 0 to 2175, as said below
- send_rows: int32 [16, 8, 8, 128], P('bx', 'by'), may hold values from 0 to 1023, as said below
- weight: bfloat16 [3456, 128], replicated, may hold values from -0.109375 to 0.109375
- gain: float32 [128], replicated, may hold values from 0.5 to 1.5
- shift: float32 [128], replicated, may hold values from -3 to 3
- cotangent: bfloat16 [16, 8, 1024, 128], P('bx', 'by'), may hold values from -13 to 13
Outputs:
- activated: bfloat16 [16, 8, 1024, 128], P('bx', 'by')
- grad_features: bfloat16 [16, 8, 1024, 128], P('bx', 'by')
- grad_weight: float32 [27, 128, 128], P(None, 'bx', 'by')
Inputs may be any that keep to these rules, and one draw needn't show every extreme that they name: Rows 0 to live_count - 1 of a brick are live, the rest padding; in every draw some brick is full. `send_rows`: every entry is below its brick's live count; the eight blocks follow the directions (dx, dy) in row-major order with the brick's own position left out. `neighbour_map`: entries index the brick's extended table; offset 13 of a live row names that row itself; every entry of a padding row is 1536. With B = min(1024, 512) and q = r // B for a live row r, an entry below 1024 lies in rows q B to q B + B - 1, and an entry 1024 + b * 128 + h of incoming block b other than 4 has h in q * 128 B / 1024 to (q + 1) * 128 B / 1024 - 1.
All inputs are finite; a program needn't handle non-finite values.
Results may differ from a plain program's by a relative error of at most 0.029.
The roundings to bfloat16 on the way count: a program that leaves them out, or rounds other values in their place, can miss the bound.
Values may be sent and summed in bfloat16 or wider, within the bound.
No kernel may reach another device: no remote copies, remote signals or barrier semaphores. Data moves between devices by JAX's collectives and lax.ppermute only.
A program may use at most 64 MiB of HBM per device.

v0:
```python
import functools

import jax
import jax.numpy as jnp
from jax import lax
from jax.experimental import pallas as pl
from jax.experimental.pallas import tpu as pltpu
from jax.sharding import PartitionSpec as P

epsilon = 1e-05
axes = ("bx", "by")
F32, BF16, I32 = jnp.float32, jnp.bfloat16, jnp.int32
TAPS = 27


def forward_kernel(chunks, place_ref, own_ref, a0_ref, a2_ref, b0_ref, b2_ref, weight_ref, conv_ref, out_ref, win_ref, cols_ref, sems):
    rows, channels = own_ref.shape
    block = win_ref.shape[0]
    part = block // 8
    high = a0_ref.shape[0] // 3
    wide = TAPS // chunks * channels
    lanes = lax.broadcasted_iota(I32, (block, block), 1)

    def copy_out(q, c):
        return pltpu.make_async_copy(
            cols_ref.at[q, :, pl.ds(c * wide, wide)],
            out_ref.at[pl.ds(q * block, block), pl.ds(c * wide, wide)],
            sems.at[q, c],
        )

    def block_step(q, _):
        here = pl.ds(pl.multiple_of(q * block, block), block)
        win_ref[:, :channels] = own_ref[here, :]
        pieces = (
            (b0_ref, 0), (a0_ref, 1), (b2_ref, 0), (b0_ref, 1),
            (b2_ref, 1), (b0_ref, 2), (a2_ref, 1), (b2_ref, 2),
        )
        for slot, (ref, at) in enumerate(pieces):
            win_ref[pl.ds(slot * part, part), channels:] = ref[
                pl.ds(pl.multiple_of(at * high + q * part, part), part), :
            ]
        place = place_ref[here, :]
        for k in range(TAPS):
            column = jnp.broadcast_to(place[:, k : k + 1], (block, channels))
            beyond = column >= block
            inside = jnp.where(beyond, column - block, column)
            hot = jnp.concatenate(
                [
                    jnp.where(inside == lanes[:, c : c + channels], 1.0, 0.0).astype(BF16)
                    for c in range(0, block, channels)
                ],
                axis=1,
            )
            both = jnp.dot(hot, win_ref[...], preferred_element_type=F32)
            cols_ref[q, :, k * channels : (k + 1) * channels] = jnp.where(
                beyond, both[:, channels:], both[:, :channels]
            ).astype(BF16)
            if (k + 1) % (TAPS // chunks) == 0:
                copy_out(q, k // (TAPS // chunks)).start()
        conv_ref[here, :] = jnp.dot(
            cols_ref[q], weight_ref[...], preferred_element_type=F32
        ).astype(BF16)
        return 0

    lax.fori_loop(0, rows // block, block_step, 0)
    for q in range(rows // block):
        for c in range(chunks):
            copy_out(q, c).wait()


def forward(place, own, a0, a2, b0, b2, weight, block=512, chunks=3):
    rows, channels = own.shape
    vmem = pl.BlockSpec(memory_space=pltpu.VMEM)
    return pl.pallas_call(
        functools.partial(forward_kernel, chunks),
        in_specs=[vmem] * 7,
        out_specs=(vmem, pl.BlockSpec(memory_space=pltpu.HBM)),
        out_shape=(
            jax.ShapeDtypeStruct((rows, channels), BF16),
            pltpu.HBM((rows, TAPS * channels), BF16),
        ),
        scratch_shapes=[
            pltpu.VMEM((block, 2 * channels), BF16),
            pltpu.VMEM((rows // block, block, TAPS * channels), BF16),
            pltpu.SemaphoreType.DMA((rows // block, chunks)),
        ],
        compiler_params=pltpu.CompilerParams(vmem_limit_bytes=20 << 20),
        cost_estimate=pl.CostEstimate(
            flops=TAPS * 4 * rows * channels * block, bytes_accessed=9 << 20, transcendentals=0
        ),
    )(place, own, a0, a2, b0, b2, weight)


def backward_kernel(group, row_ref, place_ref, grad_ref, weight_ref, own_ref, lo_ref, m0_ref, m2_ref, hi_ref, acc_ref, hot_ref, rhs_ref):
    rows, channels = grad_ref.shape
    block = acc_ref.shape[0]
    part = block // 8
    high = m0_ref.shape[0]
    for q in range(rows // block):
        grad = grad_ref[pl.ds(q * block, block), :]
        place = place_ref[pl.ds(q * block, block), :]
        down = lax.broadcasted_iota(I32, (block, block), 0)
        for g in range(TAPS // group):
            for n in range(group):
                k = g * group + n
                line = row_ref[q, k : k + 1, :]
                line = jnp.where(line >= block, line - block, line)
                hot_ref[:, n * block : (n + 1) * block] = jnp.where(
                    jnp.broadcast_to(line, (block, block)) == down, 1.0, 0.0
                ).astype(BF16)
                back = lax.dot_general(
                    grad, weight_ref[k * channels : (k + 1) * channels, :],
                    (((1,), (1,)), ((), ())), preferred_element_type=F32,
                )
                beyond = jnp.broadcast_to(place[:, k : k + 1], (block, channels)) >= block
                rhs_ref[n * block : (n + 1) * block, :channels] = jnp.where(beyond, 0.0, back).astype(BF16)
                rhs_ref[n * block : (n + 1) * block, channels:] = jnp.where(beyond, back, 0.0).astype(BF16)
            term = jnp.dot(hot_ref[...], rhs_ref[...], preferred_element_type=F32)
            if g == 0:
                acc_ref[...] = term
            else:
                acc_ref[...] += term
        own_ref[pl.ds(q * block, block), :] = acc_ref[:, :channels]
        pieces = (
            (lo_ref, 0), (lo_ref, 1), (lo_ref, 2), (m0_ref, 0),
            (m2_ref, 0), (hi_ref, 0), (hi_ref, 1), (hi_ref, 2),
        )
        for slot, (ref, at) in enumerate(pieces):
            ref[pl.ds(at * high + q * part, part), :] = acc_ref[slot * part : (slot + 1) * part, channels:].astype(BF16)


def backward(row, place, grad, weight, high, block=512, group=3):
    rows, channels = grad.shape
    return pl.pallas_call(
        functools.partial(backward_kernel, group),
        out_shape=(
            jax.ShapeDtypeStruct((rows, channels), F32),
            jax.ShapeDtypeStruct((3 * high, channels), BF16),
            jax.ShapeDtypeStruct((high, channels), BF16),
            jax.ShapeDtypeStruct((high, channels), BF16),
            jax.ShapeDtypeStruct((3 * high, channels), BF16),
        ),
        scratch_shapes=[
            pltpu.VMEM((block, 2 * channels), F32),
            pltpu.VMEM((block, group * block), BF16),
            pltpu.VMEM((group * block, 2 * channels), BF16),
        ],
        compiler_params=pltpu.CompilerParams(vmem_limit_bytes=16 << 20),
        cost_estimate=pl.CostEstimate(flops=TAPS*4*rows*channels*(block+64), bytes_accessed=2<<20, transcendentals=0),
    )(row, place, grad, weight)


def terms_kernel(across, down, group, cols_ref, rhs_ref, *refs):
    count = (len(refs) - 4) // 2
    outs, stages = refs[:count], refs[count : 2 * count]
    mirror_ref, buffer_ref, in_sems, out_sems = refs[2 * count :]
    channels = cols_ref.shape[1] // TAPS
    width = channels // down
    slots = buffer_ref.shape[0]
    row = lax.broadcasted_iota(I32, (channels, channels), 0)
    lane = lax.broadcasted_iota(I32, (channels, channels), 1)
    steps = TAPS // group

    def fetch(step):
        return pltpu.make_async_copy(
            cols_ref.at[:, pl.ds(step * group * channels, group * channels)],
            buffer_ref.at[step % slots],
            in_sems.at[step % slots],
        )

    def leave(n, eighth):
        return pltpu.make_async_copy(
            stages[n].at[eighth], outs[n].at[eighth], out_sems.at[n, eighth]
        )

    for step in range(slots - 1):
        fetch(step).start()
    mirror = jnp.where(
        row == (down - lane // width) % down * width + lane % width, 1.0, 0.0
    ).astype(BF16)
    for n in range(count):
        part = slice(n * channels, (n + 1) * channels)
        mirror_ref[:, part] = jnp.dot(
            rhs_ref[:, part], mirror, preferred_element_type=F32
        ).astype(BF16)
    for step in range(steps):
        if step + slots - 1 < steps:
            fetch(step + slots - 1).start()
        fetch(step).wait()
        whole = lax.dot_general(
            buffer_ref[step % slots], mirror_ref[...],
            (((0,), (0,)), ((), ())), preferred_element_type=F32,
        )
        for n in range(count):
            for k in range(step * group, (step + 1) * group):
                at = (k - step * group) * channels
                tile = whole[at : at + channels, n * channels : (n + 1) * channels]
                tile = pltpu.roll(tile, 0, 1, stride=width, stride_axis=0)
                turn = 1
                while turn < down:
                    turned = pltpu.roll(
                        tile.reshape(across, down, channels), down - turn, 1
                    ).reshape(channels, channels)
                    tile = jnp.where((lane & (turn * width)) != 0, turned, tile)
                    turn *= 2
                stages[n][k // 8, :, k % 8, :] = pltpu.roll(
                    tile, 0, 1, stride=width, stride_axis=0
                )
                if k % 8 == 7:
                    leave(n, k // 8).start()
    for n in range(count):
        for k in range(TAPS, 32):
            stages[n][k // 8, :, k % 8, :] = jnp.zeros((channels, channels), F32)
        leave(n, 3).start()
    for n in range(count):
        for eighth in range(4):
            leave(n, eighth).wait()


def weight_parts(cols, rhs, across, down, group=3, slots=3):
    rows, wide = cols.shape
    channels = wide // TAPS
    count = rhs.shape[1] // channels
    hbm = pl.BlockSpec(memory_space=pltpu.HBM)
    shape = (4, across * down, 8, channels)
    return pl.pallas_call(
        functools.partial(terms_kernel, across, down, group),
        in_specs=[hbm, pl.BlockSpec(memory_space=pltpu.VMEM)],
        out_specs=(hbm,) * count,
        out_shape=(pltpu.HBM(shape, F32),) * count,
        scratch_shapes=[pltpu.VMEM(shape, F32)] * count
        + [
            pltpu.VMEM(rhs.shape, BF16),
            pltpu.VMEM((slots, rows, group * channels), BF16),
            pltpu.SemaphoreType.DMA((slots,)),
            pltpu.SemaphoreType.DMA((count, 4)),
        ],
        compiler_params=pltpu.CompilerParams(vmem_limit_bytes=20 << 20),
        cost_estimate=pl.CostEstimate(
            flops=2 * rows * wide * channels * count, bytes_accessed=10 << 20, transcendentals=0
        ),
    )(pltpu.with_memory_space_constraint(cols, pltpu.HBM), rhs)


def combine_kernel(down, first_ref, second_ref, third_ref, scale_ref, out_ref, placed_ref):
    devices, taps, channels = out_ref.shape
    width = channels // down

    @pl.when(pl.program_id(0) == 0)
    def _():
        row = lax.broadcasted_iota(I32, (down, channels), 0)
        lane = lax.broadcasted_iota(I32, (down, channels), 1)
        spread = jnp.where(
            lax.broadcasted_iota(I32, (channels, channels), 0) % width
            == lax.broadcasted_iota(I32, (channels, channels), 1) % width,
            1.0,
            0.0,
        )
        for n in range(3):
            own = jnp.where(
                lane // width == row,
                jnp.broadcast_to(scale_ref[n : n + 1, :], (down, channels)),
                0.0,
            )
            placed_ref[n] = jnp.dot(
                own, spread, precision=lax.Precision.HIGHEST, preferred_element_type=F32
            )

    for d in range(devices):
        y = d % down
        scales = [placed_ref[n, y : y + 1, :] for n in range(3)]
        for e in range(taps // 8):
            out_ref[d, e * 8 : (e + 1) * 8, :] = (
                first_ref[e, d] * scales[0]
                - second_ref[e, d] * scales[1]
                - third_ref[e, d] * scales[2]
            ).astype(BF16)


def combine(first, second, third, scales, down, steps=4):
    eighths, devices, eight, channels = first.shape
    some = devices // steps
    spec = pl.BlockSpec((eighths, some, eight, channels), lambda d: (0, d, 0, 0))
    return pl.pallas_call(
        functools.partial(combine_kernel, down),
        grid=(steps,),
        in_specs=[spec, spec, spec, pl.BlockSpec(scales.shape, lambda d: (0, 0))],
        out_specs=pl.BlockSpec((some, eighths * eight, channels), lambda d: (d, 0, 0)),
        out_shape=jax.ShapeDtypeStruct((devices, eighths * eight, channels), BF16),
        scratch_shapes=[pltpu.VMEM((3, down, channels), F32)],
        compiler_params=pltpu.CompilerParams(vmem_limit_bytes=16 << 20),
        cost_estimate=pl.CostEstimate(flops=5 << 19, bytes_accessed=7 << 20, transcendentals=0),
    )(*(pltpu.with_memory_space_constraint(p, pltpu.HBM) for p in (first, second, third)), scales)


def from_neighbours(low, mid_low, mid_high, high, arrived=None):
    size = mid_low.shape[0]
    ends_x, ends_y = lax.axis_size("bx") - 1, lax.axis_size("by") - 1
    up_x, down_x = [(i, i + 1) for i in range(ends_x)], [(i + 1, i) for i in range(ends_x)]
    up_y, down_y = [(i, i + 1) for i in range(ends_y)], [(i + 1, i) for i in range(ends_y)]
    a0 = lax.ppermute(high, "bx", up_x)
    a2 = lax.ppermute(low, "bx", down_x)
    if arrived is not None:
        a0, a2, arrived = lax.optimization_barrier((a0, a2, arrived))
    b0 = lax.ppermute(jnp.concatenate([a0[2 * size :], mid_high, a2[2 * size :]]), "by", up_y)
    b2 = lax.ppermute(jnp.concatenate([a0[:size], mid_low, a2[:size]]), "by", down_y)
    return a0, a2, b0, b2, arrived


def everyones(rows):
    devices = lax.axis_size("bx") * lax.axis_size("by")
    copies = jnp.broadcast_to(rows[None], (devices,) + rows.shape)
    return lax.all_to_all(copies, axes, 0, 0, tiled=True)


def per_device(features, live_count, neighbour_map, send_rows, weight, gain, shift, cotangent):
    own_rows = features[0, 0]
    rows_total, channels = own_rows.shape
    size = send_rows.shape[3]
    block_rows = min(rows_total, 512)
    part = size * block_rows // rows_total
    across, down = lax.axis_size("bx"), lax.axis_size("by")
    sent_index = send_rows[0, 0].reshape(-1)
    send_select = (
        sent_index[:, None] == lax.broadcasted_iota(I32, (1, rows_total), 1)
    ).astype(BF16)
    chosen = jnp.dot(send_select, own_rows, preferred_element_type=F32).astype(BF16)
    a0, a2, b0, b2, _ = from_neighbours(
        chosen[: 3 * size], chosen[3 * size : 4 * size], chosen[4 * size : 5 * size], chosen[5 * size :]
    )

    indices = neighbour_map[0, 0]
    block = lax.broadcasted_iota(I32, (1, rows_total), 1) // block_rows
    beyond = indices - rows_total
    target = beyond // size
    inside = beyond - target * size - block * part
    remote = block_rows + (target - (target > 4)) * part + inside
    usable = (inside >= 0) & (inside < part) & (target != 4)
    place = jnp.where(
        indices < rows_total, indices - block * block_rows, jnp.where(usable, remote, -1)
    )
    place = jnp.pad(place, ((0, 5), (0, 0)), constant_values=-1)
    place_down = place.T
    place_rows = place.reshape(-1, rows_total // block_rows, block_rows).transpose(1, 0, 2)

    conv_out, cols = forward(place_down, own_rows, a0, a2, b0, b2, weight)
    conv_float = conv_out.astype(F32)
    live_mask = (lax.broadcasted_iota(I32, (rows_total, 1), 0) < live_count[0, 0]).astype(F32)
    local_count = live_count[0, 0].astype(F32)
    local_mean = jnp.sum(conv_float * live_mask, axis=0) / local_count
    local_dev = (conv_float - local_mean) * live_mask
    local_square = jnp.sum(local_dev * local_dev, axis=0)
    stats = everyones(
        jnp.stack([local_mean, local_square, jnp.full((channels,), local_count)])
    )
    both = jnp.concatenate(
        [jnp.broadcast_to(live_mask, (rows_total, channels)).astype(BF16), conv_out], axis=1
    )
    ones_part, conv_part = weight_parts(cols, both, across, down)
    stats, ones_part, conv_part = lax.optimization_barrier((stats, ones_part, conv_part))
    counts = stats[:, 2]
    total_count = jnp.sum(counts, axis=0)
    center = jnp.sum(stats[:, 0] * counts, axis=0) / total_count
    apart = stats[:, 0] - center
    variance = jnp.sum(stats[:, 1] + counts * apart * apart, axis=0) / total_count
    inverse_std = lax.rsqrt(variance + epsilon)
    normalized = (conv_float - center) * inverse_std
    before = gain * normalized + shift
    activated = (jnp.maximum(before, 0.0) * live_mask).astype(BF16)
    upstream = cotangent[0, 0].astype(F32) * (before > 0.0) * live_mask
    sums = everyones(
        jnp.stack([jnp.sum(upstream, axis=0), jnp.sum(upstream * normalized, axis=0)])
    )
    (up_part,) = weight_parts(cols, upstream.astype(BF16), across, down)
    sums, up_part = lax.optimization_barrier((sums, up_part))
    mean_up = jnp.sum(sums[:, 0], axis=0) / total_count
    mean_cross = jnp.sum(sums[:, 1], axis=0) / total_count
    scale = gain * inverse_std
    conv_grad = (
        scale * (upstream - live_mask * (mean_up + normalized * mean_cross))
    ).astype(BF16)

    scales = jnp.stack(
        [
            scale,
            scale * (mean_up - mean_cross * inverse_std * center),
            scale * mean_cross * inverse_std,
        ]
    )
    pieces = combine(up_part, ones_part, conv_part, scales, down)
    pieces, conv_grad = lax.optimization_barrier((pieces, conv_grad))
    arrived = lax.all_to_all(pieces, axes, 0, 0, tiled=True)
    own_table, *halo = backward(place_rows, place_down, conv_grad, weight, size)
    a0, a2, b0, b2, arrived = from_neighbours(*halo, arrived)
    slots_back = jnp.concatenate(
        [
            b0[:size], a0[size : 2 * size], b2[:size], b0[size : 2 * size],
            b2[size : 2 * size], b0[2 * size :], a2[size : 2 * size], b2[2 * size :],
        ]
    )
    added_back = lax.dot_general(
        send_select,
        slots_back,
        (((0,), (0,)), ((), ())),
        preferred_element_type=F32,
    )
    own_grad = (own_table + added_back).astype(BF16)
    summed = jnp.sum(arrived[:, :TAPS].astype(F32), axis=0)
    grad_weight = summed.reshape(TAPS, channels // across, channels // down) / jnp.sqrt(
        total_count[0]
    )
    return (activated[None, None], own_grad[None, None], grad_weight)


def solution(mesh):
    return jax.shard_map(
        per_device,
        mesh=mesh,
        in_specs=(
            P("bx", "by", None, None),
            P("bx", "by"),
            P("bx", "by", None, None),
            P("bx", "by", None, None),
            P(),
            P(),
            P(),
            P("bx", "by", None, None),
        ),
        out_specs=(P("bx", "by", None, None), P("bx", "by", None, None), P(None, "bx", "by")),
        check_vma=False,
    )
```

profile of v0, /device:TPU:1, one launch (start us, length us, event | category | flops | bytes accessed | tf_op | source)
XLA Modules:
  0.0 130.8 jit_solution(14308855287942663679)
XLA Ops:
  0.7 1.9 %fusion.6 = bf16[1024,128]{1,0:T(8,128)(2,1)S(1)} fusion(s32[1024]{0:T(1024)} %bitcast.72, bf16[1,1,1024,128]{3,2,1,0:T(8,128)(2,1)} %param.8), kind=kOutput, calls=%fused_computation.8 | convolution fusion | flops 269615104 | bytes 528384 | tf_op jit(solution)/shard_map/dot_general | solution.py:327
  2.6 1.3 collective-permute-start.1
  3.9 5.0 %collective-permute-start = (bf16[384,128]{1,0:T(8,128)(2,1)S(1)}, bf16[384,128]{1,0:T(8,128)(2,1)S(1)}, u32[]{:S(2)}, u32[]{:S(2)}) collective-permute-start(bf16[384,128]{1,0:T(8,128)(2,1)S(1)} %get-tuple-element.67), channel_id=1, source_target_pairs={{0,8},{8,16},{16,24},{24,32},{32,40},{40,48},{48,56},{56,64},{64,7... | collective-permute-start | bytes 294920 | tf_op jit(solution)/shard_map/ppermute | solution.py:301
  9.6 1.1 copy.28
  10.7 0.1 pad.20.clone
  10.7 0.9 fusion.31
  11.7 0.9 fusion.45
  12.5 0.0 collective-permute-done.1.a2_ref
  12.5 0.0 collective-permute-done.a0_ref
  12.6 4.1 %collective-permute-start.2 = (bf16[384,128]{1,0:T(8,128)(2,1)S(1)}, bf16[384,128]{1,0:T(8,128)(2,1)S(1)}, u32[]{:S(2)}, u32[]{:S(2)}) collective-permute-start(bf16[384,128]{1,0:T(8,128)(2,1)S(1)} %pad_maximum_fusion.1), channel_id=1, source_target_pairs={{0,1},{1,2},{2,3},{3,4},{4,5},{5,6},{6,7},{8,9},{9,10},{10,11},{11... | collective-permute-start | bytes 294920 | tf_op jit(solution)/shard_map/ppermute | solution.py:305
  16.7 1.9 %collective-permute-start.3 = (bf16[384,128]{1,0:T(8,128)(2,1)S(1)}, bf16[384,128]{1,0:T(8,128)(2,1)S(1)}, u32[]{:S(2)}, u32[]{:S(2)}) collective-permute-start(bf16[384,128]{1,0:T(8,128)(2,1)S(1)} %pad_maximum_fusion.2), channel_id=1, source_target_pairs={{1,0},{2,1},{3,2},{4,3},{5,4},{6,5},{7,6},{9,8},{10,9},{11,10},{12... | collective-permute-start | bytes 294920 | tf_op jit(solution)/shard_map/ppermute | solution.py:306
  18.7 4.0 %collective-permute-done.3.b2_ref = bf16[384,128]{1,0:T(8,128)(2,1)S(1)} collective-permute-done((bf16[384,128]{1,0:T(8,128)(2,1)S(1)}, bf16[384,128]{1,0:T(8,128)(2,1)S(1)}, u32[]{:S(2)}, u32[]{:S(2)}) %collective-permute-start.3) | collective-permute-done | bytes 98336 | tf_op jit(solution)/shard_map/ppermute | solution.py:306
  22.7 11.8 %shard_map.103 = (bf16[1024,128]{1,0:T(8,128)(2,1)S(1)}, bf16[1024,3456]{1,0:T(8,128)(2,1)}) custom-call(s32[1024,32]{1,0:T(8,128)S(1)} %get-tuple-element.61.place_ref, bf16[1024,128]{1,0:T(8,128)(2,1)S(1)} %bitcast.61, bf16[384,128]{1,0:T(8,128)(2,1)S(1)} %collective-permute-done.a0_ref, bf16[384,128]{1,0:T(8,128)(2,1)S(1)} %collective-permute-done.1.a2_ref, ...), custom_call_target="tpu_custom_call" | custom-call | flops 7247757312 | bytes 9437184 | tf_op jit(solution)/shard_map/pallas_call | solution.py:74
  34.4 0.2 fusion.9
  34.7 0.2 fusion.12
  34.9 0.1 maximum_maximum_fusion
  35.0 0.7 broadcast_in_dim.10
  35.7 12.0 %all-to-all-start = ((f32[128,3,128]{2,1,0:T(4,128)}), f32[128,3,128]{2,1,0:T(4,128)S(1)}, u32[]{:S(2)}, u32[]{:S(2)}) async-start(f32[128,3,128]{2,1,0:T(4,128)} %broadcast_in_dim.10), calls=%async_computation | async-start | bytes 524288 | tf_op jit(solution)/shard_map/all_to_all | solution.py:313
  47.7 0.2 mul.139
  47.9 0.1 pad_maximum_fusion.rhs_ref
  48.0 0.0 copy-start.3
  48.0 0.0 copy-start.4
  48.0 0.0 copy-start.5
  48.0 10.3 %shard_map.104 = (f32[4,128,8,128]{3,2,1,0:T(8,128)}, f32[4,128,8,128]{3,2,1,0:T(8,128)}) custom-call(bf16[1024,3456]{1,0:T(8,128)(2,1)} %get-tuple-element.23.cols_ref, bf16[1024,256]{1,0:T(8,128)(2,1)S(1)} %pad_maximum_fusion.rhs_ref), custom_call_target="tpu_custom_call" | custom-call | flops 1811939328 | bytes 10485760 | tf_op jit(solution)/shard_map/pallas_call | solution.py:226
  58.3 0.2 all-to-all-done
  58.5 0.1 slice.92
  58.7 0.2 fusion.30
  59.0 0.7 broadcast_in_dim.12
  59.7 9.6 %all-to-all-start.1 = ((f32[128,2,128]{2,1,0:T(2,128)}), f32[128,2,128]{2,1,0:T(2,128)S(1)}, u32[]{:S(2)}, u32[]{:S(2)}) async-start(f32[128,2,128]{2,1,0:T(2,128)} %broadcast_in_dim.12), calls=%async_computation.1 | async-start | bytes 262144 | tf_op jit(solution)/shard_map/all_to_all | solution.py:313
  69.3 8.8 %shard_map.105.first_ref = f32[4,128,8,128]{3,2,1,0:T(8,128)} custom-call(bf16[1024,3456]{1,0:T(8,128)(2,1)} %get-tuple-element.23.cols_ref, bf16[1024,128]{1,0:T(8,128)(2,1)S(1)} %get-tuple-element.59.rhs_ref), custom_call_target="tpu_custom_call" | custom-call | flops 905969664 | bytes 10485760 | tf_op jit(solution)/shard_map/pallas_call | solution.py:226
  78.1 1.2 all-to-all-done.1
  79.2 0.1 fusion.48
  79.4 1.0 fusion.27
  80.4 4.8 %shard_map.106 = bf16[128,32,128]{2,1,0:T(8,128)(2,1)} custom-call(f32[4,128,8,128]{3,2,1,0:T(8,128)} %shard_map.105.first_ref, f32[4,128,8,128]{3,2,1,0:T(8,128)} %get-tuple-element.28.second_ref, f32[4,128,8,128]{3,2,1,0:T(8,128)} %get-tuple-element.29.third_ref, f32[3,128]{1,0:T(4,128)S(1)} %pad_maximum_fusion.5.scale_ref), custom_call_target="tpu_custom_call" | custom-call | flops 2621440 | bytes 7340032 | tf_op jit(solution)/shard_map/pallas_call | solution.py:284
  85.2 8.6 %all-to-all-start.2 = ((bf16[128,32,128]{2,1,0:T(8,128)(2,1)}), bf16[128,32,128]{2,1,0:T(8,128)(2,1)S(1)}, u32[]{:S(2)}, u32[]{:S(2)}) async-start(bf16[128,32,128]{2,1,0:T(8,128)(2,1)} %shard_map.106), calls=%async_computation.2 | async-start | bytes 2097152 | tf_op jit(solution)/shard_map/all_to_all | solution.py:392
  93.9 0.2 copy.31
  94.0 12.6 %shard_map.107 = (f32[1024,128]{1,0:T(8,128)S(1)}, bf16[384,128]{1,0:T(8,128)(2,1)S(1)}, bf16[128,128]{1,0:T(8,128)(2,1)S(1)}, bf16[128,128]{1,0:T(8,128)(2,1)S(1)}, bf16[384,128]{1,0:T(8,128)(2,1)S(1)}) custom-call(s32[2,32,512]{2,1,0:T(8,128)S(1)} %bitcast.60, s32[1024,32]{1,0:T(8,128)S(1)} %get-tuple-element.61.place_ref, ...), custom_call_target="tpu_custom_call" | custom-call | flops 8153726976 | bytes 2097152 | tf_op jit(solution)/shard_map/pallas_call | solution.py:134
  106.6 3.4 %collective-permute-start.4 = (bf16[384,128]{1,0:T(8,128)(2,1)S(1)}, bf16[384,128]{1,0:T(8,128)(2,1)S(1)}, u32[]{:S(2)}, u32[]{:S(2)}) collective-permute-start(bf16[384,128]{1,0:T(8,128)(2,1)S(1)} %get-tuple-element.33), channel_id=1, source_target_pairs={{0,8},{8,16},{16,24},{24,32},{32,40},{40,48},{48,56},{56,64},{64,7... | collective-permute-start | bytes 294920 | tf_op jit(solution)/shard_map/ppermute | solution.py:301
  110.0 1.3 collective-permute-start.5
  111.4 0.4 collective-permute-done.4
  111.8 3.6 %collective-permute-done.5 = bf16[384,128]{1,0:T(8,128)(2,1)S(1)} collective-permute-done((bf16[384,128]{1,0:T(8,128)(2,1)S(1)}, bf16[384,128]{1,0:T(8,128)(2,1)S(1)}, u32[]{:S(2)}, u32[]{:S(2)}) %collective-permute-start.5) | collective-permute-done | bytes 98336 | tf_op jit(solution)/shard_map/ppermute | solution.py:302
  115.4 4.8 %collective-permute-start.6 = (bf16[384,128]{1,0:T(8,128)(2,1)S(1)}, bf16[384,128]{1,0:T(8,128)(2,1)S(1)}, u32[]{:S(2)}, u32[]{:S(2)}) collective-permute-start(bf16[384,128]{1,0:T(8,128)(2,1)S(1)} %pad_maximum_fusion.3), channel_id=1, source_target_pairs={{0,1},{1,2},{2,3},{3,4},{4,5},{5,6},{6,7},{8,9},{9,10},{10,11},{11... | collective-permute-start | bytes 294920 | tf_op jit(solution)/shard_map/ppermute | solution.py:305
  120.3 0.2 convert_reduce_fusion
  120.5 1.4 %collective-permute-done.6 = bf16[384,128]{1,0:T(8,128)(2,1)S(1)} collective-permute-done((bf16[384,128]{1,0:T(8,128)(2,1)S(1)}, bf16[384,128]{1,0:T(8,128)(2,1)S(1)}, u32[]{:S(2)}, u32[]{:S(2)}) %collective-permute-start.6) | collective-permute-done | bytes 98336 | tf_op jit(solution)/shard_map/ppermute | solution.py:305
  121.9 1.9 %collective-permute-start.7 = (bf16[384,128]{1,0:T(8,128)(2,1)S(1)}, bf16[384,128]{1,0:T(8,128)(2,1)S(1)}, u32[]{:S(2)}, u32[]{:S(2)}) collective-permute-start(bf16[384,128]{1,0:T(8,128)(2,1)S(1)} %pad_maximum_fusion.4), channel_id=1, source_target_pairs={{1,0},{2,1},{3,2},{4,3},{5,4},{6,5},{7,6},{9,8},{10,9},{11,10},{12... | collective-permute-start | bytes 294920 | tf_op jit(solution)/shard_map/ppermute | solution.py:306
  123.9 0.7 copy.35
  124.6 3.9 %collective-permute-done.7 = bf16[384,128]{1,0:T(8,128)(2,1)S(1)} collective-permute-done((bf16[384,128]{1,0:T(8,128)(2,1)S(1)}, bf16[384,128]{1,0:T(8,128)(2,1)S(1)}, u32[]{:S(2)}, u32[]{:S(2)}) %collective-permute-start.7) | collective-permute-done | bytes 98336 | tf_op jit(solution)/shard_map/ppermute | solution.py:306
  128.6 2.2 %fusion.7 = bf16[1,1,1024,128]{3,2,1,0:T(8,128)(2,1)} fusion(f32[1024,128]{1,0:T(8,128)S(1)} %get-tuple-element.32, bf16[1024,128]{1,0:T(8,128)(2,1)S(1)} %slice_dynamic-update-slice_fusion, s32[1024]{0:T(1024)S(1)} %bitcast.73), kind=kOutput, calls=%fused_computation.9 | convolution fusion | flops 269746176 | bytes 1052672 | tf_op jit(solution)/shard_map/dot_general | solution.py:401
  (48 shorter events, 0.4 us)
Async XLA Ops:
  0.6 22.0 %copy-start.1 = (bf16[1,1,1024,128]{3,2,1,0:T(8,128)(2,1)S(1)}, bf16[1,1,1024,128]{3,2,1,0:T(8,128)(2,1)}, u32[]{:S(2)}) copy-start(bf16[1,1,1024,128]{3,2,1,0:T(8,128)(2,1)} %param.8) | copy-start | bytes 786436
  0.6 22.0 %copy-start = (bf16[3456,128]{1,0:T(8,128)(2,1)S(1)}, bf16[3456,128]{1,0:T(8,128)(2,1)}, u32[]{:S(2)}) copy-start(bf16[3456,128]{1,0:T(8,128)(2,1)} %weight_ref.3) | copy-start | bytes 2654212
  2.6 10.0 %collective-permute-start.1 = (bf16[384,128]{1,0:T(8,128)(2,1)S(1)}, bf16[384,128]{1,0:T(8,128)(2,1)S(1)}, u32[]{:S(2)}, u32[]{:S(2)}) collective-permute-start(bf16[384,128]{1,0:T(8,128)(2,1)S(1)} %get-tuple-element.66), channel_id=1, source_target_pairs={{8,0},{16,8},{24,16},{32,24},{40,32},{48,40},{56,48},{64,56},{72,6... | collective-permute-start | bytes 294920 | tf_op jit(solution)/shard_map/ppermute | solution.py:302
  3.9 8.7 %collective-permute-start = (bf16[384,128]{1,0:T(8,128)(2,1)S(1)}, bf16[384,128]{1,0:T(8,128)(2,1)S(1)}, u32[]{:S(2)}, u32[]{:S(2)}) collective-permute-start(bf16[384,128]{1,0:T(8,128)(2,1)S(1)} %get-tuple-element.67), channel_id=1, source_target_pairs={{0,8},{8,16},{16,24},{24,32},{32,40},{40,48},{48,56},{56,64},{64,7... | collective-permute-start | bytes 294920 | tf_op jit(solution)/shard_map/ppermute | solution.py:301
  12.6 6.1 %collective-permute-start.2 = (bf16[384,128]{1,0:T(8,128)(2,1)S(1)}, bf16[384,128]{1,0:T(8,128)(2,1)S(1)}, u32[]{:S(2)}, u32[]{:S(2)}) collective-permute-start(bf16[384,128]{1,0:T(8,128)(2,1)S(1)} %pad_maximum_fusion.1), channel_id=1, source_target_pairs={{0,1},{1,2},{2,3},{3,4},{4,5},{5,6},{6,7},{8,9},{9,10},{10,11},{11... | collective-permute-start | bytes 294920 | tf_op jit(solution)/shard_map/ppermute | solution.py:305
  16.7 5.9 %collective-permute-start.3 = (bf16[384,128]{1,0:T(8,128)(2,1)S(1)}, bf16[384,128]{1,0:T(8,128)(2,1)S(1)}, u32[]{:S(2)}, u32[]{:S(2)}) collective-permute-start(bf16[384,128]{1,0:T(8,128)(2,1)S(1)} %pad_maximum_fusion.2), channel_id=1, source_target_pairs={{1,0},{2,1},{3,2},{4,3},{5,4},{6,5},{7,6},{9,8},{10,9},{11,10},{12... | collective-permute-start | bytes 294920 | tf_op jit(solution)/shard_map/ppermute | solution.py:306
  35.7 22.7 %all-to-all-start = ((f32[128,3,128]{2,1,0:T(4,128)}), f32[128,3,128]{2,1,0:T(4,128)S(1)}, u32[]{:S(2)}, u32[]{:S(2)}) async-start(f32[128,3,128]{2,1,0:T(4,128)} %broadcast_in_dim.10), calls=%async_computation | async-start | bytes 524288 | tf_op jit(solution)/shard_map/all_to_all | solution.py:313
  48.0 10.7 %copy-start.3 = (bf16[1,1,1024,128]{3,2,1,0:T(8,128)(2,1)S(1)}, bf16[1,1,1024,128]{3,2,1,0:T(8,128)(2,1)}, u32[]{:S(2)}) copy-start(bf16[1,1,1024,128]{3,2,1,0:T(8,128)(2,1)} %param.15) | copy-start | bytes 786436
  48.0 10.7 %copy-start.4 = (f32[128]{0:T(128)S(1)}, f32[128]{0:T(128)}, u32[]{:S(2)}) copy-start(f32[128]{0:T(128)} %param.13) | copy-start | bytes 1540
  48.0 10.7 %copy-start.5 = (f32[128]{0:T(128)S(1)}, f32[128]{0:T(128)}, u32[]{:S(2)}) copy-start(f32[128]{0:T(128)} %param.14) | copy-start | bytes 1540
  59.7 19.5 %all-to-all-start.1 = ((f32[128,2,128]{2,1,0:T(2,128)}), f32[128,2,128]{2,1,0:T(2,128)S(1)}, u32[]{:S(2)}, u32[]{:S(2)}) async-start(f32[128,2,128]{2,1,0:T(2,128)} %broadcast_in_dim.12), calls=%async_computation.1 | async-start | bytes 262144 | tf_op jit(solution)/shard_map/all_to_all | solution.py:313
  80.4 13.4 %copy-start.2 = (s32[32,1024]{0,1:T(8,128)S(1)}, s32[32,1024]{0,1:T(8,128)}, u32[]{:S(2)}) copy-start(s32[32,1024]{0,1:T(8,128)} %get-tuple-element.60) | copy-start | bytes 393220
  85.2 30.2 %all-to-all-start.2 = ((bf16[128,32,128]{2,1,0:T(8,128)(2,1)}), bf16[128,32,128]{2,1,0:T(8,128)(2,1)S(1)}, u32[]{:S(2)}, u32[]{:S(2)}) async-start(bf16[128,32,128]{2,1,0:T(8,128)(2,1)} %shard_map.106), calls=%async_computation.2 | async-start | bytes 2097152 | tf_op jit(solution)/shard_map/all_to_all | solution.py:392
  94.0 34.6 %copy-start.6 = (s32[1,1,8,128]{3,2,1,0:T(8,128)S(1)}, s32[1,1,8,128]{3,2,1,0:T(8,128)}, u32[]{:S(2)}) copy-start(s32[1,1,8,128]{3,2,1,0:T(8,128)} %param.11) | copy-start | bytes 12292
  106.6 5.2 %collective-permute-start.4 = (bf16[384,128]{1,0:T(8,128)(2,1)S(1)}, bf16[384,128]{1,0:T(8,128)(2,1)S(1)}, u32[]{:S(2)}, u32[]{:S(2)}) collective-permute-start(bf16[384,128]{1,0:T(8,128)(2,1)S(1)} %get-tuple-element.33), channel_id=1, source_target_pairs={{0,8},{8,16},{16,24},{24,32},{32,40},{40,48},{48,56},{56,64},{64,7... | collective-permute-start | bytes 294920 | tf_op jit(solution)/shard_map/ppermute | solution.py:301
  110.0 5.4 %collective-permute-start.5 = (bf16[384,128]{1,0:T(8,128)(2,1)S(1)}, bf16[384,128]{1,0:T(8,128)(2,1)S(1)}, u32[]{:S(2)}, u32[]{:S(2)}) collective-permute-start(bf16[384,128]{1,0:T(8,128)(2,1)S(1)} %get-tuple-element.34), channel_id=1, source_target_pairs={{8,0},{16,8},{24,16},{32,24},{40,32},{48,40},{56,48},{64,56},{72,6... | collective-permute-start | bytes 294920 | tf_op jit(solution)/shard_map/ppermute | solution.py:302
  115.4 6.5 %collective-permute-start.6 = (bf16[384,128]{1,0:T(8,128)(2,1)S(1)}, bf16[384,128]{1,0:T(8,128)(2,1)S(1)}, u32[]{:S(2)}, u32[]{:S(2)}) collective-permute-start(bf16[384,128]{1,0:T(8,128)(2,1)S(1)} %pad_maximum_fusion.3), channel_id=1, source_target_pairs={{0,1},{1,2},{2,3},{3,4},{4,5},{5,6},{6,7},{8,9},{9,10},{10,11},{11... | collective-permute-start | bytes 294920 | tf_op jit(solution)/shard_map/ppermute | solution.py:305
  121.9 6.6 %collective-permute-start.7 = (bf16[384,128]{1,0:T(8,128)(2,1)S(1)}, bf16[384,128]{1,0:T(8,128)(2,1)S(1)}, u32[]{:S(2)}, u32[]{:S(2)}) collective-permute-start(bf16[384,128]{1,0:T(8,128)(2,1)S(1)} %pad_maximum_fusion.4), channel_id=1, source_target_pairs={{1,0},{2,1},{3,2},{4,3},{5,4},{6,5},{7,6},{9,8},{10,9},{11,10},{12... | collective-permute-start | bytes 294920 | tf_op jit(solution)/shard_map/ppermute | solution.py:306
where the time goes:
time: 131 us
  starting transfers between devices  54 us (41%)
  Pallas kernels  48.2 us (37%)
  waiting for transfers between devices  14.7 us (11%)
  local copies, waits for them, and re-layouts  4.91 us (4%)
  matrix products  4.04 us (3%)
  other arithmetic  3.24 us (2%)
  between operations  1.76 us (1%)
    all_to_all x2, starting transfers between devices, everyones(): return lax.all_to_all(copies, axes, 0, 0, tiled=True)  21.6 us
    pallas_call x2, Pallas kernels, weight_parts(): pl.pallas_call(functools.partial(terms_kernel, across, down, group), in_s...  19 us
    pallas_call x1, Pallas kernels, backward(): pl.pallas_call(functools.partial(backward_kernel, group), out_shape=(jax....  12.6 us
    pallas_call x1, Pallas kernels, forward(): pl.pallas_call(functools.partial(forward_kernel, chunks), in_specs=[vmem]...  11.8 us
    ppermute x2, starting transfers between devices, from_neighbours(): lax.ppermute(jnp.concatenate([a0[2 * size:], mid_high, a2[2 * size:]]), '...  8.97 us
    all_to_all x1, starting transfers between devices, per_device(): arrived = lax.all_to_all(pieces, axes, 0, 0, tiled=True)  8.62 us
    ppermute x2, starting transfers between devices, from_neighbours(): a0 = lax.ppermute(high, 'bx', up_x)  8.42 us
    ppermute x2, waiting for transfers between devices, from_neighbours(): lax.ppermute(jnp.concatenate([a0[:size], mid_low, a2[:size]]), 'by', down_y)  7.91 us
  transfers between devices with their start and end apart: 11, of which 7 were waited for; matrix products, arithmetic and copies ran while one was open for 3% of the time, Pallas kernels for 24%

commit v1 on v0

--- a/solution.py
+++ b/solution.py
@@ -150,147 +150,69 @@
     )(row, place, grad, weight)
 
 
-def terms_kernel(across, down, group, cols_ref, rhs_ref, *refs):
-    count = (len(refs) - 4) // 2
-    outs, stages = refs[:count], refs[count : 2 * count]
-    mirror_ref, buffer_ref, in_sems, out_sems = refs[2 * count :]
-    channels = cols_ref.shape[1] // TAPS
-    width = channels // down
+def weight_kernel(across, down, group, cols_ref, grad_ref, order_ref, out_ref, line_ref, buffer_ref, sems):
+    channels = grad_ref.shape[1]
+    eighths = out_ref.shape[1]
     slots = buffer_ref.shape[0]
-    row = lax.broadcasted_iota(I32, (channels, channels), 0)
-    lane = lax.broadcasted_iota(I32, (channels, channels), 1)
     steps = TAPS // group
 
     def fetch(step):
         return pltpu.make_async_copy(
             cols_ref.at[:, pl.ds(step * group * channels, group * channels)],
             buffer_ref.at[step % slots],
-            in_sems.at[step % slots],
-        )
-
-    def leave(n, eighth):
-        return pltpu.make_async_copy(
-            stages[n].at[eighth], outs[n].at[eighth], out_sems.at[n, eighth]
+            sems.at[step % slots],
+        )
+
+    def line(k):
+        return (
+            slice(k // 8 * channels, (k // 8 + 1) * channels),
+            slice(k % 8 * channels, (k % 8 + 1) * channels),
         )
 
     for step in range(slots - 1):
         fetch(step).start()
-    mirror = jnp.where(
-        row == (down - lane // width) % down * width + lane % width, 1.0, 0.0
-    ).astype(BF16)
-    for n in range(count):
-        part = slice(n * channels, (n + 1) * channels)
-        mirror_ref[:, part] = jnp.dot(
-            rhs_ref[:, part], mirror, preferred_element_type=F32
-        ).astype(BF16)
+    for k in range(TAPS, 8 * eighths):
+        line_ref[line(k)] = jnp.zeros((channels, channels), BF16)
+    turned = grad_ref[...].T
     for step in range(steps):
         if step + slots - 1 < steps:
             fetch(step + slots - 1).start()
         fetch(step).wait()
-        whole = lax.dot_general(
-            buffer_ref[step % slots], mirror_ref[...],
-            (((0,), (0,)), ((), ())), preferred_element_type=F32,
-        )
-        for n in range(count):
-            for k in range(step * group, (step + 1) * group):
-                at = (k - step * group) * channels
-                tile = whole[at : at + channels, n * channels : (n + 1) * channels]
-                tile = pltpu.roll(tile, 0, 1, stride=width, stride_axis=0)
-                turn = 1
-                while turn < down:
-                    turned = pltpu.roll(
-                        tile.reshape(across, down, channels), down - turn, 1
-                    ).reshape(channels, channels)
-                    tile = jnp.where((lane & (turn * width)) != 0, turned, tile)
-                    turn *= 2
-                stages[n][k // 8, :, k % 8, :] = pltpu.roll(
-                    tile, 0, 1, stride=width, stride_axis=0
-                )
-                if k % 8 == 7:
-                    leave(n, k // 8).start()
-    for n in range(count):
-        for k in range(TAPS, 32):
-            stages[n][k // 8, :, k % 8, :] = jnp.zeros((channels, channels), F32)
-        leave(n, 3).start()
-    for n in range(count):
-        for eighth in range(4):
-            leave(n, eighth).wait()
-
-
-def weight_parts(cols, rhs, across, down, group=3, slots=3):
+        whole = jnp.dot(turned, buffer_ref[step % slots], preferred_element_type=F32)
+        for n in range(group):
+            line_ref[line(step * group + n)] = (
+                whole[:, n * channels : (n + 1) * channels].T.astype(BF16)
+            )
+    placed = jnp.dot(line_ref[...], order_ref[...], preferred_element_type=F32).astype(BF16)
+    for e in range(eighths):
+        for x in range(across):
+            for y in range(down):
+                row = e * channels + x * down
+                out_ref[x * down + y, e] = placed[
+                    row : row + down, y * channels : (y + 1) * channels
+                ]
+
+
+def weight_terms(cols, grad, order, across, down, group=3, slots=3):
     rows, wide = cols.shape
     channels = wide // TAPS
-    count = rhs.shape[1] // channels
-    hbm = pl.BlockSpec(memory_space=pltpu.HBM)
-    shape = (4, across * down, 8, channels)
+    eighths = -(-TAPS // 8)
+    vmem = pl.BlockSpec(memory_space=pltpu.VMEM)
     return pl.pallas_call(
-        functools.partial(terms_kernel, across, down, group),
-        in_specs=[hbm, pl.BlockSpec(memory_space=pltpu.VMEM)],
-        out_specs=(hbm,) * count,
-        out_shape=(pltpu.HBM(shape, F32),) * count,
-        scratch_shapes=[pltpu.VMEM(shape, F32)] * count
-        + [
-            pltpu.VMEM(rhs.shape, BF16),
+        functools.partial(weight_kernel, across, down, group),
+        in_specs=[pl.BlockSpec(memory_space=pltpu.HBM), vmem, vmem],
+        out_specs=vmem,
+        out_shape=jax.ShapeDtypeStruct((across * down, eighths, down, channels), BF16),
+        scratch_shapes=[
+            pltpu.VMEM((eighths * channels, 8 * channels), BF16),
             pltpu.VMEM((slots, rows, group * channels), BF16),
             pltpu.SemaphoreType.DMA((slots,)),
-            pltpu.SemaphoreType.DMA((count, 4)),
         ],
-        compiler_params=pltpu.CompilerParams(vmem_limit_bytes=20 << 20),
+        compiler_params=pltpu.CompilerParams(vmem_limit_bytes=24 << 20),
         cost_estimate=pl.CostEstimate(
-            flops=2 * rows * wide * channels * count, bytes_accessed=10 << 20, transcendentals=0
-        ),
-    )(pltpu.with_memory_space_constraint(cols, pltpu.HBM), rhs)
-
-
-def combine_kernel(down, first_ref, second_ref, third_ref, scale_ref, out_ref, placed_ref):
-    devices, taps, channels = out_ref.shape
-    width = channels // down
-
-    @pl.when(pl.program_id(0) == 0)
-    def _():
-        row = lax.broadcasted_iota(I32, (down, channels), 0)
-        lane = lax.broadcasted_iota(I32, (down, channels), 1)
-        spread = jnp.where(
-            lax.broadcasted_iota(I32, (channels, channels), 0) % width
-            == lax.broadcasted_iota(I32, (channels, channels), 1) % width,
-            1.0,
-            0.0,
-        )
-        for n in range(3):
-            own = jnp.where(
-                lane // width == row,
-                jnp.broadcast_to(scale_ref[n : n + 1, :], (down, channels)),
-                0.0,
-            )
-            placed_ref[n] = jnp.dot(
-                own, spread, precision=lax.Precision.HIGHEST, preferred_element_type=F32
-            )
-
-    for d in range(devices):
-        y = d % down
-        scales = [placed_ref[n, y : y + 1, :] for n in range(3)]
-        for e in range(taps // 8):
-            out_ref[d, e * 8 : (e + 1) * 8, :] = (
-                first_ref[e, d] * scales[0]
-                - second_ref[e, d] * scales[1]
-                - third_ref[e, d] * scales[2]
-            ).astype(BF16)
-
-
-def combine(first, second, third, scales, down, steps=4):
-    eighths, devices, eight, channels = first.shape
-    some = devices // steps
-    spec = pl.BlockSpec((eighths, some, eight, channels), lambda d: (0, d, 0, 0))
-    return pl.pallas_call(
-        functools.partial(combine_kernel, down),
-        grid=(steps,),
-        in_specs=[spec, spec, spec, pl.BlockSpec(scales.shape, lambda d: (0, 0))],
-        out_specs=pl.BlockSpec((some, eighths * eight, channels), lambda d: (d, 0, 0)),
-        out_shape=jax.ShapeDtypeStruct((devices, eighths * eight, channels), BF16),
-        scratch_shapes=[pltpu.VMEM((3, down, channels), F32)],
-        compiler_params=pltpu.CompilerParams(vmem_limit_bytes=16 << 20),
-        cost_estimate=pl.CostEstimate(flops=5 << 19, bytes_accessed=7 << 20, transcendentals=0),
-    )(*(pltpu.with_memory_space_constraint(p, pltpu.HBM) for p in (first, second, third)), scales)
+            flops=2 * rows * wide * channels, bytes_accessed=10 << 20, transcendentals=0
+        ),
+    )(pltpu.with_memory_space_constraint(cols, pltpu.HBM), grad, order)
 
 
 def from_neighbours(low, mid_low, mid_high, high, arrived=None):
@@ -353,11 +275,6 @@
     stats = everyones(
         jnp.stack([local_mean, local_square, jnp.full((channels,), local_count)])
     )
-    both = jnp.concatenate(
-        [jnp.broadcast_to(live_mask, (rows_total, channels)).astype(BF16), conv_out], axis=1
-    )
-    ones_part, conv_part = weight_parts(cols, both, across, down)
-    stats, ones_part, conv_part = lax.optimization_barrier((stats, ones_part, conv_part))
     counts = stats[:, 2]
     total_count = jnp.sum(counts, axis=0)
     center = jnp.sum(stats[:, 0] * counts, axis=0) / total_count
@@ -371,8 +288,6 @@
     sums = everyones(
         jnp.stack([jnp.sum(upstream, axis=0), jnp.sum(upstream * normalized, axis=0)])
     )
-    (up_part,) = weight_parts(cols, upstream.astype(BF16), across, down)
-    sums, up_part = lax.optimization_barrier((sums, up_part))
     mean_up = jnp.sum(sums[:, 0], axis=0) / total_count
     mean_cross = jnp.sum(sums[:, 1], axis=0) / total_count
     scale = gain * inverse_std
@@ -380,14 +295,13 @@
         scale * (upstream - live_mask * (mean_up + normalized * mean_cross))
     ).astype(BF16)
 
-    scales = jnp.stack(
-        [
-            scale,
-            scale * (mean_up - mean_cross * inverse_std * center),
-            scale * mean_cross * inverse_std,
-        ]
-    )
-    pieces = combine(up_part, ones_part, conv_part, scales, down)
+    width = channels // down
+    source = lax.broadcasted_iota(I32, (8 * channels, 1), 0)
+    spot = lax.broadcasted_iota(I32, (1, down * channels), 1)
+    order = (
+        source == (spot // width) % 8 * channels + spot // channels * width + spot % width
+    ).astype(BF16)
+    pieces = weight_terms(cols, conv_grad, order, across, down)
     pieces, conv_grad = lax.optimization_barrier((pieces, conv_grad))
     arrived = lax.all_to_all(pieces, axes, 0, 0, tiled=True)
     own_table, *halo = backward(place_rows, place_down, conv_grad, weight, size)
@@ -405,8 +319,8 @@
         preferred_element_type=F32,
     )
     own_grad = (own_table + added_back).astype(BF16)
-    summed = jnp.sum(arrived[:, :TAPS].astype(F32), axis=0)
-    grad_weight = summed.reshape(TAPS, channels // across, channels // down) / jnp.sqrt(
+    summed = jnp.sum(arrived.astype(F32), axis=0).reshape(-1, down, 8, width)
+    grad_weight = summed.transpose(0, 2, 1, 3).reshape(-1, down, width)[:TAPS] / jnp.sqrt(
         total_count[0]
     )
     return (activated[None, None], own_grad[None, None], grad_weight)

time: 131 us -> 126 us (0.962)
  waiting for transfers between devices: 14.7 us -> 33.5 us
  Pallas kernels: 48.2 us -> 31.5 us
  starting transfers between devices: 54 us -> 43.1 us
  local copies, waits for them, and re-layouts: 4.91 us -> 7.17 us
    all_to_all x2, waiting for transfers between devices: 1.35 us -> 19.8 us  [everyones(): return lax.all_to_all(copies, axes, 0, 0, tiled=True)]
    pallas_call x3 -> x1, Pallas kernels: 23.8 us -> 7.18 us  [weight_terms(): pl.pallas_call(functools.partial(weight_kernel, across, down, group), in_...]
    all_to_all x2, starting transfers between devices: 21.6 us -> 14.8 us  [everyones(): return lax.all_to_all(copies, axes, 0, 0, tiled=True)]
    all_to_all x1, starting transfers between devices: 8.62 us -> 4.3 us  [per_device(): arrived = lax.all_to_all(pieces, axes, 0, 0, tiled=True)]
  transfers between devices with their start and end apart: 11 -> 11, of which waited for: 7 -> 8; matrix products, arithmetic and copies ran while one was open for 3% -> 5% of each run, Pallas kernels for 24% -> 10%
where the time goes in v1:
time: 126 us; the launch traced here: 125 us
  starting transfers between devices  43.1 us (34%)
  waiting for transfers between devices  33.5 us (27%)
  Pallas kernels  31.5 us (25%)
  local copies, waits for them, and re-layouts  7.17 us (6%)
  matrix products  4.04 us (3%)
  other arithmetic  4.03 us (3%)
  between operations  1.74 us (1%)
    all_to_all x2, waiting for transfers between devices, everyones(): return lax.all_to_all(copies, axes, 0, 0, tiled=True)  19.8 us
    all_to_all x2, starting transfers between devices, everyones(): return lax.all_to_all(copies, axes, 0, 0, tiled=True)  14.8 us
    pallas_call x1, Pallas kernels, backward(): pl.pallas_call(functools.partial(backward_kernel, group), out_shape=(jax....  12.6 us
    pallas_call x1, Pallas kernels, forward(): pl.pallas_call(functools.partial(forward_kernel, chunks), in_specs=[vmem]...  11.8 us
    ppermute x2, starting transfers between devices, from_neighbours(): lax.ppermute(jnp.concatenate([a0[2 * size:], mid_high, a2[2 * size:]]), '...  9.84 us
    ppermute x2, waiting for transfers between devices, from_neighbours(): lax.ppermute(jnp.concatenate([a0[:size], mid_low, a2[:size]]), 'by', down_y)  7.88 us
    ppermute x2, starting transfers between devices, from_neighbours(): a0 = lax.ppermute(high, 'bx', up_x)  7.79 us
    pallas_call x1, Pallas kernels, weight_terms(): pl.pallas_call(functools.partial(weight_kernel, across, down, group), in_...  7.18 us
  transfers between devices with their start and end apart: 11, of which 8 were waited for; matrix products, arithmetic and copies ran while one was open for 5% of the time, Pallas kernels for 10%

profile of v1, /device:TPU:1, one launch (start us, length us, event | category | flops | bytes accessed | tf_op | source)
XLA Modules:
  0.0 125.2 jit_solution(337658535760294660)
XLA Ops:
  0.6 0.0 copy-start
  0.7 1.9 %fusion.7 = bf16[1024,128]{1,0:T(8,128)(2,1)S(1)} fusion(s32[1024]{0:T(1024)} %bitcast.67, bf16[1,1,1024,128]{3,2,1,0:T(8,128)(2,1)} %param.8), kind=kOutput, calls=%fused_computation.10 | convolution fusion | flops 269615104 | bytes 528384 | tf_op jit(solution)/shard_map/dot_general | solution.py:249
  2.6 4.4 %collective-permute-start = (bf16[384,128]{1,0:T(8,128)(2,1)S(1)}, bf16[384,128]{1,0:T(8,128)(2,1)S(1)}, u32[]{:S(2)}, u32[]{:S(2)}) collective-permute-start(bf16[384,128]{1,0:T(8,128)(2,1)S(1)} %get-tuple-element.50), channel_id=1, source_target_pairs={{0,8},{8,16},{16,24},{24,32},{32,40},{40,48},{48,56},{56,64},{64,7... | collective-permute-start | bytes 294920 | tf_op jit(solution)/shard_map/ppermute | solution.py:223
  6.9 1.3 %collective-permute-start.1 = (bf16[384,128]{1,0:T(8,128)(2,1)S(1)}, bf16[384,128]{1,0:T(8,128)(2,1)S(1)}, u32[]{:S(2)}, u32[]{:S(2)}) collective-permute-start(bf16[384,128]{1,0:T(8,128)(2,1)S(1)} %get-tuple-element.49), channel_id=1, source_target_pairs={{8,0},{16,8},{24,16},{32,24},{40,32},{48,40},{56,48},{64,56},{72,6... | collective-permute-start | bytes 294920 | tf_op jit(solution)/shard_map/ppermute | solution.py:224
  8.3 1.1 copy.25
  10.0 0.1 pad.15.clone
  10.1 0.9 fusion.31
  11.0 0.9 fusion.57
  12.0 0.5 collective-permute-done.1.a2_ref
  12.5 0.0 collective-permute-done.a0_ref
  12.5 5.0 %collective-permute-start.2 = (bf16[384,128]{1,0:T(8,128)(2,1)S(1)}, bf16[384,128]{1,0:T(8,128)(2,1)S(1)}, u32[]{:S(2)}, u32[]{:S(2)}) collective-permute-start(bf16[384,128]{1,0:T(8,128)(2,1)S(1)} %pad_maximum_fusion), channel_id=1, source_target_pairs={{0,1},{1,2},{2,3},{3,4},{4,5},{5,6},{6,7},{8,9},{9,10},{10,11},{11... | collective-permute-start | bytes 294920 | tf_op jit(solution)/shard_map/ppermute | solution.py:227
  17.6 1.9 %collective-permute-start.3 = (bf16[384,128]{1,0:T(8,128)(2,1)S(1)}, bf16[384,128]{1,0:T(8,128)(2,1)S(1)}, u32[]{:S(2)}, u32[]{:S(2)}) collective-permute-start(bf16[384,128]{1,0:T(8,128)(2,1)S(1)} %pad_maximum_fusion.1), channel_id=1, source_target_pairs={{1,0},{2,1},{3,2},{4,3},{5,4},{6,5},{7,6},{9,8},{10,9},{11,10},{12... | collective-permute-start | bytes 294920 | tf_op jit(solution)/shard_map/ppermute | solution.py:228
  19.5 0.0 collective-permute-done.2.b0_ref
  19.5 4.0 %collective-permute-done.3.b2_ref = bf16[384,128]{1,0:T(8,128)(2,1)S(1)} collective-permute-done((bf16[384,128]{1,0:T(8,128)(2,1)S(1)}, bf16[384,128]{1,0:T(8,128)(2,1)S(1)}, u32[]{:S(2)}, u32[]{:S(2)}) %collective-permute-start.3) | collective-permute-done | bytes 98336 | tf_op jit(solution)/shard_map/ppermute | solution.py:228
  23.5 0.0 copy-start.5
  23.5 11.8 %shard_map.103 = (bf16[1024,128]{1,0:T(8,128)(2,1)S(1)}, bf16[1024,3456]{1,0:T(8,128)(2,1)}) custom-call(s32[1024,32]{1,0:T(8,128)S(1)} %get-tuple-element.41.place_ref, bf16[1024,128]{1,0:T(8,128)(2,1)S(1)} %bitcast.51, bf16[384,128]{1,0:T(8,128)(2,1)S(1)} %collective-permute-done.a0_ref, bf16[384,128]{1,0:T(8,128)(2,1)S(1)} %collective-permute-done.1.a2_ref, ...), custom_call_target="tpu_custom_call" | custom-call | flops 7247757312 | bytes 9437184 | tf_op jit(solution)/shard_map/pallas_call | solution.py:74
  35.3 0.2 fusion.10
  35.6 0.2 fusion.13
  35.8 0.1 maximum_maximum_fusion
  35.9 0.7 broadcast_in_dim.10
  36.6 10.0 %all-to-all-start = ((f32[128,3,128]{2,1,0:T(4,128)}), f32[128,3,128]{2,1,0:T(4,128)S(1)}, u32[]{:S(2)}, u32[]{:S(2)}) async-start(f32[128,3,128]{2,1,0:T(4,128)} %broadcast_in_dim.10), calls=%async_computation | async-start | bytes 524288 | tf_op jit(solution)/shard_map/all_to_all | solution.py:235
  46.6 10.8 %all-to-all-done = f32[128,3,128]{2,1,0:T(4,128)S(1)} async-done(((f32[128,3,128]{2,1,0:T(4,128)}), f32[128,3,128]{2,1,0:T(4,128)S(1)}, u32[]{:S(2)}, u32[]{:S(2)}) %all-to-all-start) | async-done | bytes 196640 | tf_op jit(solution)/shard_map/all_to_all | solution.py:235
  57.4 0.1 fusion.58
  57.7 0.2 fusion.30
  57.9 0.7 broadcast_in_dim.12
  58.6 4.8 %all-to-all-start.1 = ((f32[128,2,128]{2,1,0:T(2,128)}), f32[128,2,128]{2,1,0:T(2,128)S(1)}, u32[]{:S(2)}, u32[]{:S(2)}) async-start(f32[128,2,128]{2,1,0:T(2,128)} %broadcast_in_dim.12), calls=%async_computation.1 | async-start | bytes 262144 | tf_op jit(solution)/shard_map/all_to_all | solution.py:235
  63.4 0.9 fusion.2.order_ref
  64.3 9.1 %all-to-all-done.1 = f32[128,2,128]{2,1,0:T(2,128)S(1)} async-done(((f32[128,2,128]{2,1,0:T(2,128)}), f32[128,2,128]{2,1,0:T(2,128)S(1)}, u32[]{:S(2)}, u32[]{:S(2)}) %all-to-all-start.1) | async-done | bytes 131104 | tf_op jit(solution)/shard_map/all_to_all | solution.py:235
  73.4 0.1 fusion.61
  73.5 1.0 fusion.28
  74.6 7.2 %shard_map.104 = bf16[128,4,8,128]{3,2,1,0:T(8,128)(2,1)} custom-call(bf16[1024,3456]{1,0:T(8,128)(2,1)} %get-tuple-element.16.cols_ref, bf16[1024,128]{1,0:T(8,128)(2,1)S(1)} %get-tuple-element.17.grad_ref, bf16[1024,1024]{1,0:T(8,128)(2,1)S(1)} %fusion.2.order_ref), custom_call_target="tpu_custom_call" | custom-call | flops 905969664 | bytes 10485760 | tf_op jit(solution)/shard_map/pallas_call | solution.py:201
  81.8 4.3 %all-to-all-start.2 = ((bf16[128,4,8,128]{3,2,1,0:T(8,128)(2,1)}), bf16[128,4,8,128]{3,2,1,0:T(8,128)(2,1)S(1)}, u32[]{:S(2)}, u32[]{:S(2)}) async-start(bf16[128,4,8,128]{3,2,1,0:T(8,128)(2,1)} %shard_map.104), calls=%async_computation.2 | async-start | bytes 2097152 | tf_op jit(solution)/shard_map/all_to_all | solution.py:306
  86.1 1.2 copy.28
  87.3 1.2 copy-done.1
  88.4 12.6 %shard_map.105 = (f32[1024,128]{1,0:T(8,128)S(1)}, bf16[384,128]{1,0:T(8,128)(2,1)S(1)}, bf16[128,128]{1,0:T(8,128)(2,1)S(1)}, bf16[128,128]{1,0:T(8,128)(2,1)S(1)}, bf16[384,128]{1,0:T(8,128)(2,1)S(1)}) custom-call(s32[2,32,512]{2,1,0:T(8,128)S(1)} %bitcast.50, s32[1024,32]{1,0:T(8,128)S(1)} %get-tuple-element.41.place_ref, ...), custom_call_target="tpu_custom_call" | custom-call | flops 8153726976 | bytes 2097152 | tf_op jit(solution)/shard_map/pallas_call | solution.py:134
  101.0 3.4 %collective-permute-start.4 = (bf16[384,128]{1,0:T(8,128)(2,1)S(1)}, bf16[384,128]{1,0:T(8,128)(2,1)S(1)}, u32[]{:S(2)}, u32[]{:S(2)}) collective-permute-start(bf16[384,128]{1,0:T(8,128)(2,1)S(1)} %get-tuple-element.19), channel_id=1, source_target_pairs={{0,8},{8,16},{16,24},{24,32},{32,40},{40,48},{48,56},{56,64},{64,7... | collective-permute-start | bytes 294920 | tf_op jit(solution)/shard_map/ppermute | solution.py:223
  104.4 1.3 %collective-permute-start.5 = (bf16[384,128]{1,0:T(8,128)(2,1)S(1)}, bf16[384,128]{1,0:T(8,128)(2,1)S(1)}, u32[]{:S(2)}, u32[]{:S(2)}) collective-permute-start(bf16[384,128]{1,0:T(8,128)(2,1)S(1)} %get-tuple-element.20), channel_id=1, source_target_pairs={{8,0},{16,8},{24,16},{32,24},{40,32},{48,40},{56,48},{64,56},{72,6... | collective-permute-start | bytes 294920 | tf_op jit(solution)/shard_map/ppermute | solution.py:224
  105.8 0.4 collective-permute-done.4
  106.2 3.6 %collective-permute-done.5 = bf16[384,128]{1,0:T(8,128)(2,1)S(1)} collective-permute-done((bf16[384,128]{1,0:T(8,128)(2,1)S(1)}, bf16[384,128]{1,0:T(8,128)(2,1)S(1)}, u32[]{:S(2)}, u32[]{:S(2)}) %collective-permute-start.5) | collective-permute-done | bytes 98336 | tf_op jit(solution)/shard_map/ppermute | solution.py:224
  109.8 0.0 all-to-all-done.2
  109.8 4.8 %collective-permute-start.6 = (bf16[384,128]{1,0:T(8,128)(2,1)S(1)}, bf16[384,128]{1,0:T(8,128)(2,1)S(1)}, u32[]{:S(2)}, u32[]{:S(2)}) collective-permute-start(bf16[384,128]{1,0:T(8,128)(2,1)S(1)} %pad_maximum_fusion.2), channel_id=1, source_target_pairs={{0,1},{1,2},{2,3},{3,4},{4,5},{5,6},{6,7},{8,9},{9,10},{10,11},{11... | collective-permute-start | bytes 294920 | tf_op jit(solution)/shard_map/ppermute | solution.py:227
  114.7 0.2 convert_reduce_fusion
  114.9 0.1 reshape.207
  115.0 1.3 %collective-permute-done.6 = bf16[384,128]{1,0:T(8,128)(2,1)S(1)} collective-permute-done((bf16[384,128]{1,0:T(8,128)(2,1)S(1)}, bf16[384,128]{1,0:T(8,128)(2,1)S(1)}, u32[]{:S(2)}, u32[]{:S(2)}) %collective-permute-start.6) | collective-permute-done | bytes 98336 | tf_op jit(solution)/shard_map/ppermute | solution.py:227
  116.3 1.9 %collective-permute-start.7 = (bf16[384,128]{1,0:T(8,128)(2,1)S(1)}, bf16[384,128]{1,0:T(8,128)(2,1)S(1)}, u32[]{:S(2)}, u32[]{:S(2)}) collective-permute-start(bf16[384,128]{1,0:T(8,128)(2,1)S(1)} %pad_maximum_fusion.3), channel_id=1, source_target_pairs={{1,0},{2,1},{3,2},{4,3},{5,4},{6,5},{7,6},{9,8},{10,9},{11,10},{12... | collective-permute-start | bytes 294920 | tf_op jit(solution)/shard_map/ppermute | solution.py:228
  118.3 0.8 copy.32
  119.0 3.9 %collective-permute-done.7 = bf16[384,128]{1,0:T(8,128)(2,1)S(1)} collective-permute-done((bf16[384,128]{1,0:T(8,128)(2,1)S(1)}, bf16[384,128]{1,0:T(8,128)(2,1)S(1)}, u32[]{:S(2)}, u32[]{:S(2)}) %collective-permute-start.7) | collective-permute-done | bytes 98336 | tf_op jit(solution)/shard_map/ppermute | solution.py:228
  123.0 2.2 %fusion.8 = bf16[1,1,1024,128]{3,2,1,0:T(8,128)(2,1)} fusion(f32[1024,128]{1,0:T(8,128)S(1)} %get-tuple-element.18, bf16[1024,128]{1,0:T(8,128)(2,1)S(1)} %slice_dynamic-update-slice_fusion, s32[1024]{0:T(1024)S(1)} %bitcast.68), kind=kOutput, calls=%fused_computation.11 | convolution fusion | flops 269746176 | bytes 1052672 | tf_op jit(solution)/shard_map/dot_general | solution.py:315
  (45 shorter events, 0.5 us)
Async XLA Ops:
  0.6 22.9 %copy-start.2 = (bf16[1,1,1024,128]{3,2,1,0:T(8,128)(2,1)S(1)}, bf16[1,1,1024,128]{3,2,1,0:T(8,128)(2,1)}, u32[]{:S(2)}) copy-start(bf16[1,1,1024,128]{3,2,1,0:T(8,128)(2,1)} %param.8) | copy-start | bytes 786436
  0.6 22.9 %copy-start = (bf16[3456,128]{1,0:T(8,128)(2,1)S(1)}, bf16[3456,128]{1,0:T(8,128)(2,1)}, u32[]{:S(2)}) copy-start(bf16[3456,128]{1,0:T(8,128)(2,1)} %weight_ref.3) | copy-start | bytes 2654212
  2.6 9.9 %collective-permute-start = (bf16[384,128]{1,0:T(8,128)(2,1)S(1)}, bf16[384,128]{1,0:T(8,128)(2,1)S(1)}, u32[]{:S(2)}, u32[]{:S(2)}) collective-permute-start(bf16[384,128]{1,0:T(8,128)(2,1)S(1)} %get-tuple-element.50), channel_id=1, source_target_pairs={{0,8},{8,16},{16,24},{24,32},{32,40},{40,48},{48,56},{56,64},{64,7... | collective-permute-start | bytes 294920 | tf_op jit(solution)/shard_map/ppermute | solution.py:223
  6.9 5.5 %collective-permute-start.1 = (bf16[384,128]{1,0:T(8,128)(2,1)S(1)}, bf16[384,128]{1,0:T(8,128)(2,1)S(1)}, u32[]{:S(2)}, u32[]{:S(2)}) collective-permute-start(bf16[384,128]{1,0:T(8,128)(2,1)S(1)} %get-tuple-element.49), channel_id=1, source_target_pairs={{8,0},{16,8},{24,16},{32,24},{40,32},{48,40},{56,48},{64,56},{72,6... | collective-permute-start | bytes 294920 | tf_op jit(solution)/shard_map/ppermute | solution.py:224
  12.5 7.0 %collective-permute-start.2 = (bf16[384,128]{1,0:T(8,128)(2,1)S(1)}, bf16[384,128]{1,0:T(8,128)(2,1)S(1)}, u32[]{:S(2)}, u32[]{:S(2)}) collective-permute-start(bf16[384,128]{1,0:T(8,128)(2,1)S(1)} %pad_maximum_fusion), channel_id=1, source_target_pairs={{0,1},{1,2},{2,3},{3,4},{4,5},{5,6},{6,7},{8,9},{9,10},{10,11},{11... | collective-permute-start | bytes 294920 | tf_op jit(solution)/shard_map/ppermute | solution.py:227
  17.6 5.9 %collective-permute-start.3 = (bf16[384,128]{1,0:T(8,128)(2,1)S(1)}, bf16[384,128]{1,0:T(8,128)(2,1)S(1)}, u32[]{:S(2)}, u32[]{:S(2)}) collective-permute-start(bf16[384,128]{1,0:T(8,128)(2,1)S(1)} %pad_maximum_fusion.1), channel_id=1, source_target_pairs={{1,0},{2,1},{3,2},{4,3},{5,4},{6,5},{7,6},{9,8},{10,9},{11,10},{12... | collective-permute-start | bytes 294920 | tf_op jit(solution)/shard_map/ppermute | solution.py:228
  23.5 34.2 %copy-start.4 = (f32[128]{0:T(128)S(1)}, f32[128]{0:T(128)}, u32[]{:S(2)}) copy-start(f32[128]{0:T(128)} %param.13) | copy-start | bytes 1540
  23.5 34.2 %copy-start.3 = (bf16[1,1,1024,128]{3,2,1,0:T(8,128)(2,1)S(1)}, bf16[1,1,1024,128]{3,2,1,0:T(8,128)(2,1)}, u32[]{:S(2)}) copy-start(bf16[1,1,1024,128]{3,2,1,0:T(8,128)(2,1)} %param.15) | copy-start | bytes 786436
  23.5 34.2 %copy-start.5 = (f32[128]{0:T(128)S(1)}, f32[128]{0:T(128)}, u32[]{:S(2)}) copy-start(f32[128]{0:T(128)} %param.14) | copy-start | bytes 1540
  36.6 20.8 %all-to-all-start = ((f32[128,3,128]{2,1,0:T(4,128)}), f32[128,3,128]{2,1,0:T(4,128)S(1)}, u32[]{:S(2)}, u32[]{:S(2)}) async-start(f32[128,3,128]{2,1,0:T(4,128)} %broadcast_in_dim.10), calls=%async_computation | async-start | bytes 524288 | tf_op jit(solution)/shard_map/all_to_all | solution.py:235
  58.6 14.7 %all-to-all-start.1 = ((f32[128,2,128]{2,1,0:T(2,128)}), f32[128,2,128]{2,1,0:T(2,128)S(1)}, u32[]{:S(2)}, u32[]{:S(2)}) async-start(f32[128,2,128]{2,1,0:T(2,128)} %broadcast_in_dim.12), calls=%async_computation.1 | async-start | bytes 262144 | tf_op jit(solution)/shard_map/all_to_all | solution.py:235
  81.8 28.1 %all-to-all-start.2 = ((bf16[128,4,8,128]{3,2,1,0:T(8,128)(2,1)}), bf16[128,4,8,128]{3,2,1,0:T(8,128)(2,1)S(1)}, u32[]{:S(2)}, u32[]{:S(2)}) async-start(bf16[128,4,8,128]{3,2,1,0:T(8,128)(2,1)} %shard_map.104), calls=%async_computation.2 | async-start | bytes 2097152 | tf_op jit(solution)/shard_map/all_to_all | solution.py:306
  87.3 1.2 copy-start.1
  88.4 34.6 %copy-start.6 = (s32[1,1,8,128]{3,2,1,0:T(8,128)S(1)}, s32[1,1,8,128]{3,2,1,0:T(8,128)}, u32[]{:S(2)}) copy-start(s32[1,1,8,128]{3,2,1,0:T(8,128)} %param.11) | copy-start | bytes 12292
  101.0 5.2 %collective-permute-start.4 = (bf16[384,128]{1,0:T(8,128)(2,1)S(1)}, bf16[384,128]{1,0:T(8,128)(2,1)S(1)}, u32[]{:S(2)}, u32[]{:S(2)}) collective-permute-start(bf16[384,128]{1,0:T(8,128)(2,1)S(1)} %get-tuple-element.19), channel_id=1, source_target_pairs={{0,8},{8,16},{16,24},{24,32},{32,40},{40,48},{48,56},{56,64},{64,7... | collective-permute-start | bytes 294920 | tf_op jit(solution)/shard_map/ppermute | solution.py:223
  104.4 5.4 %collective-permute-start.5 = (bf16[384,128]{1,0:T(8,128)(2,1)S(1)}, bf16[384,128]{1,0:T(8,128)(2,1)S(1)}, u32[]{:S(2)}, u32[]{:S(2)}) collective-permute-start(bf16[384,128]{1,0:T(8,128)(2,1)S(1)} %get-tuple-element.20), channel_id=1, source_target_pairs={{8,0},{16,8},{24,16},{32,24},{40,32},{48,40},{56,48},{64,56},{72,6... | collective-permute-start | bytes 294920 | tf_op jit(solution)/shard_map/ppermute | solution.py:224
  109.8 6.5 %collective-permute-start.6 = (bf16[384,128]{1,0:T(8,128)(2,1)S(1)}, bf16[384,128]{1,0:T(8,128)(2,1)S(1)}, u32[]{:S(2)}, u32[]{:S(2)}) collective-permute-start(bf16[384,128]{1,0:T(8,128)(2,1)S(1)} %pad_maximum_fusion.2), channel_id=1, source_target_pairs={{0,1},{1,2},{2,3},{3,4},{4,5},{5,6},{6,7},{8,9},{9,10},{10,11},{11... | collective-permute-start | bytes 294920 | tf_op jit(solution)/shard_map/ppermute | solution.py:227
  116.3 6.6 %collective-permute-start.7 = (bf16[384,128]{1,0:T(8,128)(2,1)S(1)}, bf16[384,128]{1,0:T(8,128)(2,1)S(1)}, u32[]{:S(2)}, u32[]{:S(2)}) collective-permute-start(bf16[384,128]{1,0:T(8,128)(2,1)S(1)} %pad_maximum_fusion.3), channel_id=1, source_target_pairs={{1,0},{2,1},{3,2},{4,3},{5,4},{6,5},{7,6},{9,8},{10,9},{11,10},{12... | collective-permute-start | bytes 294920 | tf_op jit(solution)/shard_map/ppermute | solution.py:228

commit v2 on v1

--- a/solution.py
+++ b/solution.py
@@ -91,16 +91,27 @@
     )(place, own, a0, a2, b0, b2, weight)
 
 
-def backward_kernel(group, row_ref, place_ref, grad_ref, weight_ref, own_ref, lo_ref, m0_ref, m2_ref, hi_ref, acc_ref, hot_ref, rhs_ref):
+def backward_kernel(group, row_ref, place_ref, grad_ref, table_ref, own_ref, lo_ref, m0_ref, m2_ref, hi_ref, acc_ref, hot_ref, rhs_ref, weight_ref, sems):
     rows, channels = grad_ref.shape
     block = acc_ref.shape[0]
     part = block // 8
     high = m0_ref.shape[0]
+    steps = TAPS // group
+    wide = group * channels
+
+    def fetch(step):
+        here = pl.ds(step * wide, wide)
+        return pltpu.make_async_copy(table_ref.at[here, :], weight_ref.at[here, :], sems.at[step])
+
+    for step in range(steps):
+        fetch(step).start()
     for q in range(rows // block):
         grad = grad_ref[pl.ds(q * block, block), :]
         place = place_ref[pl.ds(q * block, block), :]
         down = lax.broadcasted_iota(I32, (block, block), 0)
-        for g in range(TAPS // group):
+        for g in range(steps):
+            if q == 0:
+                fetch(g).wait()
             for n in range(group):
                 k = g * group + n
                 line = row_ref[q, k : k + 1, :]
@@ -131,8 +142,10 @@
 
 def backward(row, place, grad, weight, high, block=512, group=3):
     rows, channels = grad.shape
+    vmem = pl.BlockSpec(memory_space=pltpu.VMEM)
     return pl.pallas_call(
         functools.partial(backward_kernel, group),
+        in_specs=[vmem, vmem, vmem, pl.BlockSpec(memory_space=pltpu.HBM)],
         out_shape=(
             jax.ShapeDtypeStruct((rows, channels), F32),
             jax.ShapeDtypeStruct((3 * high, channels), BF16),
@@ -144,23 +157,84 @@
             pltpu.VMEM((block, 2 * channels), F32),
             pltpu.VMEM((block, group * block), BF16),
             pltpu.VMEM((group * block, 2 * channels), BF16),
+            pltpu.VMEM(weight.shape, BF16),
+            pltpu.SemaphoreType.DMA((TAPS // group,)),
         ],
         compiler_params=pltpu.CompilerParams(vmem_limit_bytes=16 << 20),
         cost_estimate=pl.CostEstimate(flops=TAPS*4*rows*channels*(block+64), bytes_accessed=2<<20, transcendentals=0),
-    )(row, place, grad, weight)
-
-
-def weight_kernel(across, down, group, cols_ref, grad_ref, order_ref, out_ref, line_ref, buffer_ref, sems):
-    channels = grad_ref.shape[1]
-    eighths = out_ref.shape[1]
+    )(row, place, grad, pltpu.with_memory_space_constraint(weight, pltpu.HBM))
+
+
+def product_kernel(group, extra, cols_ref, rhs_ref, out_ref, left_ref, whole_ref, buffer_ref, in_sems, out_sems):
+    channels = rhs_ref.shape[1]
+    wide = group * channels
     slots = buffer_ref.shape[0]
     steps = TAPS // group
 
     def fetch(step):
         return pltpu.make_async_copy(
-            cols_ref.at[:, pl.ds(step * group * channels, group * channels)],
+            cols_ref.at[:, pl.ds(step * wide, wide)],
             buffer_ref.at[step % slots],
-            sems.at[step % slots],
+            in_sems.at[step % slots],
+        )
+
+    def leave(step):
+        here = pl.ds(step * wide, wide)
+        return pltpu.make_async_copy(
+            whole_ref.at[:, here], out_ref.at[:, here], out_sems.at[step]
+        )
+
+    for step in range(slots - 1):
+        fetch(step).start()
+    left_ref[:channels, :] = rhs_ref[...].T
+    if extra:
+        left_ref[channels:, :] = jnp.ones((extra, left_ref.shape[1]), BF16)
+    for step in range(steps):
+        if step + slots - 1 < steps:
+            fetch(step + slots - 1).start()
+        fetch(step).wait()
+        whole_ref[:, step * wide : (step + 1) * wide] = jnp.dot(
+            left_ref[...], buffer_ref[step % slots], preferred_element_type=F32
+        )
+        leave(step).start()
+    for step in range(steps):
+        leave(step).wait()
+
+
+def product(cols, rhs, extra=0, group=3, slots=3):
+    rows, wide = cols.shape
+    channels = rhs.shape[1]
+    hbm = pl.BlockSpec(memory_space=pltpu.HBM)
+    return pl.pallas_call(
+        functools.partial(product_kernel, group, extra),
+        in_specs=[hbm, pl.BlockSpec(memory_space=pltpu.VMEM)],
+        out_specs=hbm,
+        out_shape=pltpu.HBM((channels + extra, wide), F32),
+        scratch_shapes=[
+            pltpu.VMEM((channels + extra, rows), BF16),
+            pltpu.VMEM((channels + extra, wide), F32),
+            pltpu.VMEM((slots, rows, group * channels), BF16),
+            pltpu.SemaphoreType.DMA((slots,)),
+            pltpu.SemaphoreType.DMA((TAPS // group,)),
+        ],
+        compiler_params=pltpu.CompilerParams(vmem_limit_bytes=16 << 20),
+        cost_estimate=pl.CostEstimate(
+            flops=2 * rows * wide * channels, bytes_accessed=9 << 20, transcendentals=0
+        ),
+    )(pltpu.with_memory_space_constraint(cols, pltpu.HBM), rhs)
+
+
+def weight_kernel(across, down, group, up_ref, conv_ref, scale_ref, order_ref, out_ref, line_ref, first_ref, second_ref, sems):
+    channels = scale_ref.shape[1]
+    eighths = out_ref.shape[1]
+    wide = group * channels
+    steps = TAPS // group
+
+    def fetch(step):
+        here = pl.ds(step * wide, wide)
+        return (
+            pltpu.make_async_copy(up_ref.at[:, here], first_ref.at[:, here], sems.at[0, step]),
+            pltpu.make_async_copy(conv_ref.at[:, here], second_ref.at[:, here], sems.at[1, step]),
         )
 
     def line(k):
@@ -169,20 +243,24 @@
             slice(k % 8 * channels, (k % 8 + 1) * channels),
         )
 
-    for step in range(slots - 1):
-        fetch(step).start()
+    for step in range(steps):
+        for copy in fetch(step):
+            copy.start()
     for k in range(TAPS, 8 * eighths):
         line_ref[line(k)] = jnp.zeros((channels, channels), BF16)
-    turned = grad_ref[...].T
+    turned = scale_ref[...].T
+    scales = [jnp.broadcast_to(turned[:, n : n + 1], (channels, channels)) for n in range(3)]
     for step in range(steps):
-        if step + slots - 1 < steps:
-            fetch(step + slots - 1).start()
-        fetch(step).wait()
-        whole = jnp.dot(turned, buffer_ref[step % slots], preferred_element_type=F32)
-        for n in range(group):
-            line_ref[line(step * group + n)] = (
-                whole[:, n * channels : (n + 1) * channels].T.astype(BF16)
+        for copy in fetch(step):
+            copy.wait()
+        for k in range(step * group, (step + 1) * group):
+            here = slice(k * channels, (k + 1) * channels)
+            term = (
+                scales[0] * first_ref[:, here]
+                - scales[1] * second_ref[channels : channels + 1, here]
+                - scales[2] * second_ref[:channels, here]
             )
+            line_ref[line(k)] = term.T.astype(BF16)
     placed = jnp.dot(line_ref[...], order_ref[...], preferred_element_type=F32).astype(BF16)
     for e in range(eighths):
         for x in range(across):
@@ -193,37 +271,72 @@
                 ]
 
 
-def weight_terms(cols, grad, order, across, down, group=3, slots=3):
-    rows, wide = cols.shape
-    channels = wide // TAPS
+def weight_terms(up_part, conv_part, scales, order, across, down, group=3):
+    channels, wide = up_part.shape
     eighths = -(-TAPS // 8)
-    vmem = pl.BlockSpec(memory_space=pltpu.VMEM)
+    vmem, hbm = pl.BlockSpec(memory_space=pltpu.VMEM), pl.BlockSpec(memory_space=pltpu.HBM)
     return pl.pallas_call(
         functools.partial(weight_kernel, across, down, group),
-        in_specs=[pl.BlockSpec(memory_space=pltpu.HBM), vmem, vmem],
+        in_specs=[hbm, hbm, vmem, vmem],
         out_specs=vmem,
         out_shape=jax.ShapeDtypeStruct((across * down, eighths, down, channels), BF16),
         scratch_shapes=[
             pltpu.VMEM((eighths * channels, 8 * channels), BF16),
-            pltpu.VMEM((slots, rows, group * channels), BF16),
-            pltpu.SemaphoreType.DMA((slots,)),
+            pltpu.VMEM(up_part.shape, F32),
+            pltpu.VMEM(conv_part.shape, F32),
+            pltpu.SemaphoreType.DMA((2, TAPS // group)),
         ],
-        compiler_params=pltpu.CompilerParams(vmem_limit_bytes=24 << 20),
+        compiler_params=pltpu.CompilerParams(vmem_limit_bytes=16 << 20),
+        cost_estimate=pl.CostEstimate(flops=1 << 30, bytes_accessed=5 << 20, transcendentals=0),
+    )(
+        pltpu.with_memory_space_constraint(up_part, pltpu.HBM),
+        pltpu.with_memory_space_constraint(conv_part, pltpu.HBM),
+        scales,
+        order,
+    )
+
+
+def add_back_kernel(index_ref, a0_ref, a2_ref, b0_ref, b2_ref, own_ref, out_ref, hot_ref, slot_ref):
+    rows, channels = own_ref.shape
+    slots, size = index_ref.shape
+    down = lax.broadcasted_iota(I32, (rows, size), 0)
+    pieces = (
+        (b0_ref, 0), (a0_ref, 1), (b2_ref, 0), (b0_ref, 1),
+        (b2_ref, 1), (b0_ref, 2), (a2_ref, 1), (b2_ref, 2),
+    )
+    for slot, (ref, at) in enumerate(pieces):
+        slot_ref[slot * size : (slot + 1) * size, :] = ref[at * size : (at + 1) * size, :]
+        hot_ref[:, slot * size : (slot + 1) * size] = jnp.where(
+            jnp.broadcast_to(index_ref[slot : slot + 1, :], (rows, size)) == down, 1.0, 0.0
+        ).astype(BF16)
+    added = jnp.dot(hot_ref[...], slot_ref[...], preferred_element_type=F32)
+    out_ref[...] = (own_ref[...] + added).astype(BF16)
+
+
+def add_back(index, a0, a2, b0, b2, own):
+    rows, channels = own.shape
+    return pl.pallas_call(
+        add_back_kernel,
+        out_shape=jax.ShapeDtypeStruct((rows, channels), BF16),
+        scratch_shapes=[
+            pltpu.VMEM((rows, index.size), BF16),
+            pltpu.VMEM((index.size, channels), BF16),
+        ],
+        compiler_params=pltpu.CompilerParams(vmem_limit_bytes=16 << 20),
         cost_estimate=pl.CostEstimate(
-            flops=2 * rows * wide * channels, bytes_accessed=10 << 20, transcendentals=0
-        ),
-    )(pltpu.with_memory_space_constraint(cols, pltpu.HBM), grad, order)
-
-
-def from_neighbours(low, mid_low, mid_high, high, arrived=None):
+            flops=2 * rows * rows * channels, bytes_accessed=2 << 20, transcendentals=0
+        ),
+    )(index, a0, a2, b0, b2, own)
+
+
+def from_neighbours(low, mid_low, mid_high, high, arrived):
     size = mid_low.shape[0]
     ends_x, ends_y = lax.axis_size("bx") - 1, lax.axis_size("by") - 1
     up_x, down_x = [(i, i + 1) for i in range(ends_x)], [(i + 1, i) for i in range(ends_x)]
     up_y, down_y = [(i, i + 1) for i in range(ends_y)], [(i + 1, i) for i in range(ends_y)]
     a0 = lax.ppermute(high, "bx", up_x)
     a2 = lax.ppermute(low, "bx", down_x)
-    if arrived is not None:
-        a0, a2, arrived = lax.optimization_barrier((a0, a2, arrived))
+    a0, a2, arrived = lax.optimization_barrier((a0, a2, arrived))
     b0 = lax.ppermute(jnp.concatenate([a0[2 * size :], mid_high, a2[2 * size :]]), "by", up_y)
     b2 = lax.ppermute(jnp.concatenate([a0[:size], mid_low, a2[:size]]), "by", down_y)
     return a0, a2, b0, b2, arrived
@@ -247,11 +360,14 @@
         sent_index[:, None] == lax.broadcasted_iota(I32, (1, rows_total), 1)
     ).astype(BF16)
     chosen = jnp.dot(send_select, own_rows, preferred_element_type=F32).astype(BF16)
-    a0, a2, b0, b2, _ = from_neighbours(
-        chosen[: 3 * size], chosen[3 * size : 4 * size], chosen[4 * size : 5 * size], chosen[5 * size :]
-    )
-
-    indices = neighbour_map[0, 0]
+    a0, a2, b0, b2, indices = from_neighbours(
+        chosen[: 3 * size],
+        chosen[3 * size : 4 * size],
+        chosen[4 * size : 5 * size],
+        chosen[5 * size :],
+        neighbour_map[0, 0],
+    )
+
     block = lax.broadcasted_iota(I32, (1, rows_total), 1) // block_rows
     beyond = indices - rows_total
     target = beyond // size
@@ -275,6 +391,8 @@
     stats = everyones(
         jnp.stack([local_mean, local_square, jnp.full((channels,), local_count)])
     )
+    conv_part = product(cols, conv_out, extra=16)
+    stats, place_rows, conv_part = lax.optimization_barrier((stats, place_rows, conv_part))
     counts = stats[:, 2]
     total_count = jnp.sum(counts, axis=0)
     center = jnp.sum(stats[:, 0] * counts, axis=0) / total_count
@@ -288,6 +406,8 @@
     sums = everyones(
         jnp.stack([jnp.sum(upstream, axis=0), jnp.sum(upstream * normalized, axis=0)])
     )
+    up_part = product(cols, upstream.astype(BF16))
+    sums, up_part = lax.optimization_barrier((sums, up_part))
     mean_up = jnp.sum(sums[:, 0], axis=0) / total_count
     mean_cross = jnp.sum(sums[:, 1], axis=0) / total_count
     scale = gain * inverse_std
@@ -301,24 +421,20 @@
     order = (
         source == (spot // width) % 8 * channels + spot // channels * width + spot % width
     ).astype(BF16)
-    pieces = weight_terms(cols, conv_grad, order, across, down)
+    scales = jnp.stack(
+        [
+            scale,
+            scale * (mean_up - mean_cross * inverse_std * center),
+            scale * mean_cross * inverse_std,
+        ]
+        + [jnp.zeros_like(scale)] * 5
+    )
+    pieces = weight_terms(up_part, conv_part, scales, order, across, down)
     pieces, conv_grad = lax.optimization_barrier((pieces, conv_grad))
     arrived = lax.all_to_all(pieces, axes, 0, 0, tiled=True)
     own_table, *halo = backward(place_rows, place_down, conv_grad, weight, size)
     a0, a2, b0, b2, arrived = from_neighbours(*halo, arrived)
-    slots_back = jnp.concatenate(
-        [
-            b0[:size], a0[size : 2 * size], b2[:size], b0[size : 2 * size],
-            b2[size : 2 * size], b0[2 * size :], a2[size : 2 * size], b2[2 * size :],
-        ]
-    )
-    added_back = lax.dot_general(
-        send_select,
-        slots_back,
-        (((0,), (0,)), ((), ())),
-        preferred_element_type=F32,
-    )
-    own_grad = (own_table + added_back).astype(BF16)
+    own_grad = add_back(send_rows[0, 0], a0, a2, b0, b2, own_table)
     summed = jnp.sum(arrived.astype(F32), axis=0).reshape(-1, down, 8, width)
     grad_weight = summed.transpose(0, 2, 1, 3).reshape(-1, down, width)[:TAPS] / jnp.sqrt(
         total_count[0]

time: 126 us -> 129 us (1.024)
  waiting for transfers between devices: 33.5 us -> 15.6 us
  Pallas kernels: 31.5 us -> 47.2 us
  starting transfers between devices: 43.1 us -> 47.8 us
  other arithmetic: 4.03 us -> 7.18 us
  matrix products: 4.04 us -> 1.88 us
    pallas_call x1 -> x4, Pallas kernels: 12.6 us -> 30.7 us  [the longest x1 17.4 us: backward(): pl.pallas_call(functools.partial(backward_kernel, group), in_specs=[vmem,...]
    all_to_all x2, waiting for transfers between devices: 19.8 us -> 7.8 us  [everyones(): return lax.all_to_all(copies, axes, 0, 0, tiled=True)]
    ppermute x2, waiting for transfers between devices: 7.88 us -> 0.01 us  [from_neighbours(): lax.ppermute(jnp.concatenate([a0[:size], mid_low, a2[:size]]), 'by', down_y)]
    ppermute x2, starting transfers between devices: 3.84 us -> 7.53 us  [from_neighbours(): lax.ppermute(jnp.concatenate([a0[:size], mid_low, a2[:size]]), 'by', down_y)]
    ppermute x2, starting transfers between devices: 9.84 us -> 6.16 us  [from_neighbours(): lax.ppermute(jnp.concatenate([a0[2 * size:], mid_high, a2[2 * size:]]), '...]
    pallas_call x1, Pallas kernels: 7.18 us -> 4.54 us  [weight_terms(): pl.pallas_call(functools.partial(weight_kernel, across, down, group), in_...]
    all_to_all x1, starting transfers between devices: 4.3 us -> 6.74 us  [per_device(): arrived = lax.all_to_all(pieces, axes, 0, 0, tiled=True)]
    another operation x0 -> x2, other arithmetic: none -> 2.43 us  [per_device(): jnp.stack([scale, scale * (mean_up - mean_cross * inverse_std * center),...]
  transfers between devices with their start and end apart: 11 -> 11, of which waited for: 8 -> 7; matrix products, arithmetic and copies ran while one was open for 5% -> 3% of each run, Pallas kernels for 10% -> 23%
where the time goes in v2:
time: 129 us; the launch traced here: 127 us
  starting transfers between devices  47.8 us (37%)
  Pallas kernels  47.2 us (37%)
  waiting for transfers between devices  15.6 us (12%)
  other arithmetic  7.18 us (6%)
  local copies, waits for them, and re-layouts  6.07 us (5%)
  matrix products  1.88 us (1%)
  between operations  1.76 us (1%)
    pallas_call x1, Pallas kernels, backward(): pl.pallas_call(functools.partial(backward_kernel, group), in_specs=[vmem,...  17.4 us
    all_to_all x2, starting transfers between devices, everyones(): return lax.all_to_all(copies, axes, 0, 0, tiled=True)  17 us
    pallas_call x1, Pallas kernels, forward(): pl.pallas_call(functools.partial(forward_kernel, chunks), in_specs=[vmem]...  12 us
    pallas_call x2, Pallas kernels, product(): pl.pallas_call(functools.partial(product_kernel, group, extra), in_specs=...  11.7 us
    all_to_all x2, waiting for transfers between devices, everyones(): return lax.all_to_all(copies, axes, 0, 0, tiled=True)  7.8 us
    ppermute x2, starting transfers between devices, from_neighbours(): a0 = lax.ppermute(high, 'bx', up_x)  7.8 us
    ppermute x2, starting transfers between devices, from_neighbours(): lax.ppermute(jnp.concatenate([a0[:size], mid_low, a2[:size]]), 'by', down_y)  7.53 us
    all_to_all x1, starting transfers between devices, per_device(): arrived = lax.all_to_all(pieces, axes, 0, 0, tiled=True)  6.74 us
  transfers between devices with their start and end apart: 11, of which 7 were waited for; matrix products, arithmetic and copies ran while one was open for 3% of the time, Pallas kernels for 23%

profile of v2, /device:TPU:1, one launch (start us, length us, event | category | flops | bytes accessed | tf_op | source)
XLA Modules:
  0.0 127.5 jit_solution(17807638253079889716)
XLA Ops:
  0.7 1.9 %fusion.3 = bf16[1024,128]{1,0:T(8,128)(2,1)S(1)} fusion(s32[1024]{0:T(1024)} %bitcast.52, bf16[1,1,1024,128]{3,2,1,0:T(8,128)(2,1)} %param.8), kind=kOutput, calls=%fused_computation.6 | convolution fusion | flops 269615104 | bytes 528384 | tf_op jit(solution)/shard_map/dot_general | solution.py:362
  2.6 4.4 %collective-permute-start = (bf16[384,128]{1,0:T(8,128)(2,1)S(1)}, bf16[384,128]{1,0:T(8,128)(2,1)S(1)}, u32[]{:S(2)}, u32[]{:S(2)}) collective-permute-start(bf16[384,128]{1,0:T(8,128)(2,1)S(1)} %get-tuple-element.67), channel_id=1, source_target_pairs={{0,8},{8,16},{16,24},{24,32},{32,40},{40,48},{48,56},{56,64},{64,7... | collective-permute-start | bytes 294920 | tf_op jit(solution)/shard_map/ppermute | solution.py:337
  6.9 1.3 %collective-permute-start.1 = (bf16[384,128]{1,0:T(8,128)(2,1)S(1)}, bf16[384,128]{1,0:T(8,128)(2,1)S(1)}, u32[]{:S(2)}, u32[]{:S(2)}) collective-permute-start(bf16[384,128]{1,0:T(8,128)(2,1)S(1)} %get-tuple-element.66), channel_id=1, source_target_pairs={{8,0},{16,8},{24,16},{32,24},{40,32},{48,40},{56,48},{64,56},{72,6... | collective-permute-start | bytes 294920 | tf_op jit(solution)/shard_map/ppermute | solution.py:338
  8.3 1.1 copy.25
  10.0 0.1 pad.15.clone
  10.1 2.4 %collective-permute-done.1.a2_ref = bf16[384,128]{1,0:T(8,128)(2,1)S(1)} collective-permute-done((bf16[384,128]{1,0:T(8,128)(2,1)S(1)}, bf16[384,128]{1,0:T(8,128)(2,1)S(1)}, u32[]{:S(2)}, u32[]{:S(2)}) %collective-permute-start.1) | collective-permute-done | bytes 98336 | tf_op jit(solution)/shard_map/ppermute | solution.py:338
  12.5 3.8 %collective-permute-start.3 = (bf16[384,128]{1,0:T(8,128)(2,1)S(1)}, bf16[384,128]{1,0:T(8,128)(2,1)S(1)}, u32[]{:S(2)}, u32[]{:S(2)}) collective-permute-start(bf16[384,128]{1,0:T(8,128)(2,1)S(1)} %pad_maximum_fusion.1), channel_id=1, source_target_pairs={{1,0},{2,1},{3,2},{4,3},{5,4},{6,5},{7,6},{9,8},{10,9},{11,10},{12... | collective-permute-start | bytes 294920 | tf_op jit(solution)/shard_map/ppermute | solution.py:341
  16.4 3.1 %collective-permute-start.2 = (bf16[384,128]{1,0:T(8,128)(2,1)S(1)}, bf16[384,128]{1,0:T(8,128)(2,1)S(1)}, u32[]{:S(2)}, u32[]{:S(2)}) collective-permute-start(bf16[384,128]{1,0:T(8,128)(2,1)S(1)} %pad_maximum_fusion), channel_id=1, source_target_pairs={{0,1},{1,2},{2,3},{3,4},{4,5},{5,6},{6,7},{8,9},{9,10},{10,11},{11... | collective-permute-start | bytes 294920 | tf_op jit(solution)/shard_map/ppermute | solution.py:340
  19.5 0.9 select_select_fusion
  20.4 0.1 fusion.52
  20.5 0.6 collective-permute-done.2.b0_ref
  21.1 12.0 %shard_map.103 = (bf16[1024,128]{1,0:T(8,128)(2,1)S(1)}, bf16[1024,3456]{1,0:T(8,128)(2,1)}) custom-call(s32[1024,32]{1,0:T(8,128)S(1)} %get-tuple-element.61.place_ref, bf16[1024,128]{1,0:T(8,128)(2,1)S(1)} %bitcast.54, bf16[384,128]{1,0:T(8,128)(2,1)S(1)} %collective-permute-done.a0_ref, bf16[384,128]{1,0:T(8,128)(2,1)S(1)} %collective-permute-done.1.a2_ref, ...), custom_call_target="tpu_custom_call" | custom-call | flops 7247757312 | bytes 9437184 | tf_op jit(solution)/shard_map/pallas_call | solution.py:74
  33.1 0.2 fusion.5
  33.3 0.2 fusion.8
  33.6 0.1 maximum_maximum_fusion
  33.6 0.7 broadcast_in_dim.10
  34.4 11.4 %all-to-all-start = ((f32[128,3,128]{2,1,0:T(4,128)}), f32[128,3,128]{2,1,0:T(4,128)S(1)}, u32[]{:S(2)}, u32[]{:S(2)}) async-start(f32[128,3,128]{2,1,0:T(4,128)} %broadcast_in_dim.10), calls=%async_computation | async-start | bytes 524288 | tf_op jit(solution)/shard_map/all_to_all | solution.py:348
  45.8 0.2 copy.26
  46.0 0.0 copy-start.4
  46.0 5.9 %shard_map.104.conv_ref = f32[144,3456]{1,0:T(8,128)} custom-call(bf16[1024,3456]{1,0:T(8,128)(2,1)} %get-tuple-element.27.cols_ref, bf16[1024,128]{1,0:T(8,128)(2,1)S(1)} %get-tuple-element.26.rhs_ref), custom_call_target="tpu_custom_call" | custom-call | flops 905969664 | bytes 9437184 | tf_op jit(solution)/shard_map/pallas_call | solution.py:208
  52.0 4.6 %all-to-all-done = f32[128,3,128]{2,1,0:T(4,128)S(1)} async-done(((f32[128,3,128]{2,1,0:T(4,128)}), f32[128,3,128]{2,1,0:T(4,128)S(1)}, u32[]{:S(2)}, u32[]{:S(2)}) %all-to-all-start) | async-done | bytes 196640 | tf_op jit(solution)/shard_map/all_to_all | solution.py:348
  56.7 0.1 slice.68
  56.8 0.4 copy-done.5
  57.2 0.2 fusion.26
  57.5 0.7 broadcast_in_dim.12
  58.2 5.6 %all-to-all-start.1 = ((f32[128,2,128]{2,1,0:T(2,128)}), f32[128,2,128]{2,1,0:T(2,128)}, u32[]{:S(2)}, u32[]{:S(2)}) async-start(f32[128,2,128]{2,1,0:T(2,128)} %broadcast_in_dim.12), calls=%async_computation.1 | async-start | bytes 262144 | tf_op jit(solution)/shard_map/all_to_all | solution.py:348
  63.8 0.9 fusion.1.order_ref
  64.7 5.8 %shard_map.105.up_ref = f32[128,3456]{1,0:T(8,128)} custom-call(bf16[1024,3456]{1,0:T(8,128)(2,1)} %get-tuple-element.27.cols_ref, bf16[1024,128]{1,0:T(8,128)(2,1)S(1)} %get-tuple-element.59.rhs_ref), custom_call_target="tpu_custom_call" | custom-call | flops 905969664 | bytes 9437184 | tf_op jit(solution)/shard_map/pallas_call | solution.py:208
  70.5 3.2 %all-to-all-done.1 = f32[128,2,128]{2,1,0:T(2,128)} async-done(((f32[128,2,128]{2,1,0:T(2,128)}), f32[128,2,128]{2,1,0:T(2,128)}, u32[]{:S(2)}, u32[]{:S(2)}) %all-to-all-start.1) | async-done | bytes 131104 | tf_op jit(solution)/shard_map/all_to_all | solution.py:348
  73.6 1.1 fusion.55
  74.8 1.2 multiply_bitcast_fusion
  76.0 1.2 multiply_bitcast_fusion.1
  77.2 1.7 %fusion.23 = (bf16[1024,128]{1,0:T(8,128)(2,1)S(1)}, bf16[1,1,1024,128]{3,2,1,0:T(8,128)(2,1)}) fusion(bf16[1024,128]{1,0:T(8,128)(2,1)S(1)} %get-tuple-element.26.rhs_ref, bf16[1,1,1024,128]{3,2,1,0:T(8,128)(2,1)S(1)} %copy-done.3, f32[128]{0:T(128)} %copy-done.7, f32[128]{0:T(128)S(1)} %get-tuple-element.58, f32[128]{0:T(128)S(1)} %get-tuple-element.56, ...), kind=kLoop, calls=%fused_computation.33 | loop fusion | flops 2359296 | bytes 1056256 | tf_op jit(solution)/shard_map/convert_element_type | solution.py:416
  78.9 0.7 stack.40.scale_ref
  79.6 4.5 %shard_map.106 = bf16[128,4,8,128]{3,2,1,0:T(8,128)(2,1)} custom-call(f32[128,3456]{1,0:T(8,128)} %shard_map.105.up_ref, f32[144,3456]{1,0:T(8,128)} %shard_map.104.conv_ref, f32[8,128]{1,0:T(8,128)S(1)} %stack.40.scale_ref, bf16[1024,1024]{1,0:T(8,128)(2,1)S(1)} %fusion.1.order_ref), custom_call_target="tpu_custom_call" | custom-call | flops 1073741824 | bytes 5242880 | tf_op jit(solution)/shard_map/pallas_call | solution.py:278
  84.2 6.7 %all-to-all-start.2 = ((bf16[128,4,8,128]{3,2,1,0:T(8,128)(2,1)}), bf16[128,4,8,128]{3,2,1,0:T(8,128)(2,1)S(1)}, u32[]{:S(2)}, u32[]{:S(2)}) async-start(bf16[128,4,8,128]{3,2,1,0:T(8,128)(2,1)} %shard_map.106), calls=%async_computation.2 | async-start | bytes 2097152 | tf_op jit(solution)/shard_map/all_to_all | solution.py:434
  90.9 17.4 %shard_map.107 = (f32[1024,128]{1,0:T(8,128)S(1)}, bf16[384,128]{1,0:T(8,128)(2,1)S(1)}, bf16[128,128]{1,0:T(8,128)(2,1)S(1)}, bf16[128,128]{1,0:T(8,128)(2,1)S(1)}, bf16[384,128]{1,0:T(8,128)(2,1)S(1)}) custom-call(s32[2,32,512]{2,1,0:T(8,128)S(1)} %bitcast.51, s32[1024,32]{1,0:T(8,128)S(1)} %get-tuple-element.61.place_ref, ...), custom_call_target="tpu_custom_call" | custom-call | flops 8153726976 | bytes 2097152 | tf_op jit(solution)/shard_map/pallas_call | solution.py:146
  108.4 3.4 %collective-permute-start.4 = (bf16[384,128]{1,0:T(8,128)(2,1)S(1)}, bf16[384,128]{1,0:T(8,128)(2,1)S(1)}, u32[]{:S(2)}, u32[]{:S(2)}) collective-permute-start(bf16[384,128]{1,0:T(8,128)(2,1)S(1)} %get-tuple-element.34), channel_id=1, source_target_pairs={{0,8},{8,16},{16,24},{24,32},{32,40},{40,48},{48,56},{56,64},{64,7... | collective-permute-start | bytes 294920 | tf_op jit(solution)/shard_map/ppermute | solution.py:337
  111.8 1.3 %collective-permute-start.5 = (bf16[384,128]{1,0:T(8,128)(2,1)S(1)}, bf16[384,128]{1,0:T(8,128)(2,1)S(1)}, u32[]{:S(2)}, u32[]{:S(2)}) collective-permute-start(bf16[384,128]{1,0:T(8,128)(2,1)S(1)} %get-tuple-element.35), channel_id=1, source_target_pairs={{8,0},{16,8},{24,16},{32,24},{40,32},{48,40},{56,48},{64,56},{72,6... | collective-permute-start | bytes 294920 | tf_op jit(solution)/shard_map/ppermute | solution.py:338
  113.2 0.4 collective-permute-done.4.a0_ref
  113.6 3.6 %collective-permute-done.5.a2_ref = bf16[384,128]{1,0:T(8,128)(2,1)S(1)} collective-permute-done((bf16[384,128]{1,0:T(8,128)(2,1)S(1)}, bf16[384,128]{1,0:T(8,128)(2,1)S(1)}, u32[]{:S(2)}, u32[]{:S(2)}) %collective-permute-start.5) | collective-permute-done | bytes 98336 | tf_op jit(solution)/shard_map/ppermute | solution.py:338
  117.1 0.2 convert_reduce_fusion
  117.3 0.1 reshape.207
  117.5 3.7 %collective-permute-start.7 = (bf16[384,128]{1,0:T(8,128)(2,1)S(1)}, bf16[384,128]{1,0:T(8,128)(2,1)S(1)}, u32[]{:S(2)}, u32[]{:S(2)}) collective-permute-start(bf16[384,128]{1,0:T(8,128)(2,1)S(1)} %pad_maximum_fusion.3), channel_id=1, source_target_pairs={{1,0},{2,1},{3,2},{4,3},{5,4},{6,5},{7,6},{9,8},{10,9},{11,10},{12... | collective-permute-start | bytes 294920 | tf_op jit(solution)/shard_map/ppermute | solution.py:341
  121.2 3.1 %collective-permute-start.6 = (bf16[384,128]{1,0:T(8,128)(2,1)S(1)}, bf16[384,128]{1,0:T(8,128)(2,1)S(1)}, u32[]{:S(2)}, u32[]{:S(2)}) collective-permute-start(bf16[384,128]{1,0:T(8,128)(2,1)S(1)} %pad_maximum_fusion.2), channel_id=1, source_target_pairs={{0,1},{1,2},{2,3},{3,4},{4,5},{5,6},{6,7},{8,9},{9,10},{10,11},{11... | collective-permute-start | bytes 294920 | tf_op jit(solution)/shard_map/ppermute | solution.py:340
  124.3 0.8 copy.32
  125.1 0.8 collective-permute-done.6.b0_ref
  125.9 1.6 %shard_map.108 = bf16[1024,128]{1,0:T(8,128)(2,1)} custom-call(s32[8,128]{1,0:T(8,128)S(1)} %bitcast.53, bf16[384,128]{1,0:T(8,128)(2,1)S(1)} %collective-permute-done.4.a0_ref, bf16[384,128]{1,0:T(8,128)(2,1)S(1)} %collective-permute-done.5.a2_ref, bf16[384,128]{1,0:T(8,128)(2,1)S(1)} %collective-permute-done.6.b0_ref, ...), custom_call_target="tpu_custom_call" | custom-call | flops 268435456 | bytes 2097152 | tf_op jit(solution)/shard_map/pallas_call | solution.py:318
  (47 shorter events, 0.4 us)
Async XLA Ops:
  0.6 20.5 %copy-start.2 = (bf16[1,1,1024,128]{3,2,1,0:T(8,128)(2,1)S(1)}, bf16[1,1,1024,128]{3,2,1,0:T(8,128)(2,1)}, u32[]{:S(2)}) copy-start(bf16[1,1,1024,128]{3,2,1,0:T(8,128)(2,1)} %param.8) | copy-start | bytes 786436
  0.6 20.5 %copy-start.1 = (bf16[3456,128]{1,0:T(8,128)(2,1)S(1)}, bf16[3456,128]{1,0:T(8,128)(2,1)}, u32[]{:S(2)}) copy-start(bf16[3456,128]{1,0:T(8,128)(2,1)} %table_ref.1) | copy-start | bytes 2654212
  2.6 7.6 %collective-permute-start = (bf16[384,128]{1,0:T(8,128)(2,1)S(1)}, bf16[384,128]{1,0:T(8,128)(2,1)S(1)}, u32[]{:S(2)}, u32[]{:S(2)}) collective-permute-start(bf16[384,128]{1,0:T(8,128)(2,1)S(1)} %get-tuple-element.67), channel_id=1, source_target_pairs={{0,8},{8,16},{16,24},{24,32},{32,40},{40,48},{48,56},{56,64},{64,7... | collective-permute-start | bytes 294920 | tf_op jit(solution)/shard_map/ppermute | solution.py:337
  6.9 5.5 %collective-permute-start.1 = (bf16[384,128]{1,0:T(8,128)(2,1)S(1)}, bf16[384,128]{1,0:T(8,128)(2,1)S(1)}, u32[]{:S(2)}, u32[]{:S(2)}) collective-permute-start(bf16[384,128]{1,0:T(8,128)(2,1)S(1)} %get-tuple-element.66), channel_id=1, source_target_pairs={{8,0},{16,8},{24,16},{32,24},{40,32},{48,40},{56,48},{64,56},{72,6... | collective-permute-start | bytes 294920 | tf_op jit(solution)/shard_map/ppermute | solution.py:338
  12.5 8.0 %collective-permute-start.3 = (bf16[384,128]{1,0:T(8,128)(2,1)S(1)}, bf16[384,128]{1,0:T(8,128)(2,1)S(1)}, u32[]{:S(2)}, u32[]{:S(2)}) collective-permute-start(bf16[384,128]{1,0:T(8,128)(2,1)S(1)} %pad_maximum_fusion.1), channel_id=1, source_target_pairs={{1,0},{2,1},{3,2},{4,3},{5,4},{6,5},{7,6},{9,8},{10,9},{11,10},{12... | collective-permute-start | bytes 294920 | tf_op jit(solution)/shard_map/ppermute | solution.py:341
  16.4 4.7 %collective-permute-start.2 = (bf16[384,128]{1,0:T(8,128)(2,1)S(1)}, bf16[384,128]{1,0:T(8,128)(2,1)S(1)}, u32[]{:S(2)}, u32[]{:S(2)}) collective-permute-start(bf16[384,128]{1,0:T(8,128)(2,1)S(1)} %pad_maximum_fusion), channel_id=1, source_target_pairs={{0,1},{1,2},{2,3},{3,4},{4,5},{5,6},{6,7},{8,9},{9,10},{10,11},{11... | collective-permute-start | bytes 294920 | tf_op jit(solution)/shard_map/ppermute | solution.py:340
  34.4 22.2 %all-to-all-start = ((f32[128,3,128]{2,1,0:T(4,128)}), f32[128,3,128]{2,1,0:T(4,128)S(1)}, u32[]{:S(2)}, u32[]{:S(2)}) async-start(f32[128,3,128]{2,1,0:T(4,128)} %broadcast_in_dim.10), calls=%async_computation | async-start | bytes 524288 | tf_op jit(solution)/shard_map/all_to_all | solution.py:348
  46.0 11.2 %copy-start.3 = (bf16[1,1,1024,128]{3,2,1,0:T(8,128)(2,1)S(1)}, bf16[1,1,1024,128]{3,2,1,0:T(8,128)(2,1)}, u32[]{:S(2)}) copy-start(bf16[1,1,1024,128]{3,2,1,0:T(8,128)(2,1)} %param.15) | copy-start | bytes 786436
  46.0 11.2 %copy-start.4 = (f32[128]{0:T(128)S(1)}, f32[128]{0:T(128)}, u32[]{:S(2)}) copy-start(f32[128]{0:T(128)} %param.13) | copy-start | bytes 1540
  46.0 11.2 %copy-start.8 = (f32[128]{0:T(128)S(1)}, f32[128]{0:T(128)}, u32[]{:S(2)}) copy-start(f32[128]{0:T(128)} %param.14) | copy-start | bytes 1540
  56.7 0.5 copy-start.5
  58.2 15.5 %all-to-all-start.1 = ((f32[128,2,128]{2,1,0:T(2,128)}), f32[128,2,128]{2,1,0:T(2,128)}, u32[]{:S(2)}, u32[]{:S(2)}) async-start(f32[128,2,128]{2,1,0:T(2,128)} %broadcast_in_dim.12), calls=%async_computation.1 | async-start | bytes 262144 | tf_op jit(solution)/shard_map/all_to_all | solution.py:348
  76.0 1.3 %copy-start.7 = (f32[128]{0:T(128)}, f32[128]{0:T(128)S(1)}, u32[]{:S(2)}) copy-start(f32[128]{0:T(128)S(1)} %get-tuple-element.55) | copy-start | bytes 1540
  84.2 33.0 %all-to-all-start.2 = ((bf16[128,4,8,128]{3,2,1,0:T(8,128)(2,1)}), bf16[128,4,8,128]{3,2,1,0:T(8,128)(2,1)S(1)}, u32[]{:S(2)}, u32[]{:S(2)}) async-start(bf16[128,4,8,128]{3,2,1,0:T(8,128)(2,1)} %shard_map.106), calls=%async_computation.2 | async-start | bytes 2097152 | tf_op jit(solution)/shard_map/all_to_all | solution.py:434
  90.9 22.2 %copy-start.6 = (f32[128]{0:T(128)S(1)}, f32[128]{0:T(128)}, u32[]{:S(2)}) copy-start(f32[128]{0:T(128)} %copy-done.5) | copy-start | bytes 1540
  90.9 35.0 %copy-start = (s32[1,1,8,128]{3,2,1,0:T(8,128)S(1)}, s32[1,1,8,128]{3,2,1,0:T(8,128)}, u32[]{:S(2)}) copy-start(s32[1,1,8,128]{3,2,1,0:T(8,128)} %param.11) | copy-start | bytes 12292
  108.4 5.2 %collective-permute-start.4 = (bf16[384,128]{1,0:T(8,128)(2,1)S(1)}, bf16[384,128]{1,0:T(8,128)(2,1)S(1)}, u32[]{:S(2)}, u32[]{:S(2)}) collective-permute-start(bf16[384,128]{1,0:T(8,128)(2,1)S(1)} %get-tuple-element.34), channel_id=1, source_target_pairs={{0,8},{8,16},{16,24},{24,32},{32,40},{40,48},{48,56},{56,64},{64,7... | collective-permute-start | bytes 294920 | tf_op jit(solution)/shard_map/ppermute | solution.py:337
  111.8 5.4 %collective-permute-start.5 = (bf16[384,128]{1,0:T(8,128)(2,1)S(1)}, bf16[384,128]{1,0:T(8,128)(2,1)S(1)}, u32[]{:S(2)}, u32[]{:S(2)}) collective-permute-start(bf16[384,128]{1,0:T(8,128)(2,1)S(1)} %get-tuple-element.35), channel_id=1, source_target_pairs={{8,0},{16,8},{24,16},{32,24},{40,32},{48,40},{56,48},{64,56},{72,6... | collective-permute-start | bytes 294920 | tf_op jit(solution)/shard_map/ppermute | solution.py:338
  117.5 7.6 %collective-permute-start.7 = (bf16[384,128]{1,0:T(8,128)(2,1)S(1)}, bf16[384,128]{1,0:T(8,128)(2,1)S(1)}, u32[]{:S(2)}, u32[]{:S(2)}) collective-permute-start(bf16[384,128]{1,0:T(8,128)(2,1)S(1)} %pad_maximum_fusion.3), channel_id=1, source_target_pairs={{1,0},{2,1},{3,2},{4,3},{5,4},{6,5},{7,6},{9,8},{10,9},{11,10},{12... | collective-permute-start | bytes 294920 | tf_op jit(solution)/shard_map/ppermute | solution.py:341
  121.2 4.7 %collective-permute-start.6 = (bf16[384,128]{1,0:T(8,128)(2,1)S(1)}, bf16[384,128]{1,0:T(8,128)(2,1)S(1)}, u32[]{:S(2)}, u32[]{:S(2)}) collective-permute-start(bf16[384,128]{1,0:T(8,128)(2,1)S(1)} %pad_maximum_fusion.2), channel_id=1, source_target_pairs={{0,1},{1,2},{2,3},{3,4},{4,5},{5,6},{6,7},{8,9},{9,10},{10,11},{11... | collective-permute-start | bytes 294920 | tf_op jit(solution)/shard_map/ppermute | solution.py:340

commit v3 on v2

--- a/solution.py
+++ b/solution.py
@@ -91,27 +91,16 @@
     )(place, own, a0, a2, b0, b2, weight)
 
 
-def backward_kernel(group, row_ref, place_ref, grad_ref, table_ref, own_ref, lo_ref, m0_ref, m2_ref, hi_ref, acc_ref, hot_ref, rhs_ref, weight_ref, sems):
+def backward_kernel(group, row_ref, place_ref, grad_ref, weight_ref, own_ref, lo_ref, m0_ref, m2_ref, hi_ref, acc_ref, hot_ref, rhs_ref):
     rows, channels = grad_ref.shape
     block = acc_ref.shape[0]
     part = block // 8
     high = m0_ref.shape[0]
-    steps = TAPS // group
-    wide = group * channels
-
-    def fetch(step):
-        here = pl.ds(step * wide, wide)
-        return pltpu.make_async_copy(table_ref.at[here, :], weight_ref.at[here, :], sems.at[step])
-
-    for step in range(steps):
-        fetch(step).start()
     for q in range(rows // block):
         grad = grad_ref[pl.ds(q * block, block), :]
         place = place_ref[pl.ds(q * block, block), :]
         down = lax.broadcasted_iota(I32, (block, block), 0)
-        for g in range(steps):
-            if q == 0:
-                fetch(g).wait()
+        for g in range(TAPS // group):
             for n in range(group):
                 k = g * group + n
                 line = row_ref[q, k : k + 1, :]
@@ -142,10 +131,8 @@
 
 def backward(row, place, grad, weight, high, block=512, group=3):
     rows, channels = grad.shape
-    vmem = pl.BlockSpec(memory_space=pltpu.VMEM)
     return pl.pallas_call(
         functools.partial(backward_kernel, group),
-        in_specs=[vmem, vmem, vmem, pl.BlockSpec(memory_space=pltpu.HBM)],
         out_shape=(
             jax.ShapeDtypeStruct((rows, channels), F32),
             jax.ShapeDtypeStruct((3 * high, channels), BF16),
@@ -157,12 +144,10 @@
             pltpu.VMEM((block, 2 * channels), F32),
             pltpu.VMEM((block, group * block), BF16),
             pltpu.VMEM((group * block, 2 * channels), BF16),
-            pltpu.VMEM(weight.shape, BF16),
-            pltpu.SemaphoreType.DMA((TAPS // group,)),
         ],
         compiler_params=pltpu.CompilerParams(vmem_limit_bytes=16 << 20),
         cost_estimate=pl.CostEstimate(flops=TAPS*4*rows*channels*(block+64), bytes_accessed=2<<20, transcendentals=0),
-    )(row, place, grad, pltpu.with_memory_space_constraint(weight, pltpu.HBM))
+    )(row, place, grad, weight)
 
 
 def product_kernel(group, extra, cols_ref, rhs_ref, out_ref, left_ref, whole_ref, buffer_ref, in_sems, out_sems):
@@ -224,9 +209,9 @@
     )(pltpu.with_memory_space_constraint(cols, pltpu.HBM), rhs)
 
 
-def weight_kernel(across, down, group, up_ref, conv_ref, scale_ref, order_ref, out_ref, line_ref, first_ref, second_ref, sems):
-    channels = scale_ref.shape[1]
-    eighths = out_ref.shape[1]
+def weight_kernel(across, down, group, live_ref, sums_ref, batch_ref, upstream_ref, conv_out_ref, up_ref, conv_ref, order_ref, pieces_ref, grad_out_ref, line_ref, first_ref, second_ref, out_ref, grad_ref, sems, out_sems):
+    rows, channels = grad_ref.shape
+    eighths = pieces_ref.shape[1]
     wide = group * channels
     steps = TAPS // group
 
@@ -248,7 +233,26 @@
             copy.start()
     for k in range(TAPS, 8 * eighths):
         line_ref[line(k)] = jnp.zeros((channels, channels), BF16)
-    turned = scale_ref[...].T
+    grad_copy = pltpu.make_async_copy(grad_ref, grad_out_ref, out_sems.at[eighths])
+    scale, inverse_std, center, total = [batch_ref[n : n + 1, :] for n in range(4)]
+    sums = jnp.sum(sums_ref[...], axis=0)
+    mean_up, mean_cross = sums[0:1] / total, sums[1:2] / total
+    live = lax.broadcasted_iota(I32, (rows, channels), 0) < live_ref[0, 0]
+    normalized = (conv_out_ref[...].astype(F32) - center) * inverse_std
+    grad_ref[...] = (
+        scale
+        * (
+            upstream_ref[...].astype(F32)
+            - jnp.where(live, mean_up + normalized * mean_cross, 0.0)
+        )
+    ).astype(BF16)
+    grad_copy.start()
+    per_cross = scale * mean_cross * inverse_std
+    turned = jnp.concatenate(
+        [scale, scale * mean_up - per_cross * center, per_cross]
+        + [jnp.zeros((5, channels), F32)],
+        axis=0,
+    ).T
     scales = [jnp.broadcast_to(turned[:, n : n + 1], (channels, channels)) for n in range(3)]
     for step in range(steps):
         for copy in fetch(step):
@@ -262,6 +266,7 @@
             )
             line_ref[line(k)] = term.T.astype(BF16)
     placed = jnp.dot(line_ref[...], order_ref[...], preferred_element_type=F32).astype(BF16)
+    copies = []
     for e in range(eighths):
         for x in range(across):
             for y in range(down):
@@ -269,29 +274,46 @@
                 out_ref[x * down + y, e] = placed[
                     row : row + down, y * channels : (y + 1) * channels
                 ]
-
-
-def weight_terms(up_part, conv_part, scales, order, across, down, group=3):
+        copies.append(
+            pltpu.make_async_copy(out_ref.at[:, e], pieces_ref.at[:, e], out_sems.at[e])
+        )
+        copies[e].start()
+    for copy in copies:
+        copy.wait()
+    grad_copy.wait()
+
+
+def weight_terms(live, sums, batch, upstream, conv_out, up_part, conv_part, order, across, down, group=3):
     channels, wide = up_part.shape
     eighths = -(-TAPS // 8)
     vmem, hbm = pl.BlockSpec(memory_space=pltpu.VMEM), pl.BlockSpec(memory_space=pltpu.HBM)
     return pl.pallas_call(
         functools.partial(weight_kernel, across, down, group),
-        in_specs=[hbm, hbm, vmem, vmem],
-        out_specs=vmem,
-        out_shape=jax.ShapeDtypeStruct((across * down, eighths, down, channels), BF16),
+        in_specs=[pl.BlockSpec(memory_space=pltpu.SMEM), vmem, vmem, vmem, vmem, hbm, hbm, vmem],
+        out_specs=(hbm, hbm),
+        out_shape=(
+            pltpu.HBM((across * down, eighths, down, channels), BF16),
+            pltpu.HBM(upstream.shape, BF16),
+        ),
         scratch_shapes=[
             pltpu.VMEM((eighths * channels, 8 * channels), BF16),
             pltpu.VMEM(up_part.shape, F32),
             pltpu.VMEM(conv_part.shape, F32),
+            pltpu.VMEM((across * down, eighths, down, channels), BF16),
+            pltpu.VMEM(upstream.shape, BF16),
             pltpu.SemaphoreType.DMA((2, TAPS // group)),
+            pltpu.SemaphoreType.DMA((eighths + 1,)),
         ],
-        compiler_params=pltpu.CompilerParams(vmem_limit_bytes=16 << 20),
+        compiler_params=pltpu.CompilerParams(vmem_limit_bytes=20 << 20),
         cost_estimate=pl.CostEstimate(flops=1 << 30, bytes_accessed=5 << 20, transcendentals=0),
     )(
+        live,
+        sums,
+        batch,
+        upstream,
+        conv_out,
         pltpu.with_memory_space_constraint(up_part, pltpu.HBM),
         pltpu.with_memory_space_constraint(conv_part, pltpu.HBM),
-        scales,
         order,
     )
 
@@ -391,8 +413,16 @@
     stats = everyones(
         jnp.stack([local_mean, local_square, jnp.full((channels,), local_count)])
     )
+    width = channels // down
+    source = lax.broadcasted_iota(I32, (8 * channels, 1), 0)
+    spot = lax.broadcasted_iota(I32, (1, down * channels), 1)
+    order = (
+        source == (spot // width) % 8 * channels + spot // channels * width + spot % width
+    ).astype(BF16)
     conv_part = product(cols, conv_out, extra=16)
-    stats, place_rows, conv_part = lax.optimization_barrier((stats, place_rows, conv_part))
+    stats, place_rows, conv_part, order = lax.optimization_barrier(
+        (stats, place_rows, conv_part, order)
+    )
     counts = stats[:, 2]
     total_count = jnp.sum(counts, axis=0)
     center = jnp.sum(stats[:, 0] * counts, axis=0) / total_count
@@ -406,31 +436,17 @@
     sums = everyones(
         jnp.stack([jnp.sum(upstream, axis=0), jnp.sum(upstream * normalized, axis=0)])
     )
-    up_part = product(cols, upstream.astype(BF16))
-    sums, up_part = lax.optimization_barrier((sums, up_part))
-    mean_up = jnp.sum(sums[:, 0], axis=0) / total_count
-    mean_cross = jnp.sum(sums[:, 1], axis=0) / total_count
+    upstream = upstream.astype(BF16)
+    up_part = product(cols, upstream)
     scale = gain * inverse_std
-    conv_grad = (
-        scale * (upstream - live_mask * (mean_up + normalized * mean_cross))
-    ).astype(BF16)
-
-    width = channels // down
-    source = lax.broadcasted_iota(I32, (8 * channels, 1), 0)
-    spot = lax.broadcasted_iota(I32, (1, down * channels), 1)
-    order = (
-        source == (spot // width) % 8 * channels + spot // channels * width + spot % width
-    ).astype(BF16)
-    scales = jnp.stack(
-        [
-            scale,
-            scale * (mean_up - mean_cross * inverse_std * center),
-            scale * mean_cross * inverse_std,
-        ]
-        + [jnp.zeros_like(scale)] * 5
-    )
-    pieces = weight_terms(up_part, conv_part, scales, order, across, down)
-    pieces, conv_grad = lax.optimization_barrier((pieces, conv_grad))
+    batch = jnp.stack(
+        [scale, inverse_std, center, jnp.broadcast_to(total_count, scale.shape)]
+        + [jnp.zeros_like(scale)] * 4
+    )
+    sums, up_part, batch = lax.optimization_barrier((sums, up_part, batch))
+    pieces, conv_grad = weight_terms(
+        live_count, sums, batch, upstream, conv_out, up_part, conv_part, order, across, down
+    )
     arrived = lax.all_to_all(pieces, axes, 0, 0, tiled=True)
     own_table, *halo = backward(place_rows, place_down, conv_grad, weight, size)
     a0, a2, b0, b2, arrived = from_neighbours(*halo, arrived)

time: 129 us -> 128 us (level)
  Pallas kernels: 47.2 us -> 42.2 us
  local copies, waits for them, and re-layouts: 6.07 us -> 9.13 us
  starting transfers between devices: 47.8 us -> 50.7 us
  other arithmetic: 7.18 us -> 5.63 us
    ppermute x2, waiting for transfers between devices: 0.01 us -> 6.06 us  [from_neighbours(): lax.ppermute(jnp.concatenate([a0[:size], mid_low, a2[:size]]), 'by', down_y)]
    pallas_call x1, Pallas kernels: 17.4 us -> 12.6 us  [backward(): pl.pallas_call(functools.partial(backward_kernel, group), out_shape=(jax....]
    ppermute x2, starting transfers between devices: 7.53 us -> 3.84 us  [from_neighbours(): lax.ppermute(jnp.concatenate([a0[:size], mid_low, a2[:size]]), 'by', down_y)]
    ppermute x2, starting transfers between devices: 6.16 us -> 9.26 us  [from_neighbours(): lax.ppermute(jnp.concatenate([a0[2 * size:], mid_high, a2[2 * size:]]), '...]
    all_to_all x2, starting transfers between devices: 17 us -> 19.6 us  [everyones(): return lax.all_to_all(copies, axes, 0, 0, tiled=True)]
    ppermute x2, waiting for transfers between devices: 5.93 us -> 3.57 us  [from_neighbours(): a2 = lax.ppermute(low, 'bx', down_x)]
    unnamed x20 -> x18, local copies, waits for them, and re-layouts: 2.28 us -> 4.53 us
    another operation x2 -> x1, other arithmetic: 2.43 us -> 0.6 us  [per_device(): jnp.stack([scale, inverse_std, center, jnp.broadcast_to(total_count, scal...]
  transfers between devices with their start and end apart: 11 -> 11, of which waited for: 7 -> 6; matrix products, arithmetic and copies ran while one was open for 3% -> 4% of each run, Pallas kernels for 23% -> 19%
where the time goes in v3:
time: 128 us
  starting transfers between devices  50.7 us (40%)
  Pallas kernels  42.2 us (33%)
  waiting for transfers between devices  16.4 us (13%)
  local copies, waits for them, and re-layouts  9.13 us (7%)
  other arithmetic  5.63 us (4%)
  matrix products  1.88 us (1%)
  between operations  1.71 us (1%)
    all_to_all x2, starting transfers between devices, everyones(): return lax.all_to_all(copies, axes, 0, 0, tiled=True)  19.6 us
    pallas_call x1, Pallas kernels, backward(): pl.pallas_call(functools.partial(backward_kernel, group), out_shape=(jax....  12.6 us
    pallas_call x1, Pallas kernels, forward(): pl.pallas_call(functools.partial(forward_kernel, chunks), in_specs=[vmem]...  11.7 us
    pallas_call x2, Pallas kernels, product(): pl.pallas_call(functools.partial(product_kernel, group, extra), in_specs=...  11.7 us
    ppermute x2, starting transfers between devices, from_neighbours(): lax.ppermute(jnp.concatenate([a0[2 * size:], mid_high, a2[2 * size:]]), '...  9.26 us
    ppermute x2, starting transfers between devices, from_neighbours(): a0 = lax.ppermute(high, 'bx', up_x)  8.42 us
    all_to_all x1, starting transfers between devices, per_device(): arrived = lax.all_to_all(pieces, axes, 0, 0, tiled=True)  6.99 us
    all_to_all x2, waiting for transfers between devices, everyones(): return lax.all_to_all(copies, axes, 0, 0, tiled=True)  6.35 us
  transfers between devices with their start and end apart: 11, of which 6 were waited for; matrix products, arithmetic and copies ran while one was open for 4% of the time, Pallas kernels for 19%

profile of v3, /device:TPU:1, one launch (start us, length us, event | category | flops | bytes accessed | tf_op | source)
XLA Modules:
  0.0 127.6 jit_solution(3152465379844912224)
XLA Ops:
  0.7 1.9 %fusion.3 = bf16[1024,128]{1,0:T(8,128)(2,1)S(1)} fusion(s32[1024]{0:T(1024)} %bitcast.55, bf16[1,1,1024,128]{3,2,1,0:T(8,128)(2,1)} %param.8), kind=kOutput, calls=%fused_computation.6 | convolution fusion | flops 269615104 | bytes 528384 | tf_op jit(solution)/shard_map/dot_general | solution.py:384
  2.6 1.3 %collective-permute-start.1 = (bf16[384,128]{1,0:T(8,128)(2,1)S(1)}, bf16[384,128]{1,0:T(8,128)(2,1)S(1)}, u32[]{:S(2)}, u32[]{:S(2)}) collective-permute-start(bf16[384,128]{1,0:T(8,128)(2,1)S(1)} %get-tuple-element.66), channel_id=1, source_target_pairs={{8,0},{16,8},{24,16},{32,24},{40,32},{48,40},{56,48},{64,56},{72,6... | collective-permute-start | bytes 294920 | tf_op jit(solution)/shard_map/ppermute | solution.py:360
  3.9 5.0 %collective-permute-start = (bf16[384,128]{1,0:T(8,128)(2,1)S(1)}, bf16[384,128]{1,0:T(8,128)(2,1)S(1)}, u32[]{:S(2)}, u32[]{:S(2)}) collective-permute-start(bf16[384,128]{1,0:T(8,128)(2,1)S(1)} %get-tuple-element.67), channel_id=1, source_target_pairs={{0,8},{8,16},{16,24},{24,32},{32,40},{40,48},{48,56},{56,64},{64,7... | collective-permute-start | bytes 294920 | tf_op jit(solution)/shard_map/ppermute | solution.py:359
  9.6 1.1 copy.25
  10.7 0.1 pad.15.clone
  10.8 4.4 %collective-permute-start.2 = (bf16[384,128]{1,0:T(8,128)(2,1)S(1)}, bf16[384,128]{1,0:T(8,128)(2,1)S(1)}, u32[]{:S(2)}, u32[]{:S(2)}) collective-permute-start(bf16[384,128]{1,0:T(8,128)(2,1)S(1)} %pad_maximum_fusion), channel_id=1, source_target_pairs={{0,1},{1,2},{2,3},{3,4},{4,5},{5,6},{6,7},{8,9},{9,10},{10,11},{11... | collective-permute-start | bytes 294920 | tf_op jit(solution)/shard_map/ppermute | solution.py:362
  15.3 1.9 %collective-permute-start.3 = (bf16[384,128]{1,0:T(8,128)(2,1)S(1)}, bf16[384,128]{1,0:T(8,128)(2,1)S(1)}, u32[]{:S(2)}, u32[]{:S(2)}) collective-permute-start(bf16[384,128]{1,0:T(8,128)(2,1)S(1)} %pad_maximum_fusion.1), channel_id=1, source_target_pairs={{1,0},{2,1},{3,2},{4,3},{5,4},{6,5},{7,6},{9,8},{10,9},{11,10},{12... | collective-permute-start | bytes 294920 | tf_op jit(solution)/shard_map/ppermute | solution.py:363
  17.2 0.9 select_select_fusion
  18.1 0.1 fusion.46
  18.2 3.0 %collective-permute-done.3.b2_ref = bf16[384,128]{1,0:T(8,128)(2,1)S(1)} collective-permute-done((bf16[384,128]{1,0:T(8,128)(2,1)S(1)}, bf16[384,128]{1,0:T(8,128)(2,1)S(1)}, u32[]{:S(2)}, u32[]{:S(2)}) %collective-permute-start.3) | collective-permute-done | bytes 98336 | tf_op jit(solution)/shard_map/ppermute | solution.py:363
  21.2 11.7 %shard_map.103 = (bf16[1024,128]{1,0:T(8,128)(2,1)S(1)}, bf16[1024,3456]{1,0:T(8,128)(2,1)}) custom-call(s32[1024,32]{1,0:T(8,128)S(1)} %get-tuple-element.62.place_ref, bf16[1024,128]{1,0:T(8,128)(2,1)S(1)} %bitcast.57, bf16[384,128]{1,0:T(8,128)(2,1)S(1)} %collective-permute-done.a0_ref, bf16[384,128]{1,0:T(8,128)(2,1)S(1)} %collective-permute-done.1.a2_ref, ...), custom_call_target="tpu_custom_call" | custom-call | flops 7247757312 | bytes 9437184 | tf_op jit(solution)/shard_map/pallas_call | solution.py:74
  32.9 0.2 fusion.5
  33.2 0.2 fusion.8
  33.4 0.1 maximum_maximum_fusion
  33.5 0.7 broadcast_in_dim.10
  34.2 13.3 %all-to-all-start = ((f32[128,3,128]{2,1,0:T(4,128)}), f32[128,3,128]{2,1,0:T(4,128)}, u32[]{:S(2)}, u32[]{:S(2)}) async-start(f32[128,3,128]{2,1,0:T(4,128)} %broadcast_in_dim.10), calls=%async_computation | async-start | bytes 524288 | tf_op jit(solution)/shard_map/all_to_all | solution.py:370
  47.5 0.9 fusion.1.order_ref
  48.4 0.2 copy.26
  48.6 0.0 copy-start.5
  48.6 5.9 %shard_map.104.conv_ref = f32[144,3456]{1,0:T(8,128)} custom-call(bf16[1024,3456]{1,0:T(8,128)(2,1)} %get-tuple-element.29.cols_ref, bf16[1024,128]{1,0:T(8,128)(2,1)S(1)} %get-tuple-element.28.rhs_ref.conv_out_ref), custom_call_target="tpu_custom_call" | custom-call | flops 905969664 | bytes 9437184 | tf_op jit(solution)/shard_map/pallas_call | solution.py:193
  54.6 3.6 %all-to-all-done = f32[128,3,128]{2,1,0:T(4,128)} async-done(((f32[128,3,128]{2,1,0:T(4,128)}), f32[128,3,128]{2,1,0:T(4,128)}, u32[]{:S(2)}, u32[]{:S(2)}) %all-to-all-start) | async-done | bytes 196640 | tf_op jit(solution)/shard_map/all_to_all | solution.py:370
  58.1 1.0 slice.62
  59.1 1.0 copy.27
  60.2 0.5 copy-done.7
  60.8 0.6 multiply_bitcast_fusion
  61.4 1.6 %fusion.20 = (f32[128]{0:T(128)S(1)}, f32[128]{0:T(128)S(1)}, bf16[1024,128]{1,0:T(8,128)(2,1)S(1)}, bf16[1,1,1024,128]{3,2,1,0:T(8,128)(2,1)}) fusion(bf16[1,1,1024,128]{3,2,1,0:T(8,128)(2,1)S(1)} %copy-done.5, f32[1024]{0:T(1024)S(1)} %fusion.44, f32[128]{0:T(128)} %param.14, f32[128]{0:T(128)S(1)} %get-tuple-element.59, f32[128]{0:T(128)S(1)} %div.96, ...), kind=kLoop, calls=%fused_computation.31 | loop fusion | flops 2096896 | bytes 1055744 | tf_op jit(solution)/shard_map/reduce_sum | solution.py:437
  63.0 0.7 broadcast_in_dim.12
  63.7 6.2 %all-to-all-start.1 = ((f32[128,2,128]{2,1,0:T(2,128)}), f32[128,2,128]{2,1,0:T(2,128)S(1)}, u32[]{:S(2)}, u32[]{:S(2)}) async-start(f32[128,2,128]{2,1,0:T(2,128)} %broadcast_in_dim.12), calls=%async_computation.1 | async-start | bytes 262144 | tf_op jit(solution)/shard_map/all_to_all | solution.py:370
  69.9 0.6 bitcast_divide_fusion
  70.6 0.7 stack.35.batch_ref
  71.3 5.8 %shard_map.105.up_ref = f32[128,3456]{1,0:T(8,128)} custom-call(bf16[1024,3456]{1,0:T(8,128)(2,1)} %get-tuple-element.29.cols_ref, bf16[1024,128]{1,0:T(8,128)(2,1)S(1)} %get-tuple-element.60.rhs_ref.upstream_ref), custom_call_target="tpu_custom_call" | custom-call | flops 905969664 | bytes 9437184 | tf_op jit(solution)/shard_map/pallas_call | solution.py:193
  77.1 2.8 %all-to-all-done.1.sums_ref = f32[128,2,128]{2,1,0:T(2,128)S(1)} async-done(((f32[128,2,128]{2,1,0:T(2,128)}), f32[128,2,128]{2,1,0:T(2,128)S(1)}, u32[]{:S(2)}, u32[]{:S(2)}) %all-to-all-start.1) | async-done | bytes 131104 | tf_op jit(solution)/shard_map/all_to_all | solution.py:370
  79.9 4.6 %shard_map.106 = (bf16[128,4,8,128]{3,2,1,0:T(8,128)(2,1)}, bf16[1024,128]{1,0:T(8,128)(2,1)}) custom-call(s32[1,1]{1,0:T(1,128)} %copy.31.live_ref, f32[128,2,128]{2,1,0:T(2,128)S(1)} %all-to-all-done.1.sums_ref, f32[8,128]{1,0:T(8,128)S(1)} %stack.35.batch_ref, bf16[1024,128]{1,0:T(8,128)(2,1)S(1)} %get-tuple-element.60.rhs_ref.upstream_ref, ...), custom_call_target="tpu_custom_call" | custom-call | flops 1073741824 | bytes 5242880 | tf_op jit(solution)/shard_map/pallas_call | solution.py:290
  84.5 7.0 %all-to-all-start.2 = ((bf16[128,4,8,128]{3,2,1,0:T(8,128)(2,1)}), bf16[128,4,8,128]{3,2,1,0:T(8,128)(2,1)S(1)}, u32[]{:S(2)}, u32[]{:S(2)}) async-start(bf16[128,4,8,128]{3,2,1,0:T(8,128)(2,1)} %get-tuple-element.40), calls=%async_computation.2 | async-start | bytes 2097152 | tf_op jit(solution)/shard_map/all_to_all | solution.py:450
  91.5 1.2 copy-done.2
  92.7 0.9 copy-done.4
  93.6 12.6 %shard_map.107 = (f32[1024,128]{1,0:T(8,128)S(1)}, bf16[384,128]{1,0:T(8,128)(2,1)S(1)}, bf16[128,128]{1,0:T(8,128)(2,1)S(1)}, bf16[128,128]{1,0:T(8,128)(2,1)S(1)}, bf16[384,128]{1,0:T(8,128)(2,1)S(1)}) custom-call(s32[2,32,512]{2,1,0:T(8,128)S(1)} %bitcast.54, s32[1024,32]{1,0:T(8,128)S(1)} %get-tuple-element.62.place_ref, ...), custom_call_target="tpu_custom_call" | custom-call | flops 8153726976 | bytes 2097152 | tf_op jit(solution)/shard_map/pallas_call | solution.py:134
  106.2 3.4 %collective-permute-start.4 = (bf16[384,128]{1,0:T(8,128)(2,1)S(1)}, bf16[384,128]{1,0:T(8,128)(2,1)S(1)}, u32[]{:S(2)}, u32[]{:S(2)}) collective-permute-start(bf16[384,128]{1,0:T(8,128)(2,1)S(1)} %get-tuple-element.38), channel_id=1, source_target_pairs={{0,8},{8,16},{16,24},{24,32},{32,40},{40,48},{48,56},{56,64},{64,7... | collective-permute-start | bytes 294920 | tf_op jit(solution)/shard_map/ppermute | solution.py:359
  109.6 1.3 %collective-permute-start.5 = (bf16[384,128]{1,0:T(8,128)(2,1)S(1)}, bf16[384,128]{1,0:T(8,128)(2,1)S(1)}, u32[]{:S(2)}, u32[]{:S(2)}) collective-permute-start(bf16[384,128]{1,0:T(8,128)(2,1)S(1)} %get-tuple-element.39), channel_id=1, source_target_pairs={{8,0},{16,8},{24,16},{32,24},{40,32},{48,40},{56,48},{64,56},{72,6... | collective-permute-start | bytes 294920 | tf_op jit(solution)/shard_map/ppermute | solution.py:360
  111.0 0.4 collective-permute-done.4.a0_ref
  111.4 3.6 %collective-permute-done.5.a2_ref = bf16[384,128]{1,0:T(8,128)(2,1)S(1)} collective-permute-done((bf16[384,128]{1,0:T(8,128)(2,1)S(1)}, bf16[384,128]{1,0:T(8,128)(2,1)S(1)}, u32[]{:S(2)}, u32[]{:S(2)}) %collective-permute-start.5) | collective-permute-done | bytes 98336 | tf_op jit(solution)/shard_map/ppermute | solution.py:360
  115.0 0.2 convert_reduce_fusion
  115.2 4.8 %collective-permute-start.6 = (bf16[384,128]{1,0:T(8,128)(2,1)S(1)}, bf16[384,128]{1,0:T(8,128)(2,1)S(1)}, u32[]{:S(2)}, u32[]{:S(2)}) collective-permute-start(bf16[384,128]{1,0:T(8,128)(2,1)S(1)} %pad_maximum_fusion.2), channel_id=1, source_target_pairs={{0,1},{1,2},{2,3},{3,4},{4,5},{5,6},{6,7},{8,9},{9,10},{10,11},{11... | collective-permute-start | bytes 294920 | tf_op jit(solution)/shard_map/ppermute | solution.py:362
  120.1 1.9 %collective-permute-start.7 = (bf16[384,128]{1,0:T(8,128)(2,1)S(1)}, bf16[384,128]{1,0:T(8,128)(2,1)S(1)}, u32[]{:S(2)}, u32[]{:S(2)}) collective-permute-start(bf16[384,128]{1,0:T(8,128)(2,1)S(1)} %pad_maximum_fusion.3), channel_id=1, source_target_pairs={{1,0},{2,1},{3,2},{4,3},{5,4},{6,5},{7,6},{9,8},{10,9},{11,10},{12... | collective-permute-start | bytes 294920 | tf_op jit(solution)/shard_map/ppermute | solution.py:363
  122.0 0.1 reshape.212
  122.2 0.8 copy.30
  122.9 3.1 %collective-permute-done.7.b2_ref = bf16[384,128]{1,0:T(8,128)(2,1)S(1)} collective-permute-done((bf16[384,128]{1,0:T(8,128)(2,1)S(1)}, bf16[384,128]{1,0:T(8,128)(2,1)S(1)}, u32[]{:S(2)}, u32[]{:S(2)}) %collective-permute-start.7) | collective-permute-done | bytes 98336 | tf_op jit(solution)/shard_map/ppermute | solution.py:363
  126.0 1.6 %shard_map.108 = bf16[1024,128]{1,0:T(8,128)(2,1)} custom-call(s32[8,128]{1,0:T(8,128)S(1)} %bitcast.56, bf16[384,128]{1,0:T(8,128)(2,1)S(1)} %collective-permute-done.4.a0_ref, bf16[384,128]{1,0:T(8,128)(2,1)S(1)} %collective-permute-done.5.a2_ref, bf16[384,128]{1,0:T(8,128)(2,1)S(1)} %collective-permute-done.6.b0_ref, ...), custom_call_target="tpu_custom_call" | custom-call | flops 268435456 | bytes 2097152 | tf_op jit(solution)/shard_map/pallas_call | solution.py:340
  (39 shorter events, 0.3 us)
Async XLA Ops:
  0.6 20.6 %copy-start.3 = (bf16[1,1,1024,128]{3,2,1,0:T(8,128)(2,1)S(1)}, bf16[1,1,1024,128]{3,2,1,0:T(8,128)(2,1)}, u32[]{:S(2)}) copy-start(bf16[1,1,1024,128]{3,2,1,0:T(8,128)(2,1)} %param.8) | copy-start | bytes 786436
  0.6 20.6 %copy-start.1 = (bf16[3456,128]{1,0:T(8,128)(2,1)S(1)}, bf16[3456,128]{1,0:T(8,128)(2,1)}, u32[]{:S(2)}) copy-start(bf16[3456,128]{1,0:T(8,128)(2,1)} %weight_ref.3) | copy-start | bytes 2654212
  2.6 8.2 %collective-permute-start.1 = (bf16[384,128]{1,0:T(8,128)(2,1)S(1)}, bf16[384,128]{1,0:T(8,128)(2,1)S(1)}, u32[]{:S(2)}, u32[]{:S(2)}) collective-permute-start(bf16[384,128]{1,0:T(8,128)(2,1)S(1)} %get-tuple-element.66), channel_id=1, source_target_pairs={{8,0},{16,8},{24,16},{32,24},{40,32},{48,40},{56,48},{64,56},{72,6... | collective-permute-start | bytes 294920 | tf_op jit(solution)/shard_map/ppermute | solution.py:360
  3.9 6.9 %collective-permute-start = (bf16[384,128]{1,0:T(8,128)(2,1)S(1)}, bf16[384,128]{1,0:T(8,128)(2,1)S(1)}, u32[]{:S(2)}, u32[]{:S(2)}) collective-permute-start(bf16[384,128]{1,0:T(8,128)(2,1)S(1)} %get-tuple-element.67), channel_id=1, source_target_pairs={{0,8},{8,16},{16,24},{24,32},{32,40},{40,48},{48,56},{56,64},{64,7... | collective-permute-start | bytes 294920 | tf_op jit(solution)/shard_map/ppermute | solution.py:359
  10.8 7.4 %collective-permute-start.2 = (bf16[384,128]{1,0:T(8,128)(2,1)S(1)}, bf16[384,128]{1,0:T(8,128)(2,1)S(1)}, u32[]{:S(2)}, u32[]{:S(2)}) collective-permute-start(bf16[384,128]{1,0:T(8,128)(2,1)S(1)} %pad_maximum_fusion), channel_id=1, source_target_pairs={{0,1},{1,2},{2,3},{3,4},{4,5},{5,6},{6,7},{8,9},{9,10},{10,11},{11... | collective-permute-start | bytes 294920 | tf_op jit(solution)/shard_map/ppermute | solution.py:362
  15.3 5.9 %collective-permute-start.3 = (bf16[384,128]{1,0:T(8,128)(2,1)S(1)}, bf16[384,128]{1,0:T(8,128)(2,1)S(1)}, u32[]{:S(2)}, u32[]{:S(2)}) collective-permute-start(bf16[384,128]{1,0:T(8,128)(2,1)S(1)} %pad_maximum_fusion.1), channel_id=1, source_target_pairs={{1,0},{2,1},{3,2},{4,3},{5,4},{6,5},{7,6},{9,8},{10,9},{11,10},{12... | collective-permute-start | bytes 294920 | tf_op jit(solution)/shard_map/ppermute | solution.py:363
  34.2 23.9 %all-to-all-start = ((f32[128,3,128]{2,1,0:T(4,128)}), f32[128,3,128]{2,1,0:T(4,128)}, u32[]{:S(2)}, u32[]{:S(2)}) async-start(f32[128,3,128]{2,1,0:T(4,128)} %broadcast_in_dim.10), calls=%async_computation | async-start | bytes 524288 | tf_op jit(solution)/shard_map/all_to_all | solution.py:370
  48.6 12.1 %copy-start.6 = (f32[128]{0:T(128)S(1)}, f32[128]{0:T(128)}, u32[]{:S(2)}) copy-start(f32[128]{0:T(128)} %param.13) | copy-start | bytes 1540
  48.6 12.7 %copy-start.5 = (bf16[1,1,1024,128]{3,2,1,0:T(8,128)(2,1)S(1)}, bf16[1,1,1024,128]{3,2,1,0:T(8,128)(2,1)}, u32[]{:S(2)}) copy-start(bf16[1,1,1024,128]{3,2,1,0:T(8,128)(2,1)} %param.15) | copy-start | bytes 786436
  60.2 0.5 copy-start.7
  63.7 16.2 %all-to-all-start.1 = ((f32[128,2,128]{2,1,0:T(2,128)}), f32[128,2,128]{2,1,0:T(2,128)S(1)}, u32[]{:S(2)}, u32[]{:S(2)}) async-start(f32[128,2,128]{2,1,0:T(2,128)} %broadcast_in_dim.12), calls=%async_computation.1 | async-start | bytes 262144 | tf_op jit(solution)/shard_map/all_to_all | solution.py:370
  84.5 30.5 %all-to-all-start.2 = ((bf16[128,4,8,128]{3,2,1,0:T(8,128)(2,1)}), bf16[128,4,8,128]{3,2,1,0:T(8,128)(2,1)S(1)}, u32[]{:S(2)}, u32[]{:S(2)}) async-start(bf16[128,4,8,128]{3,2,1,0:T(8,128)(2,1)} %get-tuple-element.40), calls=%async_computation.2 | async-start | bytes 2097152 | tf_op jit(solution)/shard_map/all_to_all | solution.py:450
  91.5 1.2 copy-start.2
  92.7 0.9 copy-start.4
  93.6 32.4 %copy-start = (s32[1,1,8,128]{3,2,1,0:T(8,128)S(1)}, s32[1,1,8,128]{3,2,1,0:T(8,128)}, u32[]{:S(2)}) copy-start(s32[1,1,8,128]{3,2,1,0:T(8,128)} %param.11) | copy-start | bytes 12292
  106.2 5.2 %collective-permute-start.4 = (bf16[384,128]{1,0:T(8,128)(2,1)S(1)}, bf16[384,128]{1,0:T(8,128)(2,1)S(1)}, u32[]{:S(2)}, u32[]{:S(2)}) collective-permute-start(bf16[384,128]{1,0:T(8,128)(2,1)S(1)} %get-tuple-element.38), channel_id=1, source_target_pairs={{0,8},{8,16},{16,24},{24,32},{32,40},{40,48},{48,56},{56,64},{64,7... | collective-permute-start | bytes 294920 | tf_op jit(solution)/shard_map/ppermute | solution.py:359
  109.6 5.4 %collective-permute-start.5 = (bf16[384,128]{1,0:T(8,128)(2,1)S(1)}, bf16[384,128]{1,0:T(8,128)(2,1)S(1)}, u32[]{:S(2)}, u32[]{:S(2)}) collective-permute-start(bf16[384,128]{1,0:T(8,128)(2,1)S(1)} %get-tuple-element.39), channel_id=1, source_target_pairs={{8,0},{16,8},{24,16},{32,24},{40,32},{48,40},{56,48},{64,56},{72,6... | collective-permute-start | bytes 294920 | tf_op jit(solution)/shard_map/ppermute | solution.py:360
  115.2 7.7 %collective-permute-start.6 = (bf16[384,128]{1,0:T(8,128)(2,1)S(1)}, bf16[384,128]{1,0:T(8,128)(2,1)S(1)}, u32[]{:S(2)}, u32[]{:S(2)}) collective-permute-start(bf16[384,128]{1,0:T(8,128)(2,1)S(1)} %pad_maximum_fusion.2), channel_id=1, source_target_pairs={{0,1},{1,2},{2,3},{3,4},{4,5},{5,6},{6,7},{8,9},{9,10},{10,11},{11... | collective-permute-start | bytes 294920 | tf_op jit(solution)/shard_map/ppermute | solution.py:362
  120.1 5.9 %collective-permute-start.7 = (bf16[384,128]{1,0:T(8,128)(2,1)S(1)}, bf16[384,128]{1,0:T(8,128)(2,1)S(1)}, u32[]{:S(2)}, u32[]{:S(2)}) collective-permute-start(bf16[384,128]{1,0:T(8,128)(2,1)S(1)} %pad_maximum_fusion.3), channel_id=1, source_target_pairs={{1,0},{2,1},{3,2},{4,3},{5,4},{6,5},{7,6},{9,8},{10,9},{11,10},{12... | collective-permute-start | bytes 294920 | tf_op jit(solution)/shard_map/ppermute | solution.py:363

commit v4 on v3

--- a/solution.py
+++ b/solution.py
@@ -91,7 +91,15 @@
     )(place, own, a0, a2, b0, b2, weight)
 
 
-def backward_kernel(group, row_ref, place_ref, grad_ref, weight_ref, own_ref, lo_ref, m0_ref, m2_ref, hi_ref, acc_ref, hot_ref, rhs_ref):
+def backward_kernel(group, row_ref, place_ref, grad_in_ref, weight_in_ref, own_ref, lo_ref, m0_ref, m2_ref, hi_ref, acc_ref, hot_ref, rhs_ref, grad_ref, weight_ref, sems):
+    copies = (
+        pltpu.make_async_copy(grad_in_ref, grad_ref, sems.at[0]),
+        pltpu.make_async_copy(weight_in_ref, weight_ref, sems.at[1]),
+    )
+    for copy in copies:
+        copy.start()
+    for copy in copies:
+        copy.wait()
     rows, channels = grad_ref.shape
     block = acc_ref.shape[0]
     part = block // 8
@@ -131,8 +139,10 @@
 
 def backward(row, place, grad, weight, high, block=512, group=3):
     rows, channels = grad.shape
+    vmem, hbm = pl.BlockSpec(memory_space=pltpu.VMEM), pl.BlockSpec(memory_space=pltpu.HBM)
     return pl.pallas_call(
         functools.partial(backward_kernel, group),
+        in_specs=[vmem, vmem, hbm, hbm],
         out_shape=(
             jax.ShapeDtypeStruct((rows, channels), F32),
             jax.ShapeDtypeStruct((3 * high, channels), BF16),
@@ -144,10 +154,18 @@
             pltpu.VMEM((block, 2 * channels), F32),
             pltpu.VMEM((block, group * block), BF16),
             pltpu.VMEM((group * block, 2 * channels), BF16),
+            pltpu.VMEM(grad.shape, BF16),
+            pltpu.VMEM(weight.shape, BF16),
+            pltpu.SemaphoreType.DMA((2,)),
         ],
         compiler_params=pltpu.CompilerParams(vmem_limit_bytes=16 << 20),
         cost_estimate=pl.CostEstimate(flops=TAPS*4*rows*channels*(block+64), bytes_accessed=2<<20, transcendentals=0),
-    )(row, place, grad, weight)
+    )(
+        row,
+        place,
+        pltpu.with_memory_space_constraint(grad, pltpu.HBM),
+        pltpu.with_memory_space_constraint(weight, pltpu.HBM),
+    )
 
 
 def product_kernel(group, extra, cols_ref, rhs_ref, out_ref, left_ref, whole_ref, buffer_ref, in_sems, out_sems):
@@ -413,16 +431,8 @@
     stats = everyones(
         jnp.stack([local_mean, local_square, jnp.full((channels,), local_count)])
     )
-    width = channels // down
-    source = lax.broadcasted_iota(I32, (8 * channels, 1), 0)
-    spot = lax.broadcasted_iota(I32, (1, down * channels), 1)
-    order = (
-        source == (spot // width) % 8 * channels + spot // channels * width + spot % width
-    ).astype(BF16)
     conv_part = product(cols, conv_out, extra=16)
-    stats, place_rows, conv_part, order = lax.optimization_barrier(
-        (stats, place_rows, conv_part, order)
-    )
+    stats, conv_part = lax.optimization_barrier((stats, conv_part))
     counts = stats[:, 2]
     total_count = jnp.sum(counts, axis=0)
     center = jnp.sum(stats[:, 0] * counts, axis=0) / total_count
@@ -443,7 +453,13 @@
         [scale, inverse_std, center, jnp.broadcast_to(total_count, scale.shape)]
         + [jnp.zeros_like(scale)] * 4
     )
-    sums, up_part, batch = lax.optimization_barrier((sums, up_part, batch))
+    width = channels // down
+    source = lax.broadcasted_iota(I32, (8 * channels, 1), 0)
+    spot = lax.broadcasted_iota(I32, (1, down * channels), 1)
+    order = (
+        source == (spot // width) % 8 * channels + spot // channels * width + spot % width
+    ).astype(BF16)
+    sums, up_part, batch, order = lax.optimization_barrier((sums, up_part, batch, order))
     pieces, conv_grad = weight_terms(
         live_count, sums, batch, upstream, conv_out, up_part, conv_part, order, across, down
     )

time: 128 us -> 123 us (0.961)
  starting transfers between devices: 50.7 us -> 45.7 us
  local copies, waits for them, and re-layouts: 9.13 us -> 5.77 us
  waiting for transfers between devices: 16.4 us -> 19.4 us
  other arithmetic: 5.63 us -> 3.75 us
  Pallas kernels: 42.2 us -> 43.5 us
    all_to_all x2, starting transfers between devices: 19.6 us -> 15.9 us  [everyones(): return lax.all_to_all(copies, axes, 0, 0, tiled=True)]
    unnamed x18 -> x14, local copies, waits for them, and re-layouts: 4.53 us -> 1.89 us
    ppermute x2, waiting for transfers between devices: 3.57 us -> 5.92 us  [from_neighbours(): a2 = lax.ppermute(low, 'bx', down_x)]
    all_to_all x2, waiting for transfers between devices: 6.35 us -> 7.99 us  [everyones(): return lax.all_to_all(copies, axes, 0, 0, tiled=True)]
    pallas_call x1, Pallas kernels: 12.6 us -> 13.9 us  [backward(): pl.pallas_call(functools.partial(backward_kernel, group), in_specs=[vmem,...]
    all_to_all x1, starting transfers between devices: 6.99 us -> 5.7 us  [per_device(): arrived = lax.all_to_all(pieces, axes, 0, 0, tiled=True)]
  transfers between devices with their start and end apart: 11 -> 11, of which waited for: 6 -> 7; matrix products, arithmetic and copies ran while one was open for 4% -> 5% of each run, Pallas kernels for 19% -> 21%
where the time goes in v4:
time: 123 us; the launch traced here: 122 us
  starting transfers between devices  45.7 us (37%)
  Pallas kernels  43.5 us (35%)
  waiting for transfers between devices  19.4 us (16%)
  local copies, waits for them, and re-layouts  5.77 us (5%)
  other arithmetic  3.75 us (3%)
  matrix products  1.88 us (2%)
  between operations  1.73 us (1%)
    all_to_all x2, starting transfers between devices, everyones(): return lax.all_to_all(copies, axes, 0, 0, tiled=True)  15.9 us
    pallas_call x1, Pallas kernels, backward(): pl.pallas_call(functools.partial(backward_kernel, group), in_specs=[vmem,...  13.9 us
    pallas_call x1, Pallas kernels, forward(): pl.pallas_call(functools.partial(forward_kernel, chunks), in_specs=[vmem]...  11.8 us
    pallas_call x2, Pallas kernels, product(): pl.pallas_call(functools.partial(product_kernel, group, extra), in_specs=...  11.7 us
    ppermute x2, starting transfers between devices, from_neighbours(): lax.ppermute(jnp.concatenate([a0[2 * size:], mid_high, a2[2 * size:]]), '...  9.85 us
    all_to_all x2, waiting for transfers between devices, everyones(): return lax.all_to_all(copies, axes, 0, 0, tiled=True)  7.99 us
    ppermute x2, starting transfers between devices, from_neighbours(): a0 = lax.ppermute(high, 'bx', up_x)  7.79 us
    ppermute x2, waiting for transfers between devices, from_neighbours(): a2 = lax.ppermute(low, 'bx', down_x)  5.92 us
  transfers between devices with their start and end apart: 11, of which 7 were waited for; matrix products, arithmetic and copies ran while one was open for 5% of the time, Pallas kernels for 21%

profile of v4, /device:TPU:1, one launch (start us, length us, event | category | flops | bytes accessed | tf_op | source)
XLA Modules:
  0.0 121.7 jit_solution(9568832856350440251)
XLA Ops:
  0.6 0.0 copy-start.1
  0.7 1.9 %fusion.3 = bf16[1024,128]{1,0:T(8,128)(2,1)S(1)} fusion(s32[1024]{0:T(1024)} %bitcast.55, bf16[1,1,1024,128]{3,2,1,0:T(8,128)(2,1)} %param.8), kind=kOutput, calls=%fused_computation.6 | convolution fusion | flops 269615104 | bytes 528384 | tf_op jit(solution)/shard_map/dot_general | solution.py:402
  2.6 4.4 %collective-permute-start = (bf16[384,128]{1,0:T(8,128)(2,1)S(1)}, bf16[384,128]{1,0:T(8,128)(2,1)S(1)}, u32[]{:S(2)}, u32[]{:S(2)}) collective-permute-start(bf16[384,128]{1,0:T(8,128)(2,1)S(1)} %get-tuple-element.65), channel_id=1, source_target_pairs={{0,8},{8,16},{16,24},{24,32},{32,40},{40,48},{48,56},{56,64},{64,7... | collective-permute-start | bytes 294920 | tf_op jit(solution)/shard_map/ppermute | solution.py:377
  6.9 1.3 %collective-permute-start.1 = (bf16[384,128]{1,0:T(8,128)(2,1)S(1)}, bf16[384,128]{1,0:T(8,128)(2,1)S(1)}, u32[]{:S(2)}, u32[]{:S(2)}) collective-permute-start(bf16[384,128]{1,0:T(8,128)(2,1)S(1)} %get-tuple-element.64), channel_id=1, source_target_pairs={{8,0},{16,8},{24,16},{32,24},{40,32},{48,40},{56,48},{64,56},{72,6... | collective-permute-start | bytes 294920 | tf_op jit(solution)/shard_map/ppermute | solution.py:378
  8.9 1.1 copy.25
  10.1 0.1 pad.15.clone
  10.1 0.0 collective-permute-done.a0_ref
  10.1 2.4 %collective-permute-done.1.a2_ref = bf16[384,128]{1,0:T(8,128)(2,1)S(1)} collective-permute-done((bf16[384,128]{1,0:T(8,128)(2,1)S(1)}, bf16[384,128]{1,0:T(8,128)(2,1)S(1)}, u32[]{:S(2)}, u32[]{:S(2)}) %collective-permute-start.1) | collective-permute-done | bytes 98336 | tf_op jit(solution)/shard_map/ppermute | solution.py:378
  12.5 5.0 %collective-permute-start.2 = (bf16[384,128]{1,0:T(8,128)(2,1)S(1)}, bf16[384,128]{1,0:T(8,128)(2,1)S(1)}, u32[]{:S(2)}, u32[]{:S(2)}) collective-permute-start(bf16[384,128]{1,0:T(8,128)(2,1)S(1)} %pad_maximum_fusion), channel_id=1, source_target_pairs={{0,1},{1,2},{2,3},{3,4},{4,5},{5,6},{6,7},{8,9},{9,10},{10,11},{11... | collective-permute-start | bytes 294920 | tf_op jit(solution)/shard_map/ppermute | solution.py:380
  17.6 1.9 %collective-permute-start.3 = (bf16[384,128]{1,0:T(8,128)(2,1)S(1)}, bf16[384,128]{1,0:T(8,128)(2,1)S(1)}, u32[]{:S(2)}, u32[]{:S(2)}) collective-permute-start(bf16[384,128]{1,0:T(8,128)(2,1)S(1)} %pad_maximum_fusion.1), channel_id=1, source_target_pairs={{1,0},{2,1},{3,2},{4,3},{5,4},{6,5},{7,6},{9,8},{10,9},{11,10},{12... | collective-permute-start | bytes 294920 | tf_op jit(solution)/shard_map/ppermute | solution.py:381
  19.5 0.9 select_select_fusion
  20.4 0.9 fusion.46
  21.3 0.0 collective-permute-done.2.b0_ref
  21.3 2.2 %collective-permute-done.3.b2_ref = bf16[384,128]{1,0:T(8,128)(2,1)S(1)} collective-permute-done((bf16[384,128]{1,0:T(8,128)(2,1)S(1)}, bf16[384,128]{1,0:T(8,128)(2,1)S(1)}, u32[]{:S(2)}, u32[]{:S(2)}) %collective-permute-start.3) | collective-permute-done | bytes 98336 | tf_op jit(solution)/shard_map/ppermute | solution.py:381
  23.5 11.8 %shard_map.103 = (bf16[1024,128]{1,0:T(8,128)(2,1)S(1)}, bf16[1024,3456]{1,0:T(8,128)(2,1)}) custom-call(s32[1024,32]{1,0:T(8,128)S(1)} %get-tuple-element.60.place_ref, bf16[1024,128]{1,0:T(8,128)(2,1)S(1)} %bitcast.57, bf16[384,128]{1,0:T(8,128)(2,1)S(1)} %collective-permute-done.a0_ref, bf16[384,128]{1,0:T(8,128)(2,1)S(1)} %collective-permute-done.1.a2_ref, ...), custom_call_target="tpu_custom_call" | custom-call | flops 7247757312 | bytes 9437184 | tf_op jit(solution)/shard_map/pallas_call | solution.py:74
  35.3 0.2 fusion.5
  35.5 0.2 fusion.8
  35.7 0.1 maximum_maximum_fusion
  35.8 0.7 broadcast_in_dim.10
  36.5 10.0 %all-to-all-start = ((f32[128,3,128]{2,1,0:T(4,128)}), f32[128,3,128]{2,1,0:T(4,128)S(1)}, u32[]{:S(2)}, u32[]{:S(2)}) async-start(f32[128,3,128]{2,1,0:T(4,128)} %broadcast_in_dim.10), calls=%async_computation | async-start | bytes 524288 | tf_op jit(solution)/shard_map/all_to_all | solution.py:388
  46.6 0.9 fusion.1.order_ref
  47.5 0.0 copy-start.4
  47.5 0.0 copy-start.3
  47.5 0.0 copy-start.5
  47.5 5.9 %shard_map.104.conv_ref = f32[144,3456]{1,0:T(8,128)} custom-call(bf16[1024,3456]{1,0:T(8,128)(2,1)} %get-tuple-element.28.cols_ref, bf16[1024,128]{1,0:T(8,128)(2,1)S(1)} %get-tuple-element.27.rhs_ref.conv_out_ref), custom_call_target="tpu_custom_call" | custom-call | flops 905969664 | bytes 9437184 | tf_op jit(solution)/shard_map/pallas_call | solution.py:211
  53.4 3.9 %all-to-all-done = f32[128,3,128]{2,1,0:T(4,128)S(1)} async-done(((f32[128,3,128]{2,1,0:T(4,128)}), f32[128,3,128]{2,1,0:T(4,128)S(1)}, u32[]{:S(2)}, u32[]{:S(2)}) %all-to-all-start) | async-done | bytes 196640 | tf_op jit(solution)/shard_map/all_to_all | solution.py:388
  57.4 0.1 slice.62
  57.6 1.0 fusion.20
  58.6 0.7 broadcast_in_dim.12
  59.3 5.9 %all-to-all-start.1 = ((f32[128,2,128]{2,1,0:T(2,128)}), f32[128,2,128]{2,1,0:T(2,128)S(1)}, u32[]{:S(2)}, u32[]{:S(2)}) async-start(f32[128,2,128]{2,1,0:T(2,128)} %broadcast_in_dim.12), calls=%async_computation.1 | async-start | bytes 262144 | tf_op jit(solution)/shard_map/all_to_all | solution.py:388
  65.2 5.8 %shard_map.105.up_ref = f32[128,3456]{1,0:T(8,128)} custom-call(bf16[1024,3456]{1,0:T(8,128)(2,1)} %get-tuple-element.28.cols_ref, bf16[1024,128]{1,0:T(8,128)(2,1)S(1)} %get-tuple-element.58.rhs_ref.upstream_ref), custom_call_target="tpu_custom_call" | custom-call | flops 905969664 | bytes 9437184 | tf_op jit(solution)/shard_map/pallas_call | solution.py:211
  71.1 4.1 %all-to-all-done.1.sums_ref = f32[128,2,128]{2,1,0:T(2,128)S(1)} async-done(((f32[128,2,128]{2,1,0:T(2,128)}), f32[128,2,128]{2,1,0:T(2,128)S(1)}, u32[]{:S(2)}, u32[]{:S(2)}) %all-to-all-start.1) | async-done | bytes 131104 | tf_op jit(solution)/shard_map/all_to_all | solution.py:388
  75.1 4.6 %shard_map.106 = (bf16[128,4,8,128]{3,2,1,0:T(8,128)(2,1)}, bf16[1024,128]{1,0:T(8,128)(2,1)}) custom-call(s32[1,1]{1,0:T(1,128)} %copy.31.live_ref, f32[128,2,128]{2,1,0:T(2,128)S(1)} %all-to-all-done.1.sums_ref, f32[8,128]{1,0:T(8,128)S(1)} %stack.35.batch_ref, bf16[1024,128]{1,0:T(8,128)(2,1)S(1)} %get-tuple-element.58.rhs_ref.upstream_ref, ...), custom_call_target="tpu_custom_call" | custom-call | flops 1073741824 | bytes 5242880 | tf_op jit(solution)/shard_map/pallas_call | solution.py:308
  79.8 5.7 %all-to-all-start.2 = ((bf16[128,4,8,128]{3,2,1,0:T(8,128)(2,1)}), bf16[128,4,8,128]{3,2,1,0:T(8,128)(2,1)S(1)}, u32[]{:S(2)}, u32[]{:S(2)}) async-start(bf16[128,4,8,128]{3,2,1,0:T(8,128)(2,1)} %get-tuple-element.38), calls=%async_computation.2 | async-start | bytes 2097152 | tf_op jit(solution)/shard_map/all_to_all | solution.py:466
  85.5 1.2 copy.28
  86.7 13.9 %shard_map.107 = (f32[1024,128]{1,0:T(8,128)S(1)}, bf16[384,128]{1,0:T(8,128)(2,1)S(1)}, bf16[128,128]{1,0:T(8,128)(2,1)S(1)}, bf16[128,128]{1,0:T(8,128)(2,1)S(1)}, bf16[384,128]{1,0:T(8,128)(2,1)S(1)}) custom-call(s32[2,32,512]{2,1,0:T(8,128)S(1)} %bitcast.54, s32[1024,32]{1,0:T(8,128)S(1)} %get-tuple-element.60.place_ref, ...), custom_call_target="tpu_custom_call" | custom-call | flops 8153726976 | bytes 2097152 | tf_op jit(solution)/shard_map/pallas_call | solution.py:143
  100.5 3.4 %collective-permute-start.4 = (bf16[384,128]{1,0:T(8,128)(2,1)S(1)}, bf16[384,128]{1,0:T(8,128)(2,1)S(1)}, u32[]{:S(2)}, u32[]{:S(2)}) collective-permute-start(bf16[384,128]{1,0:T(8,128)(2,1)S(1)} %get-tuple-element.36), channel_id=1, source_target_pairs={{0,8},{8,16},{16,24},{24,32},{32,40},{40,48},{48,56},{56,64},{64,7... | collective-permute-start | bytes 294920 | tf_op jit(solution)/shard_map/ppermute | solution.py:377
  104.0 1.3 %collective-permute-start.5 = (bf16[384,128]{1,0:T(8,128)(2,1)S(1)}, bf16[384,128]{1,0:T(8,128)(2,1)S(1)}, u32[]{:S(2)}, u32[]{:S(2)}) collective-permute-start(bf16[384,128]{1,0:T(8,128)(2,1)S(1)} %get-tuple-element.37), channel_id=1, source_target_pairs={{8,0},{16,8},{24,16},{32,24},{40,32},{48,40},{56,48},{64,56},{72,6... | collective-permute-start | bytes 294920 | tf_op jit(solution)/shard_map/ppermute | solution.py:378
  105.3 0.4 collective-permute-done.4.a0_ref
  105.8 3.6 %collective-permute-done.5.a2_ref = bf16[384,128]{1,0:T(8,128)(2,1)S(1)} collective-permute-done((bf16[384,128]{1,0:T(8,128)(2,1)S(1)}, bf16[384,128]{1,0:T(8,128)(2,1)S(1)}, u32[]{:S(2)}, u32[]{:S(2)}) %collective-permute-start.5) | collective-permute-done | bytes 98336 | tf_op jit(solution)/shard_map/ppermute | solution.py:378
  109.4 4.8 %collective-permute-start.6 = (bf16[384,128]{1,0:T(8,128)(2,1)S(1)}, bf16[384,128]{1,0:T(8,128)(2,1)S(1)}, u32[]{:S(2)}, u32[]{:S(2)}) collective-permute-start(bf16[384,128]{1,0:T(8,128)(2,1)S(1)} %pad_maximum_fusion.2), channel_id=1, source_target_pairs={{0,1},{1,2},{2,3},{3,4},{4,5},{5,6},{6,7},{8,9},{9,10},{10,11},{11... | collective-permute-start | bytes 294920 | tf_op jit(solution)/shard_map/ppermute | solution.py:380
  114.2 1.9 %collective-permute-start.7 = (bf16[384,128]{1,0:T(8,128)(2,1)S(1)}, bf16[384,128]{1,0:T(8,128)(2,1)S(1)}, u32[]{:S(2)}, u32[]{:S(2)}) collective-permute-start(bf16[384,128]{1,0:T(8,128)(2,1)S(1)} %pad_maximum_fusion.3), channel_id=1, source_target_pairs={{1,0},{2,1},{3,2},{4,3},{5,4},{6,5},{7,6},{9,8},{10,9},{11,10},{12... | collective-permute-start | bytes 294920 | tf_op jit(solution)/shard_map/ppermute | solution.py:381
  116.2 0.2 convert_reduce_fusion
  116.4 0.1 reshape.212
  116.5 0.8 copy.30
  117.3 0.0 collective-permute-done.6.b0_ref
  117.3 2.9 %collective-permute-done.7.b2_ref = bf16[384,128]{1,0:T(8,128)(2,1)S(1)} collective-permute-done((bf16[384,128]{1,0:T(8,128)(2,1)S(1)}, bf16[384,128]{1,0:T(8,128)(2,1)S(1)}, u32[]{:S(2)}, u32[]{:S(2)}) %collective-permute-start.7) | collective-permute-done | bytes 98336 | tf_op jit(solution)/shard_map/ppermute | solution.py:381
  120.2 1.6 %shard_map.108 = bf16[1024,128]{1,0:T(8,128)(2,1)} custom-call(s32[8,128]{1,0:T(8,128)S(1)} %bitcast.56, bf16[384,128]{1,0:T(8,128)(2,1)S(1)} %collective-permute-done.4.a0_ref, bf16[384,128]{1,0:T(8,128)(2,1)S(1)} %collective-permute-done.5.a2_ref, bf16[384,128]{1,0:T(8,128)(2,1)S(1)} %collective-permute-done.6.b0_ref, ...), custom_call_target="tpu_custom_call" | custom-call | flops 268435456 | bytes 2097152 | tf_op jit(solution)/shard_map/pallas_call | solution.py:358
  (35 shorter events, 0.4 us)
Async XLA Ops:
  0.6 22.9 %copy-start.2 = (bf16[1,1,1024,128]{3,2,1,0:T(8,128)(2,1)S(1)}, bf16[1,1,1024,128]{3,2,1,0:T(8,128)(2,1)}, u32[]{:S(2)}) copy-start(bf16[1,1,1024,128]{3,2,1,0:T(8,128)(2,1)} %param.8) | copy-start | bytes 786436
  0.6 22.9 %copy-start.1 = (bf16[3456,128]{1,0:T(8,128)(2,1)S(1)}, bf16[3456,128]{1,0:T(8,128)(2,1)}, u32[]{:S(2)}) copy-start(bf16[3456,128]{1,0:T(8,128)(2,1)} %weight_in_ref.1) | copy-start | bytes 2654212
  2.6 7.6 %collective-permute-start = (bf16[384,128]{1,0:T(8,128)(2,1)S(1)}, bf16[384,128]{1,0:T(8,128)(2,1)S(1)}, u32[]{:S(2)}, u32[]{:S(2)}) collective-permute-start(bf16[384,128]{1,0:T(8,128)(2,1)S(1)} %get-tuple-element.65), channel_id=1, source_target_pairs={{0,8},{8,16},{16,24},{24,32},{32,40},{40,48},{48,56},{56,64},{64,7... | collective-permute-start | bytes 294920 | tf_op jit(solution)/shard_map/ppermute | solution.py:377
  6.9 5.5 %collective-permute-start.1 = (bf16[384,128]{1,0:T(8,128)(2,1)S(1)}, bf16[384,128]{1,0:T(8,128)(2,1)S(1)}, u32[]{:S(2)}, u32[]{:S(2)}) collective-permute-start(bf16[384,128]{1,0:T(8,128)(2,1)S(1)} %get-tuple-element.64), channel_id=1, source_target_pairs={{8,0},{16,8},{24,16},{32,24},{40,32},{48,40},{56,48},{64,56},{72,6... | collective-permute-start | bytes 294920 | tf_op jit(solution)/shard_map/ppermute | solution.py:378
  12.5 8.8 %collective-permute-start.2 = (bf16[384,128]{1,0:T(8,128)(2,1)S(1)}, bf16[384,128]{1,0:T(8,128)(2,1)S(1)}, u32[]{:S(2)}, u32[]{:S(2)}) collective-permute-start(bf16[384,128]{1,0:T(8,128)(2,1)S(1)} %pad_maximum_fusion), channel_id=1, source_target_pairs={{0,1},{1,2},{2,3},{3,4},{4,5},{5,6},{6,7},{8,9},{9,10},{10,11},{11... | collective-permute-start | bytes 294920 | tf_op jit(solution)/shard_map/ppermute | solution.py:380
  17.6 5.9 %collective-permute-start.3 = (bf16[384,128]{1,0:T(8,128)(2,1)S(1)}, bf16[384,128]{1,0:T(8,128)(2,1)S(1)}, u32[]{:S(2)}, u32[]{:S(2)}) collective-permute-start(bf16[384,128]{1,0:T(8,128)(2,1)S(1)} %pad_maximum_fusion.1), channel_id=1, source_target_pairs={{1,0},{2,1},{3,2},{4,3},{5,4},{6,5},{7,6},{9,8},{10,9},{11,10},{12... | collective-permute-start | bytes 294920 | tf_op jit(solution)/shard_map/ppermute | solution.py:381
  36.5 20.8 %all-to-all-start = ((f32[128,3,128]{2,1,0:T(4,128)}), f32[128,3,128]{2,1,0:T(4,128)S(1)}, u32[]{:S(2)}, u32[]{:S(2)}) async-start(f32[128,3,128]{2,1,0:T(4,128)} %broadcast_in_dim.10), calls=%async_computation | async-start | bytes 524288 | tf_op jit(solution)/shard_map/all_to_all | solution.py:388
  47.5 10.1 %copy-start.4 = (f32[128]{0:T(128)S(1)}, f32[128]{0:T(128)}, u32[]{:S(2)}) copy-start(f32[128]{0:T(128)} %param.13) | copy-start | bytes 1540
  47.5 10.1 %copy-start.3 = (bf16[1,1,1024,128]{3,2,1,0:T(8,128)(2,1)S(1)}, bf16[1,1,1024,128]{3,2,1,0:T(8,128)(2,1)}, u32[]{:S(2)}) copy-start(bf16[1,1,1024,128]{3,2,1,0:T(8,128)(2,1)} %param.15) | copy-start | bytes 786436
  47.5 10.1 %copy-start.5 = (f32[128]{0:T(128)S(1)}, f32[128]{0:T(128)}, u32[]{:S(2)}) copy-start(f32[128]{0:T(128)} %param.14) | copy-start | bytes 1540
  59.3 15.8 %all-to-all-start.1 = ((f32[128,2,128]{2,1,0:T(2,128)}), f32[128,2,128]{2,1,0:T(2,128)S(1)}, u32[]{:S(2)}, u32[]{:S(2)}) async-start(f32[128,2,128]{2,1,0:T(2,128)} %broadcast_in_dim.12), calls=%async_computation.1 | async-start | bytes 262144 | tf_op jit(solution)/shard_map/all_to_all | solution.py:388
  79.8 29.6 %all-to-all-start.2 = ((bf16[128,4,8,128]{3,2,1,0:T(8,128)(2,1)}), bf16[128,4,8,128]{3,2,1,0:T(8,128)(2,1)S(1)}, u32[]{:S(2)}, u32[]{:S(2)}) async-start(bf16[128,4,8,128]{3,2,1,0:T(8,128)(2,1)} %get-tuple-element.38), calls=%async_computation.2 | async-start | bytes 2097152 | tf_op jit(solution)/shard_map/all_to_all | solution.py:466
  86.7 33.5 %copy-start = (s32[1,1,8,128]{3,2,1,0:T(8,128)S(1)}, s32[1,1,8,128]{3,2,1,0:T(8,128)}, u32[]{:S(2)}) copy-start(s32[1,1,8,128]{3,2,1,0:T(8,128)} %param.11) | copy-start | bytes 12292
  100.5 5.2 %collective-permute-start.4 = (bf16[384,128]{1,0:T(8,128)(2,1)S(1)}, bf16[384,128]{1,0:T(8,128)(2,1)S(1)}, u32[]{:S(2)}, u32[]{:S(2)}) collective-permute-start(bf16[384,128]{1,0:T(8,128)(2,1)S(1)} %get-tuple-element.36), channel_id=1, source_target_pairs={{0,8},{8,16},{16,24},{24,32},{32,40},{40,48},{48,56},{56,64},{64,7... | collective-permute-start | bytes 294920 | tf_op jit(solution)/shard_map/ppermute | solution.py:377
  104.0 5.4 %collective-permute-start.5 = (bf16[384,128]{1,0:T(8,128)(2,1)S(1)}, bf16[384,128]{1,0:T(8,128)(2,1)S(1)}, u32[]{:S(2)}, u32[]{:S(2)}) collective-permute-start(bf16[384,128]{1,0:T(8,128)(2,1)S(1)} %get-tuple-element.37), channel_id=1, source_target_pairs={{8,0},{16,8},{24,16},{32,24},{40,32},{48,40},{56,48},{64,56},{72,6... | collective-permute-start | bytes 294920 | tf_op jit(solution)/shard_map/ppermute | solution.py:378
  109.4 7.9 %collective-permute-start.6 = (bf16[384,128]{1,0:T(8,128)(2,1)S(1)}, bf16[384,128]{1,0:T(8,128)(2,1)S(1)}, u32[]{:S(2)}, u32[]{:S(2)}) collective-permute-start(bf16[384,128]{1,0:T(8,128)(2,1)S(1)} %pad_maximum_fusion.2), channel_id=1, source_target_pairs={{0,1},{1,2},{2,3},{3,4},{4,5},{5,6},{6,7},{8,9},{9,10},{10,11},{11... | collective-permute-start | bytes 294920 | tf_op jit(solution)/shard_map/ppermute | solution.py:380
  114.2 5.9 %collective-permute-start.7 = (bf16[384,128]{1,0:T(8,128)(2,1)S(1)}, bf16[384,128]{1,0:T(8,128)(2,1)S(1)}, u32[]{:S(2)}, u32[]{:S(2)}) collective-permute-start(bf16[384,128]{1,0:T(8,128)(2,1)S(1)} %pad_maximum_fusion.3), channel_id=1, source_target_pairs={{1,0},{2,1},{3,2},{4,3},{5,4},{6,5},{7,6},{9,8},{10,9},{11,10},{12... | collective-permute-start | bytes 294920 | tf_op jit(solution)/shard_map/ppermute | solution.py:381

commit v5 on v4

--- a/solution.py
+++ b/solution.py
@@ -220,7 +220,7 @@
             pltpu.SemaphoreType.DMA((slots,)),
             pltpu.SemaphoreType.DMA((TAPS // group,)),
         ],
-        compiler_params=pltpu.CompilerParams(vmem_limit_bytes=16 << 20),
+        compiler_params=pltpu.CompilerParams(vmem_limit_bytes=8 << 20),
         cost_estimate=pl.CostEstimate(
             flops=2 * rows * wide * channels, bytes_accessed=9 << 20, transcendentals=0
         ),
@@ -459,7 +459,9 @@
     order = (
         source == (spot // width) % 8 * channels + spot // channels * width + spot % width
     ).astype(BF16)
-    sums, up_part, batch, order = lax.optimization_barrier((sums, up_part, batch, order))
+    sums, up_part, batch, order, place_rows = lax.optimization_barrier(
+        (sums, up_part, batch, order, place_rows)
+    )
     pieces, conv_grad = weight_terms(
         live_count, sums, batch, upstream, conv_out, up_part, conv_part, order, across, down
     )

time: 123 us -> 123 us (level)
  waiting for transfers between devices: 19.4 us -> 14.1 us
  starting transfers between devices: 45.7 us -> 49.1 us
  other arithmetic: 3.75 us -> 5.56 us
    ppermute x2, waiting for transfers between devices: 5.07 us -> 0.01 us  [from_neighbours(): lax.ppermute(jnp.concatenate([a0[:size], mid_low, a2[:size]]), 'by', down_y)]
    ppermute x2, starting transfers between devices: 3.84 us -> 7.53 us  [from_neighbours(): lax.ppermute(jnp.concatenate([a0[:size], mid_low, a2[:size]]), 'by', down_y)]
    ppermute x2, starting transfers between devices: 9.85 us -> 6.16 us  [from_neighbours(): lax.ppermute(jnp.concatenate([a0[2 * size:], mid_high, a2[2 * size:]]), '...]
    all_to_all x2, starting transfers between devices: 15.9 us -> 18.1 us  [everyones(): return lax.all_to_all(copies, axes, 0, 0, tiled=True)]
    all_to_all x2, waiting for transfers between devices: 7.99 us -> 6.38 us  [everyones(): return lax.all_to_all(copies, axes, 0, 0, tiled=True)]
    ppermute x2, waiting for transfers between devices: 0.01 us -> 1.41 us  [from_neighbours(): lax.ppermute(jnp.concatenate([a0[2 * size:], mid_high, a2[2 * size:]]), '...]
    all_to_all x1, starting transfers between devices: 5.7 us -> 6.94 us  [per_device(): arrived = lax.all_to_all(pieces, axes, 0, 0, tiled=True)]
  transfers between devices with their start and end apart: 11 -> 11, of which waited for: 7 -> 7; matrix products, arithmetic and copies ran while one was open for 5% -> 4% of each run, Pallas kernels for 21% -> 21%
where the time goes in v5:
time: 123 us; the launch traced here: 122 us
  starting transfers between devices  49.1 us (40%)
  Pallas kernels  43.5 us (35%)
  waiting for transfers between devices  14.1 us (11%)
  local copies, waits for them, and re-layouts  6.41 us (5%)
  other arithmetic  5.56 us (5%)
  matrix products  1.88 us (2%)
  between operations  1.72 us (1%)
    all_to_all x2, starting transfers between devices, everyones(): return lax.all_to_all(copies, axes, 0, 0, tiled=True)  18.1 us
    pallas_call x1, Pallas kernels, backward(): pl.pallas_call(functools.partial(backward_kernel, group), in_specs=[vmem,...  13.8 us
    pallas_call x1, Pallas kernels, forward(): pl.pallas_call(functools.partial(forward_kernel, chunks), in_specs=[vmem]...  11.8 us
    pallas_call x2, Pallas kernels, product(): pl.pallas_call(functools.partial(product_kernel, group, extra), in_specs=...  11.7 us
    ppermute x2, starting transfers between devices, from_neighbours(): a0 = lax.ppermute(high, 'bx', up_x)  7.79 us
    ppermute x2, starting transfers between devices, from_neighbours(): lax.ppermute(jnp.concatenate([a0[:size], mid_low, a2[:size]]), 'by', down_y)  7.53 us
    all_to_all x1, starting transfers between devices, per_device(): arrived = lax.all_to_all(pieces, axes, 0, 0, tiled=True)  6.94 us
    all_to_all x2, waiting for transfers between devices, everyones(): return lax.all_to_all(copies, axes, 0, 0, tiled=True)  6.38 us
  transfers between devices with their start and end apart: 11, of which 7 were waited for; matrix products, arithmetic and copies ran while one was open for 4% of the time, Pallas kernels for 21%

profile of v5, /device:TPU:1, one launch (start us, length us, event | category | flops | bytes accessed | tf_op | source)
XLA Modules:
  0.0 122.4 jit_solution(6969316027364205551)
XLA Ops:
  0.6 0.0 copy-start.1
  0.7 1.9 %fusion.3 = bf16[1024,128]{1,0:T(8,128)(2,1)S(1)} fusion(s32[1024]{0:T(1024)} %bitcast.55, bf16[1,1,1024,128]{3,2,1,0:T(8,128)(2,1)} %param.8), kind=kOutput, calls=%fused_computation.6 | convolution fusion | flops 269615104 | bytes 528384 | tf_op jit(solution)/shard_map/dot_general | solution.py:402
  2.6 4.4 %collective-permute-start = (bf16[384,128]{1,0:T(8,128)(2,1)S(1)}, bf16[384,128]{1,0:T(8,128)(2,1)S(1)}, u32[]{:S(2)}, u32[]{:S(2)}) collective-permute-start(bf16[384,128]{1,0:T(8,128)(2,1)S(1)} %get-tuple-element.67), channel_id=1, source_target_pairs={{0,8},{8,16},{16,24},{24,32},{32,40},{40,48},{48,56},{56,64},{64,7... | collective-permute-start | bytes 294920 | tf_op jit(solution)/shard_map/ppermute | solution.py:377
  6.9 1.3 %collective-permute-start.1 = (bf16[384,128]{1,0:T(8,128)(2,1)S(1)}, bf16[384,128]{1,0:T(8,128)(2,1)S(1)}, u32[]{:S(2)}, u32[]{:S(2)}) collective-permute-start(bf16[384,128]{1,0:T(8,128)(2,1)S(1)} %get-tuple-element.66), channel_id=1, source_target_pairs={{8,0},{16,8},{24,16},{32,24},{40,32},{48,40},{56,48},{64,56},{72,6... | collective-permute-start | bytes 294920 | tf_op jit(solution)/shard_map/ppermute | solution.py:378
  8.3 1.1 copy.25
  10.1 0.1 pad.15.clone
  10.1 2.4 %collective-permute-done.1.a2_ref = bf16[384,128]{1,0:T(8,128)(2,1)S(1)} collective-permute-done((bf16[384,128]{1,0:T(8,128)(2,1)S(1)}, bf16[384,128]{1,0:T(8,128)(2,1)S(1)}, u32[]{:S(2)}, u32[]{:S(2)}) %collective-permute-start.1) | collective-permute-done | bytes 98336 | tf_op jit(solution)/shard_map/ppermute | solution.py:378
  12.5 3.8 %collective-permute-start.3 = (bf16[384,128]{1,0:T(8,128)(2,1)S(1)}, bf16[384,128]{1,0:T(8,128)(2,1)S(1)}, u32[]{:S(2)}, u32[]{:S(2)}) collective-permute-start(bf16[384,128]{1,0:T(8,128)(2,1)S(1)} %pad_maximum_fusion.1), channel_id=1, source_target_pairs={{1,0},{2,1},{3,2},{4,3},{5,4},{6,5},{7,6},{9,8},{10,9},{11,10},{12... | collective-permute-start | bytes 294920 | tf_op jit(solution)/shard_map/ppermute | solution.py:381
  16.4 3.1 %collective-permute-start.2 = (bf16[384,128]{1,0:T(8,128)(2,1)S(1)}, bf16[384,128]{1,0:T(8,128)(2,1)S(1)}, u32[]{:S(2)}, u32[]{:S(2)}) collective-permute-start(bf16[384,128]{1,0:T(8,128)(2,1)S(1)} %pad_maximum_fusion), channel_id=1, source_target_pairs={{0,1},{1,2},{2,3},{3,4},{4,5},{5,6},{6,7},{8,9},{9,10},{10,11},{11... | collective-permute-start | bytes 294920 | tf_op jit(solution)/shard_map/ppermute | solution.py:380
  19.5 0.9 select_select_fusion
  20.4 0.1 fusion.46
  20.5 0.6 collective-permute-done.2.b0_ref
  21.1 11.8 %shard_map.103 = (bf16[1024,128]{1,0:T(8,128)(2,1)S(1)}, bf16[1024,3456]{1,0:T(8,128)(2,1)}) custom-call(s32[1024,32]{1,0:T(8,128)S(1)} %get-tuple-element.62.place_ref, bf16[1024,128]{1,0:T(8,128)(2,1)S(1)} %bitcast.57, bf16[384,128]{1,0:T(8,128)(2,1)S(1)} %collective-permute-done.a0_ref, bf16[384,128]{1,0:T(8,128)(2,1)S(1)} %collective-permute-done.1.a2_ref, ...), custom_call_target="tpu_custom_call" | custom-call | flops 7247757312 | bytes 9437184 | tf_op jit(solution)/shard_map/pallas_call | solution.py:74
  32.9 0.2 fusion.5
  33.1 0.2 fusion.8
  33.3 0.1 maximum_maximum_fusion
  33.4 0.7 broadcast_in_dim.10
  34.2 11.9 %all-to-all-start = ((f32[128,3,128]{2,1,0:T(4,128)}), f32[128,3,128]{2,1,0:T(4,128)}, u32[]{:S(2)}, u32[]{:S(2)}) async-start(f32[128,3,128]{2,1,0:T(4,128)} %broadcast_in_dim.10), calls=%async_computation | async-start | bytes 524288 | tf_op jit(solution)/shard_map/all_to_all | solution.py:388
  46.1 0.9 fusion.1.order_ref
  46.9 0.2 copy.28
  47.1 0.0 copy-start.3
  47.1 5.9 %shard_map.104.conv_ref = f32[144,3456]{1,0:T(8,128)} custom-call(bf16[1024,3456]{1,0:T(8,128)(2,1)} %get-tuple-element.29.cols_ref, bf16[1024,128]{1,0:T(8,128)(2,1)S(1)} %get-tuple-element.28.rhs_ref.conv_out_ref), custom_call_target="tpu_custom_call" | custom-call | flops 905969664 | bytes 9437184 | tf_op jit(solution)/shard_map/pallas_call | solution.py:211
  53.1 3.5 %all-to-all-done = f32[128,3,128]{2,1,0:T(4,128)} async-done(((f32[128,3,128]{2,1,0:T(4,128)}), f32[128,3,128]{2,1,0:T(4,128)}, u32[]{:S(2)}, u32[]{:S(2)}) %all-to-all-start) | async-done | bytes 196640 | tf_op jit(solution)/shard_map/all_to_all | solution.py:388
  56.6 1.0 copy.26
  57.6 1.0 slice.62
  58.7 0.5 multiply_bitcast_fusion
  59.3 1.6 %fusion.20 = (f32[128]{0:T(128)S(1)}, f32[128]{0:T(128)S(1)}, bf16[1024,128]{1,0:T(8,128)(2,1)S(1)}, bf16[1,1,1024,128]{3,2,1,0:T(8,128)(2,1)}) fusion(bf16[1,1,1024,128]{3,2,1,0:T(8,128)(2,1)S(1)} %copy-done.3, f32[1024]{0:T(1024)S(1)} %fusion.44, f32[128]{0:T(128)} %param.14, f32[128]{0:T(128)S(1)} %get-tuple-element.59, f32[128]{0:T(128)S(1)} %div.93, ...), kind=kLoop, calls=%fused_computation.31 | loop fusion | flops 2096896 | bytes 1055744 | tf_op jit(solution)/shard_map/reduce_sum | solution.py:447
  60.9 0.7 broadcast_in_dim.12
  61.6 6.2 %all-to-all-start.1 = ((f32[128,2,128]{2,1,0:T(2,128)}), f32[128,2,128]{2,1,0:T(2,128)S(1)}, u32[]{:S(2)}, u32[]{:S(2)}) async-start(f32[128,2,128]{2,1,0:T(2,128)} %broadcast_in_dim.12), calls=%async_computation.1 | async-start | bytes 262144 | tf_op jit(solution)/shard_map/all_to_all | solution.py:388
  67.8 0.7 bitcast_divide_fusion
  68.5 0.6 stack.35.batch_ref
  69.1 5.8 %shard_map.105.up_ref = f32[128,3456]{1,0:T(8,128)} custom-call(bf16[1024,3456]{1,0:T(8,128)(2,1)} %get-tuple-element.29.cols_ref, bf16[1024,128]{1,0:T(8,128)(2,1)S(1)} %get-tuple-element.60.rhs_ref.upstream_ref), custom_call_target="tpu_custom_call" | custom-call | flops 905969664 | bytes 9437184 | tf_op jit(solution)/shard_map/pallas_call | solution.py:211
  75.0 2.8 %all-to-all-done.1.sums_ref = f32[128,2,128]{2,1,0:T(2,128)S(1)} async-done(((f32[128,2,128]{2,1,0:T(2,128)}), f32[128,2,128]{2,1,0:T(2,128)S(1)}, u32[]{:S(2)}, u32[]{:S(2)}) %all-to-all-start.1) | async-done | bytes 131104 | tf_op jit(solution)/shard_map/all_to_all | solution.py:388
  77.8 4.6 %shard_map.106 = (bf16[128,4,8,128]{3,2,1,0:T(8,128)(2,1)}, bf16[1024,128]{1,0:T(8,128)(2,1)}) custom-call(s32[1,1]{1,0:T(1,128)} %copy.31.live_ref, f32[128,2,128]{2,1,0:T(2,128)S(1)} %all-to-all-done.1.sums_ref, f32[8,128]{1,0:T(8,128)S(1)} %stack.35.batch_ref, bf16[1024,128]{1,0:T(8,128)(2,1)S(1)} %get-tuple-element.60.rhs_ref.upstream_ref, ...), custom_call_target="tpu_custom_call" | custom-call | flops 1073741824 | bytes 5242880 | tf_op jit(solution)/shard_map/pallas_call | solution.py:308
  82.4 6.9 %all-to-all-start.2 = ((bf16[128,4,8,128]{3,2,1,0:T(8,128)(2,1)}), bf16[128,4,8,128]{3,2,1,0:T(8,128)(2,1)S(1)}, u32[]{:S(2)}, u32[]{:S(2)}) async-start(bf16[128,4,8,128]{3,2,1,0:T(8,128)(2,1)} %get-tuple-element.40), calls=%async_computation.2 | async-start | bytes 2097152 | tf_op jit(solution)/shard_map/all_to_all | solution.py:468
  89.4 0.0 copy-start
  89.4 13.8 %shard_map.107 = (f32[1024,128]{1,0:T(8,128)S(1)}, bf16[384,128]{1,0:T(8,128)(2,1)S(1)}, bf16[128,128]{1,0:T(8,128)(2,1)S(1)}, bf16[128,128]{1,0:T(8,128)(2,1)S(1)}, bf16[384,128]{1,0:T(8,128)(2,1)S(1)}) custom-call(s32[2,32,512]{2,1,0:T(8,128)S(1)} %bitcast.54, s32[1024,32]{1,0:T(8,128)S(1)} %get-tuple-element.62.place_ref, ...), custom_call_target="tpu_custom_call" | custom-call | flops 8153726976 | bytes 2097152 | tf_op jit(solution)/shard_map/pallas_call | solution.py:143
  103.2 3.4 %collective-permute-start.4 = (bf16[384,128]{1,0:T(8,128)(2,1)S(1)}, bf16[384,128]{1,0:T(8,128)(2,1)S(1)}, u32[]{:S(2)}, u32[]{:S(2)}) collective-permute-start(bf16[384,128]{1,0:T(8,128)(2,1)S(1)} %get-tuple-element.38), channel_id=1, source_target_pairs={{0,8},{8,16},{16,24},{24,32},{32,40},{40,48},{48,56},{56,64},{64,7... | collective-permute-start | bytes 294920 | tf_op jit(solution)/shard_map/ppermute | solution.py:377
  106.6 1.3 %collective-permute-start.5 = (bf16[384,128]{1,0:T(8,128)(2,1)S(1)}, bf16[384,128]{1,0:T(8,128)(2,1)S(1)}, u32[]{:S(2)}, u32[]{:S(2)}) collective-permute-start(bf16[384,128]{1,0:T(8,128)(2,1)S(1)} %get-tuple-element.39), channel_id=1, source_target_pairs={{8,0},{16,8},{24,16},{32,24},{40,32},{48,40},{56,48},{64,56},{72,6... | collective-permute-start | bytes 294920 | tf_op jit(solution)/shard_map/ppermute | solution.py:378
  108.0 0.4 collective-permute-done.4.a0_ref
  108.4 3.6 %collective-permute-done.5.a2_ref = bf16[384,128]{1,0:T(8,128)(2,1)S(1)} collective-permute-done((bf16[384,128]{1,0:T(8,128)(2,1)S(1)}, bf16[384,128]{1,0:T(8,128)(2,1)S(1)}, u32[]{:S(2)}, u32[]{:S(2)}) %collective-permute-start.5) | collective-permute-done | bytes 98336 | tf_op jit(solution)/shard_map/ppermute | solution.py:378
  112.0 0.2 convert_reduce_fusion
  112.2 0.1 reshape.212
  112.4 3.7 %collective-permute-start.7 = (bf16[384,128]{1,0:T(8,128)(2,1)S(1)}, bf16[384,128]{1,0:T(8,128)(2,1)S(1)}, u32[]{:S(2)}, u32[]{:S(2)}) collective-permute-start(bf16[384,128]{1,0:T(8,128)(2,1)S(1)} %pad_maximum_fusion.3), channel_id=1, source_target_pairs={{1,0},{2,1},{3,2},{4,3},{5,4},{6,5},{7,6},{9,8},{10,9},{11,10},{12... | collective-permute-start | bytes 294920 | tf_op jit(solution)/shard_map/ppermute | solution.py:381
  116.1 3.1 %collective-permute-start.6 = (bf16[384,128]{1,0:T(8,128)(2,1)S(1)}, bf16[384,128]{1,0:T(8,128)(2,1)S(1)}, u32[]{:S(2)}, u32[]{:S(2)}) collective-permute-start(bf16[384,128]{1,0:T(8,128)(2,1)S(1)} %pad_maximum_fusion.2), channel_id=1, source_target_pairs={{0,1},{1,2},{2,3},{3,4},{4,5},{5,6},{6,7},{8,9},{9,10},{10,11},{11... | collective-permute-start | bytes 294920 | tf_op jit(solution)/shard_map/ppermute | solution.py:380
  119.2 0.8 copy.30
  120.0 0.8 collective-permute-done.6.b0_ref
  120.8 1.6 %shard_map.108 = bf16[1024,128]{1,0:T(8,128)(2,1)} custom-call(s32[8,128]{1,0:T(8,128)S(1)} %bitcast.56, bf16[384,128]{1,0:T(8,128)(2,1)S(1)} %collective-permute-done.4.a0_ref, bf16[384,128]{1,0:T(8,128)(2,1)S(1)} %collective-permute-done.5.a2_ref, bf16[384,128]{1,0:T(8,128)(2,1)S(1)} %collective-permute-done.6.b0_ref, ...), custom_call_target="tpu_custom_call" | custom-call | flops 268435456 | bytes 2097152 | tf_op jit(solution)/shard_map/pallas_call | solution.py:358
  (35 shorter events, 0.3 us)
Async XLA Ops:
  0.6 20.5 %copy-start.2 = (bf16[1,1,1024,128]{3,2,1,0:T(8,128)(2,1)S(1)}, bf16[1,1,1024,128]{3,2,1,0:T(8,128)(2,1)}, u32[]{:S(2)}) copy-start(bf16[1,1,1024,128]{3,2,1,0:T(8,128)(2,1)} %param.8) | copy-start | bytes 786436
  0.6 20.5 %copy-start.1 = (bf16[3456,128]{1,0:T(8,128)(2,1)S(1)}, bf16[3456,128]{1,0:T(8,128)(2,1)}, u32[]{:S(2)}) copy-start(bf16[3456,128]{1,0:T(8,128)(2,1)} %weight_in_ref.1) | copy-start | bytes 2654212
  2.6 7.6 %collective-permute-start = (bf16[384,128]{1,0:T(8,128)(2,1)S(1)}, bf16[384,128]{1,0:T(8,128)(2,1)S(1)}, u32[]{:S(2)}, u32[]{:S(2)}) collective-permute-start(bf16[384,128]{1,0:T(8,128)(2,1)S(1)} %get-tuple-element.67), channel_id=1, source_target_pairs={{0,8},{8,16},{16,24},{24,32},{32,40},{40,48},{48,56},{56,64},{64,7... | collective-permute-start | bytes 294920 | tf_op jit(solution)/shard_map/ppermute | solution.py:377
  6.9 5.5 %collective-permute-start.1 = (bf16[384,128]{1,0:T(8,128)(2,1)S(1)}, bf16[384,128]{1,0:T(8,128)(2,1)S(1)}, u32[]{:S(2)}, u32[]{:S(2)}) collective-permute-start(bf16[384,128]{1,0:T(8,128)(2,1)S(1)} %get-tuple-element.66), channel_id=1, source_target_pairs={{8,0},{16,8},{24,16},{32,24},{40,32},{48,40},{56,48},{64,56},{72,6... | collective-permute-start | bytes 294920 | tf_op jit(solution)/shard_map/ppermute | solution.py:378
  12.5 8.0 %collective-permute-start.3 = (bf16[384,128]{1,0:T(8,128)(2,1)S(1)}, bf16[384,128]{1,0:T(8,128)(2,1)S(1)}, u32[]{:S(2)}, u32[]{:S(2)}) collective-permute-start(bf16[384,128]{1,0:T(8,128)(2,1)S(1)} %pad_maximum_fusion.1), channel_id=1, source_target_pairs={{1,0},{2,1},{3,2},{4,3},{5,4},{6,5},{7,6},{9,8},{10,9},{11,10},{12... | collective-permute-start | bytes 294920 | tf_op jit(solution)/shard_map/ppermute | solution.py:381
  16.4 4.7 %collective-permute-start.2 = (bf16[384,128]{1,0:T(8,128)(2,1)S(1)}, bf16[384,128]{1,0:T(8,128)(2,1)S(1)}, u32[]{:S(2)}, u32[]{:S(2)}) collective-permute-start(bf16[384,128]{1,0:T(8,128)(2,1)S(1)} %pad_maximum_fusion), channel_id=1, source_target_pairs={{0,1},{1,2},{2,3},{3,4},{4,5},{5,6},{6,7},{8,9},{9,10},{10,11},{11... | collective-permute-start | bytes 294920 | tf_op jit(solution)/shard_map/ppermute | solution.py:380
  34.2 22.4 %all-to-all-start = ((f32[128,3,128]{2,1,0:T(4,128)}), f32[128,3,128]{2,1,0:T(4,128)}, u32[]{:S(2)}, u32[]{:S(2)}) async-start(f32[128,3,128]{2,1,0:T(4,128)} %broadcast_in_dim.10), calls=%async_computation | async-start | bytes 524288 | tf_op jit(solution)/shard_map/all_to_all | solution.py:388
  47.1 11.6 %copy-start.4 = (f32[128]{0:T(128)S(1)}, f32[128]{0:T(128)}, u32[]{:S(2)}) copy-start(f32[128]{0:T(128)} %param.13) | copy-start | bytes 1540
  47.1 12.1 %copy-start.3 = (bf16[1,1,1024,128]{3,2,1,0:T(8,128)(2,1)S(1)}, bf16[1,1,1024,128]{3,2,1,0:T(8,128)(2,1)}, u32[]{:S(2)}) copy-start(bf16[1,1,1024,128]{3,2,1,0:T(8,128)(2,1)} %param.15) | copy-start | bytes 786436
  57.6 1.1 copy-start.5
  61.6 16.2 %all-to-all-start.1 = ((f32[128,2,128]{2,1,0:T(2,128)}), f32[128,2,128]{2,1,0:T(2,128)S(1)}, u32[]{:S(2)}, u32[]{:S(2)}) async-start(f32[128,2,128]{2,1,0:T(2,128)} %broadcast_in_dim.12), calls=%async_computation.1 | async-start | bytes 262144 | tf_op jit(solution)/shard_map/all_to_all | solution.py:388
  82.4 29.6 %all-to-all-start.2 = ((bf16[128,4,8,128]{3,2,1,0:T(8,128)(2,1)}), bf16[128,4,8,128]{3,2,1,0:T(8,128)(2,1)S(1)}, u32[]{:S(2)}, u32[]{:S(2)}) async-start(bf16[128,4,8,128]{3,2,1,0:T(8,128)(2,1)} %get-tuple-element.40), calls=%async_computation.2 | async-start | bytes 2097152 | tf_op jit(solution)/shard_map/all_to_all | solution.py:468
  89.4 31.4 %copy-start = (s32[1,1,8,128]{3,2,1,0:T(8,128)S(1)}, s32[1,1,8,128]{3,2,1,0:T(8,128)}, u32[]{:S(2)}) copy-start(s32[1,1,8,128]{3,2,1,0:T(8,128)} %param.11) | copy-start | bytes 12292
  103.2 5.2 %collective-permute-start.4 = (bf16[384,128]{1,0:T(8,128)(2,1)S(1)}, bf16[384,128]{1,0:T(8,128)(2,1)S(1)}, u32[]{:S(2)}, u32[]{:S(2)}) collective-permute-start(bf16[384,128]{1,0:T(8,128)(2,1)S(1)} %get-tuple-element.38), channel_id=1, source_target_pairs={{0,8},{8,16},{16,24},{24,32},{32,40},{40,48},{48,56},{56,64},{64,7... | collective-permute-start | bytes 294920 | tf_op jit(solution)/shard_map/ppermute | solution.py:377
  106.6 5.4 %collective-permute-start.5 = (bf16[384,128]{1,0:T(8,128)(2,1)S(1)}, bf16[384,128]{1,0:T(8,128)(2,1)S(1)}, u32[]{:S(2)}, u32[]{:S(2)}) collective-permute-start(bf16[384,128]{1,0:T(8,128)(2,1)S(1)} %get-tuple-element.39), channel_id=1, source_target_pairs={{8,0},{16,8},{24,16},{32,24},{40,32},{48,40},{56,48},{64,56},{72,6... | collective-permute-start | bytes 294920 | tf_op jit(solution)/shard_map/ppermute | solution.py:378
  112.4 7.6 %collective-permute-start.7 = (bf16[384,128]{1,0:T(8,128)(2,1)S(1)}, bf16[384,128]{1,0:T(8,128)(2,1)S(1)}, u32[]{:S(2)}, u32[]{:S(2)}) collective-permute-start(bf16[384,128]{1,0:T(8,128)(2,1)S(1)} %pad_maximum_fusion.3), channel_id=1, source_target_pairs={{1,0},{2,1},{3,2},{4,3},{5,4},{6,5},{7,6},{9,8},{10,9},{11,10},{12... | collective-permute-start | bytes 294920 | tf_op jit(solution)/shard_map/ppermute | solution.py:381
  116.1 4.7 %collective-permute-start.6 = (bf16[384,128]{1,0:T(8,128)(2,1)S(1)}, bf16[384,128]{1,0:T(8,128)(2,1)S(1)}, u32[]{:S(2)}, u32[]{:S(2)}) collective-permute-start(bf16[384,128]{1,0:T(8,128)(2,1)S(1)} %pad_maximum_fusion.2), channel_id=1, source_target_pairs={{0,1},{1,2},{2,3},{3,4},{4,5},{5,6},{6,7},{8,9},{9,10},{10,11},{11... | collective-permute-start | bytes 294920 | tf_op jit(solution)/shard_map/ppermute | solution.py:380
